TPU v7x, 32 devices: a whole 2x2x4 slice. The times are simulated.
32 devices in a mesh: expert: 16 (over z, y, x), replica: 2 (over core).
Axes of the slice: x: 2, y: 2, z: 4, core: 2. Of those that a mesh axis runs over, the one named last changes fastest.
Arguments:
- samples: float32 [32768, 256], P(('expert', 'replica')), may hold values from -6 to 6
- routes: int32 [32768, 1], P(('expert', 'replica')), may hold values from 0 to 15; in each aligned block of 1024 rows (0 to 1023, 1024 to 2047, ...) at most 128 rows name the same one
- cotangent: float32 [32768, 256], P(('expert', 'replica')), may hold values from -6 to 6
- weights: float32 [7, 16, 256, 256], P(None, 'expert', 'replica'), may hold values from -0.375 to 0.375
- moment_one: float32 [7, 16, 256, 256], P(None, 'expert', 'replica'), may hold values from -6 to 6
- moment_two: float32 [7, 16, 256, 256], P(None, 'expert', 'replica'), may hold values from 1 to 30
Outputs:
- outputs: float32 [32768, 256], P(('expert', 'replica'))
- new_weights: float32 [7, 16, 256, 256], P(None, 'expert', 'replica')
- new_moment_one: float32 [7, 16, 256, 256], P(None, 'expert', 'replica')
- new_moment_two: float32 [7, 16, 256, 256], P(None, 'expert', 'replica')
Inputs may be any that keep to these rules, and one draw needn't show every extreme that they name: `routes`: among the 1024 rows of one device no expert is chosen by more than 128 rows; some expert is chosen by exactly 128 rows of some device.
All inputs are finite; a program needn't handle non-finite values.
Results may differ from a plain program's by a relative error of at most 0.0002.
Values sent between devices are 32-bit elements; how exact they have to be, the bound alone decides.
No kernel may reach another device: no remote copies, remote signals or barrier semaphores. Data moves between devices by JAX's collectives and lax.ppermute only.
A program may use at most 128 MiB of HBM per device.

v0:
```python
import functools

import jax
import jax.numpy as jnp
from jax import lax
from jax.experimental import pallas as pl
from jax.experimental.pallas import tpu as pltpu
from jax.sharding import PartitionSpec as P


CORR_ONE = 0.9999734386011124
CORR_TWO = 0.09520785288629038
PLANES = 4

F32 = jnp.float32
BF16 = jnp.bfloat16


def split(value):
    high = value.astype(BF16)
    return high, (value - high.astype(F32)).astype(BF16)


def dot(a, b, dims):
    return lax.dot_general(a, b, (dims, ((), ())), preferred_element_type=F32)


def dot3(ah, al, bh, bl, dims):
    return dot(ah, bh, dims) + (dot(ah, bl, dims) + dot(al, bh, dims))


NN = ((1,), (0,))
NT = ((1,), (1,))
TN = ((0,), (0,))


def slots_of(route, rank, plane, column, size, cap):
    own = jnp.right_shift(route, size.bit_length() - 1)
    chip = jnp.bitwise_and(route, size - 1)
    near = jnp.bitwise_xor(own, plane)
    inner = jnp.bitwise_and(jnp.bitwise_xor(jnp.right_shift(own, 1), own), 1)
    step = jnp.where(near < 2, near, 3 - inner)
    mask = jnp.bitwise_xor(chip, column)
    return (step * size + mask) * cap + rank


def position(size):
    at = lax.axis_index("expert")
    return jnp.right_shift(at, size.bit_length() - 1), jnp.bitwise_and(at, size - 1)


def pack_body(size, cap, groups, steps, route_ref, rows_ref, cots_ref, *outs):
    count, _ = rows_ref.shape
    plane, column = position(size)
    route = route_ref[...]
    hot = (lax.broadcasted_iota(jnp.int32, (groups, count), 0) == route).astype(F32)
    ahead = (
        lax.broadcasted_iota(jnp.int32, (count, count), 0)
        < lax.broadcasted_iota(jnp.int32, (count, count), 1)
    ).astype(F32).astype(BF16)
    before = dot(hot.astype(BF16), ahead, NN)
    rank = jnp.sum(before * hot, axis=0, keepdims=True).astype(jnp.int32)
    slot = slots_of(route, rank, plane, column, size, cap)
    data = [split(rows_ref[...]), split(cots_ref[...])]
    block = size * cap
    for part, step in enumerate(steps):
        pick = (
            lax.broadcasted_iota(jnp.int32, (block, count), 0) + step * block == slot
        ).astype(F32).astype(BF16)
        for kind, (high, low) in enumerate(data):
            rows = dot(pick, high, NN) + dot(pick, low, NN)
            for mask in range(size):
                outs[part * size + mask][kind] = rows[mask * cap : (mask + 1) * cap]


def pack(route_row, rows, cots, size, cap, groups, steps):
    count, width = rows.shape
    made = pl.pallas_call(
        functools.partial(pack_body, size, cap, groups, steps),
        out_shape=[jax.ShapeDtypeStruct((2, cap, width), F32)] * (len(steps) * size),
        compiler_params=pltpu.CompilerParams(vmem_limit_bytes=48 * 2**20),
        cost_estimate=pl.CostEstimate(
            flops=8 * count * count * width, bytes_accessed=12 * count * width, transcendentals=0
        ),
        name="pack",
    )(route_row, rows, cots)
    return [made[i * size : (i + 1) * size] for i in range(len(steps))]


def unpack_body(size, cap, groups, route_ref, *refs):
    out_ref = refs[-1]
    count = out_ref.shape[0]
    plane, column = position(size)
    route = route_ref[...]
    hot = (lax.broadcasted_iota(jnp.int32, (count, groups), 1) == route).astype(F32)
    ahead = (
        lax.broadcasted_iota(jnp.int32, (count, count), 1)
        < lax.broadcasted_iota(jnp.int32, (count, count), 0)
    ).astype(F32).astype(BF16)
    before = dot(ahead, hot.astype(BF16), NN)
    rank = jnp.sum(before * hot, axis=1, keepdims=True).astype(jnp.int32)
    slot = slots_of(route, rank, plane, column, size, cap)
    total = None
    for index, step in enumerate(sum(PAIRS, ())):
        pair, which = divmod(index, 2)
        rows = jnp.concatenate([refs[pair * size + m][which] for m in range(size)], axis=0)
        high, low = split(rows)
        at = lax.broadcasted_iota(jnp.int32, (count, size * cap), 1) + step * size * cap
        pick = (at == slot).astype(F32).astype(BF16)
        term = dot(pick, high, NN) + dot(pick, low, NN)
        total = term if total is None else total + term
    out_ref[...] = total


def unpack(route_col, pieces, size, cap, groups):
    count = route_col.shape[0]
    width = pieces[0].shape[-1]
    return pl.pallas_call(
        functools.partial(unpack_body, size, cap, groups),
        out_shape=jax.ShapeDtypeStruct((count, width), F32),
        compiler_params=pltpu.CompilerParams(vmem_limit_bytes=48 * 2**20),
        cost_estimate=pl.CostEstimate(
            flops=8 * count * count * width, bytes_accessed=12 * count * width, transcendentals=0
        ),
        name="unpack",
    )(route_col, *pieces)


def step_body(size, cap, layers, chunks, aliased, *refs):
    sent = refs[:size]
    mine, other = refs[size : size + 2]
    at = size + 2 + (size if aliased else 0)
    outs = refs[at : at + size]
    at += size
    keeps = refs[at : at + len(chunks)]
    sends = refs[at + len(chunks) : at + 2 * len(chunks)]
    at += 2 * len(chunks)
    wh, wl, ah, al, slope, full = refs[at:]
    width = full.shape[0]
    shard = mine.shape[1]
    core = lax.axis_index("replica")
    here = pl.multiple_of(core * shard, shard)
    there = pl.multiple_of(width - shard - core * shard, shard)

    for m in range(size):
        high, low = split(sent[m][0])
        ah[0, m * cap : (m + 1) * cap] = high
        al[0, m * cap : (m + 1) * cap] = low

    def weights(layer):
        high, low = split(mine[layer])
        wh[layer, pl.ds(here, shard)] = high
        wl[layer, pl.ds(here, shard)] = low
        high, low = split(other[layer])
        wh[layer, pl.ds(there, shard)] = high
        wl[layer, pl.ds(there, shard)] = low

    def forward(layer, _):
        weights(layer)
        pre = dot3(ah[layer], al[layer], wh[layer], wl[layer], NN)
        sigma = jax.nn.sigmoid(pre)
        high, low = split(pre * sigma)
        ah[layer + 1] = high
        al[layer + 1] = low
        slope[layer] = sigma * (1.0 + pre * (1.0 - sigma))
        return 0

    lax.fori_loop(0, layers - 1, forward, 0)
    last = layers - 1
    weights(last)
    result = dot3(ah[last], al[last], wh[last], wl[last], NN)
    for m in range(size):
        outs[m][0] = result[m * cap : (m + 1) * cap]

    delta = jnp.concatenate([sent[m][1] for m in range(size)], axis=0)
    dh, dl = split(delta)
    for keep, send, chunk in zip(keeps, sends, chunks):
        for layer in chunk:
            place = layer - min(chunk)
            full[...] = dot3(ah[layer], al[layer], dh, dl, TN)
            keep[place] = full[pl.ds(here, shard)]
            send[place] = full[pl.ds(there, shard)]
            if layer > 0:
                back = dot3(dh, dl, wh[layer], wl[layer], NT)
                dh, dl = split(back * slope[layer - 1])


def step_call(sent, mine, other, buffers, which, chunks):
    size = len(sent)
    cap, width = sent[0].shape[1:]
    layers, shard = mine.shape[:2]
    items = size * cap
    row_spec = pl.BlockSpec((2, cap, width), lambda i: (0, 0, 0))
    weight_spec = pl.BlockSpec((layers, shard, width), lambda i: (0, 0, 0))
    outs = [jax.ShapeDtypeStruct((2, cap, width), F32)] * size
    out_specs = [pl.BlockSpec((1, cap, width), lambda i: (which, 0, 0))] * size
    grads = [jax.ShapeDtypeStruct((len(c), shard, width), F32) for c in chunks] * 2
    grad_specs = [pl.BlockSpec((len(c), shard, width), lambda i: (0, 0, 0)) for c in chunks] * 2
    aliased = buffers is not None
    result = pl.pallas_call(
        functools.partial(step_body, size, cap, layers, chunks, aliased),
        grid=(1,),
        in_specs=[row_spec] * size
        + [weight_spec] * 2
        + [pl.BlockSpec(memory_space=pl.ANY)] * (size if aliased else 0),
        out_specs=out_specs + grad_specs,
        out_shape=outs + grads,
        input_output_aliases={size + 2 + m: m for m in range(size)} if aliased else {},
        scratch_shapes=[
            pltpu.VMEM((layers, width, width), BF16),
            pltpu.VMEM((layers, width, width), BF16),
            pltpu.VMEM((layers, items, width), BF16),
            pltpu.VMEM((layers, items, width), BF16),
            pltpu.VMEM((layers - 1, items, width), F32),
            pltpu.VMEM((width, width), F32),
        ],
        compiler_params=pltpu.CompilerParams(vmem_limit_bytes=48 * 2**20),
        cost_estimate=pl.CostEstimate(
            flops=18 * layers * items * width * width,
            bytes_accessed=4 * (3 * items * width + 2 * layers * width * width),
            transcendentals=layers * items * width,
        ),
        name="step",
    )(*sent, mine, other, *(buffers or ()))
    n = len(chunks)
    return result[:size], result[size : size + n], result[size + n :]


PAIRS = ((1, 2), (0, 3))


def chunks_of(layers, parts):
    order = list(range(layers - 1, -1, -1))
    parts = min(parts, layers)
    sizes = [layers // parts + (1 if i < layers % parts else 0) for i in range(parts)]
    cut, at = [], 0
    for n in sizes:
        cut.append(order[at : at + n])
        at += n
    return cut


PARTS = {0: 1, 1: 1, 2: 2, 3: 4}


def on_device(samples, routes, cotangent, weights, moment_one, moment_two):
    count = samples.shape[0]
    groups = lax.axis_size("expert")
    cap = 2 * count // groups
    size = groups // PLANES
    layers = weights.shape[0]
    route_row = routes.reshape(1, count)

    def plane_pairs(pairs):
        return [(a * size + p, b * size + p) for a, b in pairs for p in range(size)]

    def along(value, pairs):
        return lax.ppermute(value, "expert", plane_pairs(pairs))

    def swap_core(value):
        return lax.ppermute(value, "replica", [(0, 1), (1, 0)])

    def exchange(values):
        moved = [values[0]]
        for mask in range(1, size):
            moved.append(
                lax.ppermute(values[mask], "expert", [(e, e ^ mask) for e in range(groups)])
            )
        return moved

    SIDES = [(0, 1), (1, 0), (2, 3), (3, 2)]
    MIDDLE = [(1, 2), (2, 1)]
    OUTWARD = [(1, 0), (2, 3)]
    INWARD = [(0, 1), (3, 2)]

    own = weights[:, 0]
    side = along(own, SIDES)
    middle = along(own, MIDDLE)
    own_other = swap_core(own)
    arrived = {}
    for steps in PAIRS:
        packed = pack(route_row, samples, cotangent, size, cap, groups, steps)
        for step, values in zip(steps, packed):
            arrived[step] = exchange(values)
    side_in = along(side, MIDDLE)
    middle_out = along(middle, OUTWARD)
    side_out = along(side_in, OUTWARD)
    second = middle + middle_out
    third = side_in + side_out
    mats = [
        (own, own_other),
        (side, swap_core(side)),
        (second, swap_core(second)),
        (third, swap_core(third)),
    ]
    outputs = {}
    sums = {}
    for i, steps in enumerate(PAIRS):
        buffers = None
        for which, step in enumerate(steps):
            buffers, keeps, sends = step_call(
                arrived[step], *mats[step], buffers, which, chunks_of(layers, PARTS[step])
            )
            sums[step] = [keep + swap_core(send) for keep, send in zip(keeps, sends)]
        outputs[i] = exchange(buffers)

    zero, one = sums[0][0], sums[1][0]
    first_in = along(one, INWARD)
    second_mid = [along(value + along(value, INWARD), MIDDLE) for value in sums[2]]
    third_out = []
    cut = chunks_of(layers, PARTS[3])
    held = lax.optimization_barrier([one[min(c) : max(c) + 1] for c in cut])
    for j, value in enumerate(sums[3]):
        inward = value + along(value, INWARD)
        passed = held[j] + along(inward, MIDDLE)
        third_out.append(along(passed, OUTWARD))
    grad = (
        zero
        + first_in
        + jnp.concatenate(second_mid[::-1], axis=0)
        + jnp.concatenate(third_out[::-1], axis=0)
    )[:, None]
    new_one = 0.9 * moment_one + 0.1 * grad
    new_two = 0.999 * moment_two + 0.001 * grad * grad
    new_w = weights - 0.01 * (new_one / CORR_ONE) / (jnp.sqrt(new_two / CORR_TWO) + 1e-08)
    result = unpack(routes, outputs[0] + outputs[1], size, cap, groups)
    return (result, new_w, new_one, new_two)


def solution(mesh):
    placed = (
        P(("expert", "replica"), None),
        P(("expert", "replica"), None),
        P(("expert", "replica"), None),
        P(None, "expert", "replica", None),
        P(None, "expert", "replica", None),
        P(None, "expert", "replica", None),
    )
    return jax.shard_map(
        on_device,
        mesh=mesh,
        in_specs=placed,
        out_specs=(
            P(("expert", "replica"), None),
            P(None, "expert", "replica", None),
            P(None, "expert", "replica", None),
            P(None, "expert", "replica", None),
        ),
        check_vma=False,
    )
```

profile of v0, /device:TPU:0, one launch (start us, length us, event | category | flops | bytes accessed | tf_op | source)
XLA Modules:
  0.0 215.9 jit_solution(15305506490733205119)
XLA Ops:
  1.4 5.9 %collective-permute-start.9 = (f32[7,128,256]{2,1,0:T(8,128)}, f32[7,128,256]{2,1,0:T(8,128)S(1)}, u32[]{:S(2)}, u32[]{:S(2)}) collective-permute-start(f32[7,128,256]{2,1,0:T(8,128)} %bitcast.43), channel_id=1, source_target_pairs={{0,8},{2,10},{4,12},{6,14},{8,0},{10,2},{12,4},{14,6},{16,24},{18,... | collective-permute-start | bytes 2752520 | tf_op jit(solution)/shard_map/ppermute | solution.py:258
  7.2 1.3 collective-permute-start.4
  9.2 1.2 copy-done.3
  10.5 1.2 copy-done.4
  11.7 2.7 %pack.2 = (f32[2,128,256]{2,1,0:T(8,128)S(1)}, f32[2,128,256]{2,1,0:T(8,128)S(1)}, f32[2,128,256]{2,1,0:T(8,128)S(1)}, f32[2,128,256]{2,1,0:T(8,128)S(1)}, f32[2...) custom-call(s32[1,1024]{1,0:T(1,128)S(1)} %bitcast.46, ...), custom_call_target="tpu_custom_call" | custom-call | flops 2147483648 | bytes 3145728 | tf_op jit(solution)/shard_map/pack/pallas_call | solution.py:78
  14.4 1.6 collective-permute-start.6
  15.9 11.6 %collective-permute-done.9.refs_4_ = f32[7,128,256]{2,1,0:T(8,128)S(1)} collective-permute-done((f32[7,128,256]{2,1,0:T(8,128)}, f32[7,128,256]{2,1,0:T(8,128)S(1)}, u32[]{:S(2)}, u32[]{:S(2)}) %collective-permute-start.9) | collective-permute-done | bytes 917536 | tf_op jit(solution)/shard_map/ppermute | solution.py:258
  27.5 1.6 collective-permute-start.17
  29.1 1.5 collective-permute-start.7
  30.7 1.4 collective-permute-start.8
  32.1 11.4 %collective-permute-done.7.refs_2_ = f32[2,128,256]{2,1,0:T(8,128)S(1)} collective-permute-done((f32[2,128,256]{2,1,0:T(8,128)S(1)}, f32[2,128,256]{2,1,0:T(8,128)S(1)}, u32[]{:S(2)}, u32[]{:S(2)}) %collective-permute-start.7) | collective-permute-done | bytes 262176 | tf_op jit(solution)/shard_map/ppermute | solution.py:267
  43.5 1.5 collective-permute-start
  45.0 2.7 %pack.3 = (f32[2,128,256]{2,1,0:T(8,128)S(1)}, f32[2,128,256]{2,1,0:T(8,128)S(1)}, f32[2,128,256]{2,1,0:T(8,128)S(1)}, f32[2,128,256]{2,1,0:T(8,128)S(1)}, f32[2...) custom-call(s32[1,1024]{1,0:T(1,128)S(1)} %bitcast.47, ...), custom_call_target="tpu_custom_call" | custom-call | flops 2147483648 | bytes 3145728 | tf_op jit(solution)/shard_map/pack/pallas_call | solution.py:78
  47.7 3.6 %collective-permute-done.refs_1_ = f32[2,128,256]{2,1,0:T(8,128)S(1)} collective-permute-done((f32[2,128,256]{2,1,0:T(8,128)S(1)}, f32[2,128,256]{2,1,0:T(8,128)S(1)}, u32[]{:S(2)}, u32[]{:S(2)}) %collective-permute-start) | collective-permute-done | bytes 262176 | tf_op jit(solution)/shard_map/ppermute | solution.py:267
  51.3 1.5 collective-permute-start.1
  52.9 1.5 collective-permute-start.20
  54.3 1.3 collective-permute-start.18
  55.8 2.6 %collective-permute-done.1.refs_2_ = f32[2,128,256]{2,1,0:T(8,128)S(1)} collective-permute-done((f32[2,128,256]{2,1,0:T(8,128)S(1)}, f32[2,128,256]{2,1,0:T(8,128)S(1)}, u32[]{:S(2)}, u32[]{:S(2)}) %collective-permute-start.1) | collective-permute-done | bytes 262176 | tf_op jit(solution)/shard_map/ppermute | solution.py:267
  58.3 1.5 collective-permute-start.21
  59.9 1.4 collective-permute-start.22
  61.3 7.1 %step.4 = (f32[2,128,256]{2,1,0:T(8,128)S(1)}, f32[2,128,256]{2,1,0:T(8,128)S(1)}, f32[2,128,256]{2,1,0:T(8,128)S(1)}, f32[2,128,256]{2,1,0:T(8,128)S(1)}, f32[7...) custom-call(f32[2,128,256]{2,1,0:T(8,128)S(1)} %get-tuple-element.60.refs_0_, ...), custom_call_target="tpu_custom_call" | custom-call | flops 4227858432 | bytes 5242880 | tf_op jit(solution)/shard_map/step/pallas_call | solution.py:200
  68.4 1.7 collective-permute-done.21.refs_2_
  70.1 2.4 %collective-permute-start.2 = (f32[2,128,256]{2,1,0:T(8,128)S(1)}, f32[2,128,256]{2,1,0:T(8,128)S(1)}, u32[]{:S(2)}, u32[]{:S(2)}) collective-permute-start(f32[2,128,256]{2,1,0:T(8,128)S(1)} %get-tuple-element.59), channel_id=1, source_target_pairs={{0,6},{2,4},{4,2},{6,0},{8,14},{10,12},{12,10},{14,8},{16,22},{18,... | collective-permute-start | bytes 786440 | tf_op jit(solution)/shard_map/ppermute | solution.py:267
  73.1 6.9 %step.6 = (f32[2,128,256]{2,1,0:T(8,128)S(1)}, f32[2,128,256]{2,1,0:T(8,128)S(1)}, f32[2,128,256]{2,1,0:T(8,128)S(1)}, f32[2,128,256]{2,1,0:T(8,128)S(1)}, f32[7...) custom-call(f32[2,128,256]{2,1,0:T(8,128)S(1)} %get-tuple-element.76.refs_0_, ...), custom_call_target="tpu_custom_call" | custom-call | flops 4227858432 | bytes 5242880 | tf_op jit(solution)/shard_map/step/pallas_call | solution.py:200
  80.0 4.8 %collective-permute-done.18 = f32[7,128,256]{2,1,0:T(8,128)} collective-permute-done((f32[7,128,256]{2,1,0:T(8,128)}, f32[7,128,256]{2,1,0:T(8,128)}, u32[]{:S(2)}, u32[]{:S(2)}) %collective-permute-start.18) | collective-permute-done | bytes 917536 | tf_op jit(solution)/shard_map/ppermute | solution.py:258
  84.8 1.6 add.82.refs_4_
  87.5 2.4 %collective-permute-start.16 = (f32[2,128,256]{2,1,0:T(8,128)S(1)}, f32[2,128,256]{2,1,0:T(8,128)S(1)}, u32[]{:S(2)}, u32[]{:S(2)}) collective-permute-start(f32[2,128,256]{2,1,0:T(8,128)S(1)} %get-tuple-element.75), channel_id=1, source_target_pairs={{0,6},{2,4},{4,2},{6,0},{8,14},{10,12},{12,10},{14,8},{16,22},{18,... | collective-permute-start | bytes 786440 | tf_op jit(solution)/shard_map/ppermute | solution.py:267
  89.9 6.9 %step.5 = (f32[2,128,256]{2,1,0:T(8,128)S(1)}, f32[2,128,256]{2,1,0:T(8,128)S(1)}, f32[2,128,256]{2,1,0:T(8,128)S(1)}, f32[2,128,256]{2,1,0:T(8,128)S(1)}, f32[4...) custom-call(f32[2,128,256]{2,1,0:T(8,128)S(1)} %get-tuple-element.56, ...), custom_call_target="tpu_custom_call", output_to_operand_aliasing={{0}: (6, {}), {1}: (7, {}), {2}: (8, {}), {3}: (9, {})} | custom-call | flops 4227858432 | bytes 5242880 | tf_op jit(solution)/shard_map/step/pallas_call | solution.py:200
  97.5 1.3 add.84
  98.8 2.1 collective-permute-done.15.refs_2_
  101.4 9.0 %collective-permute-start.29 = (f32[7,128,256]{2,1,0:T(8,128)S(1)}, f32[7,128,256]{2,1,0:T(8,128)S(1)}, u32[]{:S(2)}, u32[]{:S(2)}) collective-permute-start(f32[7,128,256]{2,1,0:T(8,128)S(1)} %add.84), channel_id=1, source_target_pairs={{0,8},{2,10},{4,12},{6,14},{24,16},{26,18},{28,20},{30,22},{1,9},{... | collective-permute-start | bytes 2752520 | tf_op jit(solution)/shard_map/ppermute | solution.py:258
  111.0 1.5 collective-permute-start.13
  112.5 6.9 %step.7 = (f32[2,128,256]{2,1,0:T(8,128)S(1)}, f32[2,128,256]{2,1,0:T(8,128)S(1)}, f32[2,128,256]{2,1,0:T(8,128)S(1)}, f32[2,128,256]{2,1,0:T(8,128)S(1)}, f32[2...) custom-call(f32[2,128,256]{2,1,0:T(8,128)S(1)} %copy-done.14, ...), custom_call_target="tpu_custom_call", output_to_operand_aliasing={{0}: (6, {}), {1}: (7, {}), {2}: (8, {}), {3}: (9, {})} | custom-call | flops 4227858432 | bytes 5242880 | tf_op jit(solution)/shard_map/step/pallas_call | solution.py:200
  120.1 4.0 %collective-permute-done.12.refs_2_ = f32[2,128,256]{2,1,0:T(8,128)S(1)} collective-permute-done((f32[2,128,256]{2,1,0:T(8,128)S(1)}, f32[2,128,256]{2,1,0:T(8,128)S(1)}, u32[]{:S(2)}, u32[]{:S(2)}) %collective-permute-start.12) | collective-permute-done | bytes 262176 | tf_op jit(solution)/shard_map/ppermute | solution.py:267
  124.0 1.5 collective-permute-start.31
  126.3 1.3 collective-permute-start.34
  127.6 1.3 collective-permute-start.41
  129.0 1.3 collective-permute-start.45
  130.4 8.9 %collective-permute-done.31 = f32[3,128,256]{2,1,0:T(8,128)S(1)} collective-permute-done((f32[3,128,256]{2,1,0:T(8,128)S(1)}, f32[3,128,256]{2,1,0:T(8,128)S(1)}, u32[]{:S(2)}, u32[]{:S(2)}) %collective-permute-start.31) | collective-permute-done | bytes 393248 | tf_op jit(solution)/shard_map/ppermute | solution.py:258
  139.3 4.4 %collective-permute-start.49 = (f32[2,128,256]{2,1,0:T(8,128)S(1)}, f32[2,128,256]{2,1,0:T(8,128)S(1)}, u32[]{:S(2)}, u32[]{:S(2)}) collective-permute-start(f32[2,128,256]{2,1,0:T(8,128)S(1)} %add.100), channel_id=1, source_target_pairs={{0,8},{2,10},{4,12},{6,14},{24,16},{26,18},{28,20},{30,22},{1,9},{... | collective-permute-start | bytes 786440 | tf_op jit(solution)/shard_map/ppermute | solution.py:258
  144.4 11.7 %collective-permute-done.41 = f32[2,128,256]{2,1,0:T(8,128)S(1)} collective-permute-done((f32[2,128,256]{2,1,0:T(8,128)S(1)}, f32[2,128,256]{2,1,0:T(8,128)S(1)}, u32[]{:S(2)}, u32[]{:S(2)}) %collective-permute-start.41) | collective-permute-done | bytes 262176 | tf_op jit(solution)/shard_map/ppermute | solution.py:258
  156.2 5.6 %collective-permute-done.45 = f32[2,128,256]{2,1,0:T(8,128)S(1)} collective-permute-done((f32[2,128,256]{2,1,0:T(8,128)S(1)}, f32[2,128,256]{2,1,0:T(8,128)S(1)}, u32[]{:S(2)}, u32[]{:S(2)}) %collective-permute-start.45) | collective-permute-done | bytes 262176 | tf_op jit(solution)/shard_map/ppermute | solution.py:258
  162.5 4.0 %collective-permute-done.49 = f32[2,128,256]{2,1,0:T(8,128)S(1)} collective-permute-done((f32[2,128,256]{2,1,0:T(8,128)S(1)}, f32[2,128,256]{2,1,0:T(8,128)S(1)}, u32[]{:S(2)}, u32[]{:S(2)}) %collective-permute-start.49) | collective-permute-done | bytes 262176 | tf_op jit(solution)/shard_map/ppermute | solution.py:258
  167.9 8.9 %collective-permute-start.37 = (f32[1,128,256]{2,1,0:T(8,128)S(1)}, f32[1,128,256]{2,1,0:T(8,128)S(1)}, u32[]{:S(2)}, u32[]{:S(2)}) collective-permute-start(f32[1,128,256]{2,1,0:T(8,128)S(1)} %add.91), channel_id=1, source_target_pairs={{0,8},{2,10},{4,12},{6,14},{24,16},{26,18},{28,20},{30,22},{1,9},{... | collective-permute-start | bytes 393224 | tf_op jit(solution)/shard_map/ppermute | solution.py:258
  176.8 0.9 add.89
  178.2 1.1 collective-permute-done.37
  179.8 1.5 collective-permute-start.35
  181.3 1.5 collective-permute-start.26
  182.8 1.3 collective-permute-start.38
  185.0 0.8 add.99
  185.7 0.8 add.102
  187.2 1.3 collective-permute-start.43
  188.5 2.5 %collective-permute-done.25.refs_6_ = f32[2,128,256]{2,1,0:T(8,128)S(1)} collective-permute-done((f32[2,128,256]{2,1,0:T(8,128)S(1)}, f32[2,128,256]{2,1,0:T(8,128)S(1)}, u32[]{:S(2)}, u32[]{:S(2)}) %collective-permute-start.25) | collective-permute-done | bytes 262176 | tf_op jit(solution)/shard_map/ppermute | solution.py:267
  191.7 1.3 collective-permute-start.47
  193.0 1.3 collective-permute-start.51
  194.6 1.0 add.93
  195.5 1.3 collective-permute-start.39
  196.9 0.9 copy-done.8
  197.8 0.9 copy-done.10
  198.8 0.9 copy-done.12
  199.7 7.0 %unpack.1 = f32[1024,256]{1,0:T(8,128)} custom-call(s32[1024,1]{1,0:T(8,128)S(1)} %copy.18.route_ref, f32[2,128,256]{2,1,0:T(8,128)S(1)} %copy-done.12, f32[2,128,256]{2,1,0:T(8,128)S(1)} %collective-permute-done.11.refs_1_, f32[2,128,256]{2,1,0:T(8,128)S(1)} %collective-permute-done.12.refs_2_, f32[2,128,256]{2,1,0:T(8,128)S(1)} %collective-permute-done.13.refs_3_, ...), custom_call_target="tpu_custom_call" | custom-call | flops 2147483648 | bytes 3145728 | tf_op jit(solution)/shard_map/unpack/pallas_call | solution.py:118
  206.7 4.6 %collective-permute-done.39 = f32[1,128,256]{2,1,0:T(8,128)S(1)} collective-permute-done((f32[1,128,256]{2,1,0:T(8,128)S(1)}, f32[1,128,256]{2,1,0:T(8,128)S(1)}, u32[]{:S(2)}, u32[]{:S(2)}) %collective-permute-start.39) | collective-permute-done | bytes 131104 | tf_op jit(solution)/shard_map/ppermute | solution.py:258
  211.4 2.7 %fusion.5 = (f32[7,1,128,256]{3,2,1,0:T(8,128)}, f32[7,128,256]{2,1,0:T(8,128)S(1)}) fusion(f32[7,1,128,256]{3,2,1,0:T(8,128)S(1)} %copy-done.15, f32[2,128,256]{2,1,0:T(8,128)} %collective-permute-done.51, f32[2,128,256]{2,1,0:T(8,128)} %collective-permute-done.47, f32[2,128,256]{2,1,0:T(8,128)} %collective-permute-done.43, ...), kind=kLoop, calls=%fused_computation.11 | loop fusion | flops 2752512 | bytes 7340032
  214.1 1.8 fusion.4
  (117 shorter events, 12.8 us)
Async XLA Ops:
  0.6 6.6 %collective-permute-start.3 = (f32[7,128,256]{2,1,0:T(8,128)}, f32[7,128,256]{2,1,0:T(8,128)S(1)}, u32[]{:S(2)}, u32[]{:S(2)}) collective-permute-start(f32[7,128,256]{2,1,0:T(8,128)} %bitcast.42), channel_id=1, source_target_pairs={{8,16},{10,18},{12,20},{14,22},{16,8},{18,10},{20,12},{22,14},{9,1... | collective-permute-start | bytes 2752520 | tf_op jit(solution)/shard_map/ppermute | solution.py:258
  1.4 26.2 %collective-permute-start.9 = (f32[7,128,256]{2,1,0:T(8,128)}, f32[7,128,256]{2,1,0:T(8,128)S(1)}, u32[]{:S(2)}, u32[]{:S(2)}) collective-permute-start(f32[7,128,256]{2,1,0:T(8,128)} %bitcast.43), channel_id=1, source_target_pairs={{0,8},{2,10},{4,12},{6,14},{8,0},{10,2},{12,4},{14,6},{16,24},{18,... | collective-permute-start | bytes 2752520 | tf_op jit(solution)/shard_map/ppermute | solution.py:258
  7.2 45.6 %collective-permute-start.4 = (f32[7,128,256]{2,1,0:T(8,128)S(1)}, f32[7,128,256]{2,1,0:T(8,128)S(1)}, u32[]{:S(2)}, u32[]{:S(2)}) collective-permute-start(f32[7,128,256]{2,1,0:T(8,128)S(1)} %collective-permute-done.3), channel_id=1, source_target_pairs={{8,0},{10,2},{12,4},{14,6},{16,24},{18,26},{20,28},{22,30},{9,1},{... | collective-permute-start | bytes 2752520 | tf_op jit(solution)/shard_map/ppermute | solution.py:258
  11.7 33.3 %copy-start = (f32[7,1,128,256]{3,2,1,0:T(8,128)S(1)}, f32[7,1,128,256]{3,2,1,0:T(8,128)}, u32[]{:S(2)}) copy-start(f32[7,1,128,256]{3,2,1,0:T(8,128)} %param.9) | copy-start | bytes 2752516
  14.4 16.3 %collective-permute-start.6 = (f32[2,128,256]{2,1,0:T(8,128)S(1)}, f32[2,128,256]{2,1,0:T(8,128)S(1)}, u32[]{:S(2)}, u32[]{:S(2)}) collective-permute-start(f32[2,128,256]{2,1,0:T(8,128)S(1)} %get-tuple-element.61), channel_id=1, source_target_pairs={{0,2},{2,0},{4,6},{6,4},{8,10},{10,8},{12,14},{14,12},{16,18},{18,... | collective-permute-start | bytes 786440 | tf_op jit(solution)/shard_map/ppermute | solution.py:267
  27.5 26.8 %collective-permute-start.17 = (f32[7,128,256]{2,1,0:T(8,128)S(1)}, f32[7,128,256]{2,1,0:T(8,128)}, u32[]{:S(2)}, u32[]{:S(2)}) collective-permute-start(f32[7,128,256]{2,1,0:T(8,128)S(1)} %collective-permute-done.9.refs_4_), channel_id=1, source_target_pairs={{8,16},{10,18},{12,20},{14,22},{16,8},{18,10},{20,12},{22,14},{9,1... | collective-permute-start | bytes 2752520 | tf_op jit(solution)/shard_map/ppermute | solution.py:258
  29.1 32.2 %collective-permute-start.10 = (f32[7,128,256]{2,1,0:T(8,128)S(1)}, f32[7,128,256]{2,1,0:T(8,128)S(1)}, u32[]{:S(2)}, u32[]{:S(2)}) collective-permute-start(f32[7,128,256]{2,1,0:T(8,128)S(1)} %collective-permute-done.9.refs_4_), channel_id=1, source_target_pairs={{0,1},{1,0},{2,3},{3,2},{4,5},{5,4},{6,7},{7,6},{8,9},{9,8},{10,11... | collective-permute-start | bytes 2752520 | tf_op jit(solution)/shard_map/ppermute | solution.py:261
  29.1 14.3 %collective-permute-start.7 = (f32[2,128,256]{2,1,0:T(8,128)S(1)}, f32[2,128,256]{2,1,0:T(8,128)S(1)}, u32[]{:S(2)}, u32[]{:S(2)}) collective-permute-start(f32[2,128,256]{2,1,0:T(8,128)S(1)} %get-tuple-element.62), channel_id=1, source_target_pairs={{0,4},{2,6},{4,0},{6,2},{8,12},{10,14},{12,8},{14,10},{16,20},{18,... | collective-permute-start | bytes 786440 | tf_op jit(solution)/shard_map/ppermute | solution.py:267
  30.7 14.3 %collective-permute-start.8 = (f32[2,128,256]{2,1,0:T(8,128)S(1)}, f32[2,128,256]{2,1,0:T(8,128)S(1)}, u32[]{:S(2)}, u32[]{:S(2)}) collective-permute-start(f32[2,128,256]{2,1,0:T(8,128)S(1)} %get-tuple-element.63), channel_id=1, source_target_pairs={{0,6},{2,4},{4,2},{6,0},{8,14},{10,12},{12,10},{14,8},{16,22},{18,... | collective-permute-start | bytes 786440 | tf_op jit(solution)/shard_map/ppermute | solution.py:267
  43.5 7.9 %collective-permute-start = (f32[2,128,256]{2,1,0:T(8,128)S(1)}, f32[2,128,256]{2,1,0:T(8,128)S(1)}, u32[]{:S(2)}, u32[]{:S(2)}) collective-permute-start(f32[2,128,256]{2,1,0:T(8,128)S(1)} %get-tuple-element.57), channel_id=1, source_target_pairs={{0,2},{2,0},{4,6},{6,4},{8,10},{10,8},{12,14},{14,12},{16,18},{18,... | collective-permute-start | bytes 786440 | tf_op jit(solution)/shard_map/ppermute | solution.py:267
  45.0 28.1 %collective-permute-start.23 = (f32[7,128,256]{2,1,0:T(8,128)S(1)}, f32[7,128,256]{2,1,0:T(8,128)S(1)}, u32[]{:S(2)}, u32[]{:S(2)}) collective-permute-start(f32[7,128,256]{2,1,0:T(8,128)S(1)} %bitcast.44), channel_id=1, source_target_pairs={{0,1},{1,0},{2,3},{3,2},{4,5},{5,4},{6,7},{7,6},{8,9},{9,8},{10,11... | collective-permute-start | bytes 2752520 | tf_op jit(solution)/shard_map/ppermute | solution.py:261
  47.7 8.1 %copy-start.13 = (f32[2,128,256]{2,1,0:T(8,128)}, f32[2,128,256]{2,1,0:T(8,128)S(1)}, u32[]{:S(2)}) copy-start(f32[2,128,256]{2,1,0:T(8,128)S(1)} %get-tuple-element.72.refs_0_) | copy-start | bytes 786436
  51.3 7.0 %collective-permute-start.1 = (f32[2,128,256]{2,1,0:T(8,128)S(1)}, f32[2,128,256]{2,1,0:T(8,128)S(1)}, u32[]{:S(2)}, u32[]{:S(2)}) collective-permute-start(f32[2,128,256]{2,1,0:T(8,128)S(1)} %get-tuple-element.58), channel_id=1, source_target_pairs={{0,4},{2,6},{4,0},{6,2},{8,12},{10,14},{12,8},{14,10},{16,20},{18,... | collective-permute-start | bytes 786440 | tf_op jit(solution)/shard_map/ppermute | solution.py:267
  52.9 7.0 %collective-permute-start.20 = (f32[2,128,256]{2,1,0:T(8,128)S(1)}, f32[2,128,256]{2,1,0:T(8,128)S(1)}, u32[]{:S(2)}, u32[]{:S(2)}) collective-permute-start(f32[2,128,256]{2,1,0:T(8,128)S(1)} %get-tuple-element.77), channel_id=1, source_target_pairs={{0,2},{2,0},{4,6},{6,4},{8,10},{10,8},{12,14},{14,12},{16,18},{18,... | collective-permute-start | bytes 786440 | tf_op jit(solution)/shard_map/ppermute | solution.py:267
  54.3 30.5 %collective-permute-start.18 = (f32[7,128,256]{2,1,0:T(8,128)}, f32[7,128,256]{2,1,0:T(8,128)}, u32[]{:S(2)}, u32[]{:S(2)}) collective-permute-start(f32[7,128,256]{2,1,0:T(8,128)} %collective-permute-done.17), channel_id=1, source_target_pairs={{8,0},{10,2},{12,4},{14,6},{16,24},{18,26},{20,28},{22,30},{9,1},{... | collective-permute-start | bytes 2752520 | tf_op jit(solution)/shard_map/ppermute | solution.py:258
  58.3 11.8 %collective-permute-start.21 = (f32[2,128,256]{2,1,0:T(8,128)S(1)}, f32[2,128,256]{2,1,0:T(8,128)S(1)}, u32[]{:S(2)}, u32[]{:S(2)}) collective-permute-start(f32[2,128,256]{2,1,0:T(8,128)S(1)} %get-tuple-element.78), channel_id=1, source_target_pairs={{0,4},{2,6},{4,0},{6,2},{8,12},{10,14},{12,8},{14,10},{16,20},{18,... | collective-permute-start | bytes 786440 | tf_op jit(solution)/shard_map/ppermute | solution.py:267
  59.9 12.7 %collective-permute-start.22 = (f32[2,128,256]{2,1,0:T(8,128)S(1)}, f32[2,128,256]{2,1,0:T(8,128)S(1)}, u32[]{:S(2)}, u32[]{:S(2)}) collective-permute-start(f32[2,128,256]{2,1,0:T(8,128)S(1)} %get-tuple-element.79), channel_id=1, source_target_pairs={{0,6},{2,4},{4,2},{6,0},{8,14},{10,12},{12,10},{14,8},{16,22},{18,... | collective-permute-start | bytes 786440 | tf_op jit(solution)/shard_map/ppermute | solution.py:267
  61.3 26.2 %collective-permute-start.5 = (f32[7,128,256]{2,1,0:T(8,128)S(1)}, f32[7,128,256]{2,1,0:T(8,128)S(1)}, u32[]{:S(2)}, u32[]{:S(2)}) collective-permute-start(f32[7,128,256]{2,1,0:T(8,128)S(1)} %add.81.refs_4_), channel_id=1, source_target_pairs={{0,1},{1,0},{2,3},{3,2},{4,5},{5,4},{6,7},{7,6},{8,9},{9,8},{10,11... | collective-permute-start | bytes 2752520 | tf_op jit(solution)/shard_map/ppermute | solution.py:261
  70.1 16.3 %collective-permute-start.2 = (f32[2,128,256]{2,1,0:T(8,128)S(1)}, f32[2,128,256]{2,1,0:T(8,128)S(1)}, u32[]{:S(2)}, u32[]{:S(2)}) collective-permute-start(f32[2,128,256]{2,1,0:T(8,128)S(1)} %get-tuple-element.59), channel_id=1, source_target_pairs={{0,6},{2,4},{4,2},{6,0},{8,14},{10,12},{12,10},{14,8},{16,22},{18,... | collective-permute-start | bytes 786440 | tf_op jit(solution)/shard_map/ppermute | solution.py:267
  72.6 14.4 %collective-permute-start.14 = (f32[2,128,256]{2,1,0:T(8,128)S(1)}, f32[2,128,256]{2,1,0:T(8,128)S(1)}, u32[]{:S(2)}, u32[]{:S(2)}) collective-permute-start(f32[2,128,256]{2,1,0:T(8,128)S(1)} %get-tuple-element.73), channel_id=1, source_target_pairs={{0,2},{2,0},{4,6},{6,4},{8,10},{10,8},{12,14},{14,12},{16,18},{18,... | collective-permute-start | bytes 786440 | tf_op jit(solution)/shard_map/ppermute | solution.py:267
  73.1 23.8 %collective-permute-start.28 = (f32[7,128,256]{2,1,0:T(8,128)S(1)}, f32[7,128,256]{2,1,0:T(8,128)}, u32[]{:S(2)}, u32[]{:S(2)}) collective-permute-start(f32[7,128,256]{2,1,0:T(8,128)S(1)} %get-tuple-element.91), channel_id=1, source_target_pairs={{0,1},{1,0},{2,3},{3,2},{4,5},{5,4},{6,7},{7,6},{8,9},{9,8},{10,11... | collective-permute-start | bytes 2752520 | tf_op jit(solution)/shard_map/ppermute | solution.py:261
  84.8 16.6 %collective-permute-start.27 = (f32[7,128,256]{2,1,0:T(8,128)S(1)}, f32[7,128,256]{2,1,0:T(8,128)S(1)}, u32[]{:S(2)}, u32[]{:S(2)}) collective-permute-start(f32[7,128,256]{2,1,0:T(8,128)S(1)} %get-tuple-element.89), channel_id=1, source_target_pairs={{0,1},{1,0},{2,3},{3,2},{4,5},{5,4},{6,7},{7,6},{8,9},{9,8},{10,11... | collective-permute-start | bytes 2752520 | tf_op jit(solution)/shard_map/ppermute | solution.py:261
  86.4 24.6 %collective-permute-start.19 = (f32[7,128,256]{2,1,0:T(8,128)S(1)}, f32[7,128,256]{2,1,0:T(8,128)S(1)}, u32[]{:S(2)}, u32[]{:S(2)}) collective-permute-start(f32[7,128,256]{2,1,0:T(8,128)S(1)} %add.82.refs_4_), channel_id=1, source_target_pairs={{0,1},{1,0},{2,3},{3,2},{4,5},{5,4},{6,7},{7,6},{8,9},{9,8},{10,11... | collective-permute-start | bytes 2752520 | tf_op jit(solution)/shard_map/ppermute | solution.py:261
  87.0 13.9 %collective-permute-start.15 = (f32[2,128,256]{2,1,0:T(8,128)S(1)}, f32[2,128,256]{2,1,0:T(8,128)S(1)}, u32[]{:S(2)}, u32[]{:S(2)}) collective-permute-start(f32[2,128,256]{2,1,0:T(8,128)S(1)} %get-tuple-element.74), channel_id=1, source_target_pairs={{0,4},{2,6},{4,0},{6,2},{8,12},{10,14},{12,8},{14,10},{16,20},{18,... | collective-permute-start | bytes 786440 | tf_op jit(solution)/shard_map/ppermute | solution.py:267
  87.5 13.4 %collective-permute-start.16 = (f32[2,128,256]{2,1,0:T(8,128)S(1)}, f32[2,128,256]{2,1,0:T(8,128)S(1)}, u32[]{:S(2)}, u32[]{:S(2)}) collective-permute-start(f32[2,128,256]{2,1,0:T(8,128)S(1)} %get-tuple-element.75), channel_id=1, source_target_pairs={{0,6},{2,4},{4,2},{6,0},{8,14},{10,12},{12,10},{14,8},{16,22},{18,... | collective-permute-start | bytes 786440 | tf_op jit(solution)/shard_map/ppermute | solution.py:267
  96.9 13.5 %collective-permute-start.11 = (f32[2,128,256]{2,1,0:T(8,128)S(1)}, f32[2,128,256]{2,1,0:T(8,128)S(1)}, u32[]{:S(2)}, u32[]{:S(2)}) collective-permute-start(f32[2,128,256]{2,1,0:T(8,128)S(1)} %get-tuple-element.69), channel_id=1, source_target_pairs={{0,2},{2,0},{4,6},{6,4},{8,10},{10,8},{12,14},{14,12},{16,18},{18,... | collective-permute-start | bytes 786440 | tf_op jit(solution)/shard_map/ppermute | solution.py:267
  97.5 15.0 %copy-start.14 = (f32[2,128,256]{2,1,0:T(8,128)S(1)}, f32[2,128,256]{2,1,0:T(8,128)}, u32[]{:S(2)}) copy-start(f32[2,128,256]{2,1,0:T(8,128)} %copy-done.13) | copy-start | bytes 786436
  100.9 18.5 %collective-permute-start.30 = (f32[3,128,256]{2,1,0:T(8,128)S(1)}, f32[3,128,256]{2,1,0:T(8,128)S(1)}, u32[]{:S(2)}, u32[]{:S(2)}) collective-permute-start(f32[3,128,256]{2,1,0:T(8,128)S(1)} %get-tuple-element.93), channel_id=1, source_target_pairs={{0,1},{1,0},{2,3},{3,2},{4,5},{5,4},{6,7},{7,6},{8,9},{9,8},{10,11... | collective-permute-start | bytes 1179656 | tf_op jit(solution)/shard_map/ppermute | solution.py:261
  100.9 24.8 %collective-permute-start.33 = (f32[4,128,256]{2,1,0:T(8,128)S(1)}, f32[4,128,256]{2,1,0:T(8,128)S(1)}, u32[]{:S(2)}, u32[]{:S(2)}) collective-permute-start(f32[4,128,256]{2,1,0:T(8,128)S(1)} %get-tuple-element.95), channel_id=1, source_target_pairs={{0,1},{1,0},{2,3},{3,2},{4,5},{5,4},{6,7},{7,6},{8,9},{9,8},{10,11... | collective-permute-start | bytes 1572872 | tf_op jit(solution)/shard_map/ppermute | solution.py:261
  101.4 11.0 %copy-start.16 = (f32[7,128,256]{2,1,0:T(8,128)}, f32[7,128,256]{2,1,0:T(8,128)S(1)}, u32[]{:S(2)}) copy-start(f32[7,128,256]{2,1,0:T(8,128)S(1)} %collective-permute-done.27) | copy-start | bytes 2752516
  101.4 42.3 %collective-permute-start.29 = (f32[7,128,256]{2,1,0:T(8,128)S(1)}, f32[7,128,256]{2,1,0:T(8,128)S(1)}, u32[]{:S(2)}, u32[]{:S(2)}) collective-permute-start(f32[7,128,256]{2,1,0:T(8,128)S(1)} %add.84), channel_id=1, source_target_pairs={{0,8},{2,10},{4,12},{6,14},{24,16},{26,18},{28,20},{30,22},{1,9},{... | collective-permute-start | bytes 2752520 | tf_op jit(solution)/shard_map/ppermute | solution.py:258
  110.4 13.6 %collective-permute-start.12 = (f32[2,128,256]{2,1,0:T(8,128)S(1)}, f32[2,128,256]{2,1,0:T(8,128)S(1)}, u32[]{:S(2)}, u32[]{:S(2)}) collective-permute-start(f32[2,128,256]{2,1,0:T(8,128)S(1)} %get-tuple-element.70), channel_id=1, source_target_pairs={{0,4},{2,6},{4,0},{6,2},{8,12},{10,14},{12,8},{14,10},{16,20},{18,... | collective-permute-start | bytes 786440 | tf_op jit(solution)/shard_map/ppermute | solution.py:267
  111.0 14.6 %collective-permute-start.13 = (f32[2,128,256]{2,1,0:T(8,128)S(1)}, f32[2,128,256]{2,1,0:T(8,128)S(1)}, u32[]{:S(2)}, u32[]{:S(2)}) collective-permute-start(f32[2,128,256]{2,1,0:T(8,128)S(1)} %get-tuple-element.71), channel_id=1, source_target_pairs={{0,6},{2,4},{4,2},{6,0},{8,14},{10,12},{12,10},{14,8},{16,22},{18,... | collective-permute-start | bytes 786440 | tf_op jit(solution)/shard_map/ppermute | solution.py:267
  119.4 6.9 %collective-permute-start.40 = (f32[2,128,256]{2,1,0:T(8,128)S(1)}, f32[2,128,256]{2,1,0:T(8,128)S(1)}, u32[]{:S(2)}, u32[]{:S(2)}) collective-permute-start(f32[2,128,256]{2,1,0:T(8,128)S(1)} %get-tuple-element.101), channel_id=1, source_target_pairs={{0,1},{1,0},{2,3},{3,2},{4,5},{5,4},{6,7},{7,6},{8,9},{9,8},{10,11... | collective-permute-start | bytes 786440 | tf_op jit(solution)/shard_map/ppermute | solution.py:261
  124.0 15.2 %collective-permute-start.31 = (f32[3,128,256]{2,1,0:T(8,128)S(1)}, f32[3,128,256]{2,1,0:T(8,128)S(1)}, u32[]{:S(2)}, u32[]{:S(2)}) collective-permute-start(f32[3,128,256]{2,1,0:T(8,128)S(1)} %add.86), channel_id=1, source_target_pairs={{0,8},{2,10},{4,12},{6,14},{24,16},{26,18},{28,20},{30,22},{1,9},{... | collective-permute-start | bytes 1179656 | tf_op jit(solution)/shard_map/ppermute | solution.py:258
  125.6 2.0 collective-permute-start.44
  125.7 3.3 %collective-permute-start.48 = (f32[2,128,256]{2,1,0:T(8,128)S(1)}, f32[2,128,256]{2,1,0:T(8,128)S(1)}, u32[]{:S(2)}, u32[]{:S(2)}) collective-permute-start(f32[2,128,256]{2,1,0:T(8,128)S(1)} %get-tuple-element.107), channel_id=1, source_target_pairs={{0,1},{1,0},{2,3},{3,2},{4,5},{5,4},{6,7},{7,6},{8,9},{9,8},{10,11... | collective-permute-start | bytes 786440 | tf_op jit(solution)/shard_map/ppermute | solution.py:261
  126.3 41.6 %collective-permute-start.34 = (f32[4,128,256]{2,1,0:T(8,128)S(1)}, f32[4,128,256]{2,1,0:T(8,128)S(1)}, u32[]{:S(2)}, u32[]{:S(2)}) collective-permute-start(f32[4,128,256]{2,1,0:T(8,128)S(1)} %add.88), channel_id=1, source_target_pairs={{0,8},{2,10},{4,12},{6,14},{24,16},{26,18},{28,20},{30,22},{1,9},{... | collective-permute-start | bytes 1572872 | tf_op jit(solution)/shard_map/ppermute | solution.py:258
  127.6 28.5 %collective-permute-start.41 = (f32[2,128,256]{2,1,0:T(8,128)S(1)}, f32[2,128,256]{2,1,0:T(8,128)S(1)}, u32[]{:S(2)}, u32[]{:S(2)}) collective-permute-start(f32[2,128,256]{2,1,0:T(8,128)S(1)} %add.94), channel_id=1, source_target_pairs={{0,8},{2,10},{4,12},{6,14},{24,16},{26,18},{28,20},{30,22},{1,9},{... | collective-permute-start | bytes 786440 | tf_op jit(solution)/shard_map/ppermute | solution.py:258
  129.0 32.7 %collective-permute-start.45 = (f32[2,128,256]{2,1,0:T(8,128)S(1)}, f32[2,128,256]{2,1,0:T(8,128)S(1)}, u32[]{:S(2)}, u32[]{:S(2)}) collective-permute-start(f32[2,128,256]{2,1,0:T(8,128)S(1)} %add.97), channel_id=1, source_target_pairs={{0,8},{2,10},{4,12},{6,14},{24,16},{26,18},{28,20},{30,22},{1,9},{... | collective-permute-start | bytes 786440 | tf_op jit(solution)/shard_map/ppermute | solution.py:258
  139.3 27.1 %collective-permute-start.49 = (f32[2,128,256]{2,1,0:T(8,128)S(1)}, f32[2,128,256]{2,1,0:T(8,128)S(1)}, u32[]{:S(2)}, u32[]{:S(2)}) collective-permute-start(f32[2,128,256]{2,1,0:T(8,128)S(1)} %add.100), channel_id=1, source_target_pairs={{0,8},{2,10},{4,12},{6,14},{24,16},{26,18},{28,20},{30,22},{1,9},{... | collective-permute-start | bytes 786440 | tf_op jit(solution)/shard_map/ppermute | solution.py:258
  143.7 23.4 %copy-start.18 = (f32[7,128,256]{2,1,0:T(8,128)}, f32[7,128,256]{2,1,0:T(8,128)S(1)}, u32[]{:S(2)}) copy-start(f32[7,128,256]{2,1,0:T(8,128)S(1)} %collective-permute-done.29) | copy-start | bytes 2752516
  143.7 33.9 %collective-permute-start.32 = (f32[3,128,256]{2,1,0:T(8,128)S(1)}, f32[3,128,256]{2,1,0:T(8,128)S(1)}, u32[]{:S(2)}, u32[]{:S(2)}) collective-permute-start(f32[3,128,256]{2,1,0:T(8,128)S(1)} %add.87), channel_id=1, source_target_pairs={{8,16},{10,18},{12,20},{14,22},{16,8},{18,10},{20,12},{22,14},{9,1... | collective-permute-start | bytes 1179656 | tf_op jit(solution)/shard_map/ppermute | solution.py:258
  156.1 11.0 %collective-permute-start.36 = (f32[1,128,256]{2,1,0:T(8,128)S(1)}, f32[1,128,256]{2,1,0:T(8,128)S(1)}, u32[]{:S(2)}, u32[]{:S(2)}) collective-permute-start(f32[1,128,256]{2,1,0:T(8,128)S(1)} %get-tuple-element.98), channel_id=1, source_target_pairs={{0,1},{1,0},{2,3},{3,2},{4,5},{5,4},{6,7},{7,6},{8,9},{9,8},{10,11... | collective-permute-start | bytes 393224 | tf_op jit(solution)/shard_map/ppermute | solution.py:261
  161.7 18.0 %collective-permute-start.42 = (f32[2,128,256]{2,1,0:T(8,128)S(1)}, f32[2,128,256]{2,1,0:T(8,128)S(1)}, u32[]{:S(2)}, u32[]{:S(2)}) collective-permute-start(f32[2,128,256]{2,1,0:T(8,128)S(1)} %add.95), channel_id=1, source_target_pairs={{8,16},{10,18},{12,20},{14,22},{16,8},{18,10},{20,12},{22,14},{9,1... | collective-permute-start | bytes 786440 | tf_op jit(solution)/shard_map/ppermute | solution.py:258
  166.4 14.9 %collective-permute-start.46 = (f32[2,128,256]{2,1,0:T(8,128)S(1)}, f32[2,128,256]{2,1,0:T(8,128)S(1)}, u32[]{:S(2)}, u32[]{:S(2)}) collective-permute-start(f32[2,128,256]{2,1,0:T(8,128)S(1)} %add.98), channel_id=1, source_target_pairs={{8,16},{10,18},{12,20},{14,22},{16,8},{18,10},{20,12},{22,14},{9,1... | collective-permute-start | bytes 786440 | tf_op jit(solution)/shard_map/ppermute | solution.py:258
  167.2 15.7 %collective-permute-start.50 = (f32[2,128,256]{2,1,0:T(8,128)S(1)}, f32[2,128,256]{2,1,0:T(8,128)S(1)}, u32[]{:S(2)}, u32[]{:S(2)}) collective-permute-start(f32[2,128,256]{2,1,0:T(8,128)S(1)} %add.101), channel_id=1, source_target_pairs={{8,16},{10,18},{12,20},{14,22},{16,8},{18,10},{20,12},{22,14},{9,1... | collective-permute-start | bytes 786440 | tf_op jit(solution)/shard_map/ppermute | solution.py:258
  167.9 11.4 %collective-permute-start.37 = (f32[1,128,256]{2,1,0:T(8,128)S(1)}, f32[1,128,256]{2,1,0:T(8,128)S(1)}, u32[]{:S(2)}, u32[]{:S(2)}) collective-permute-start(f32[1,128,256]{2,1,0:T(8,128)S(1)} %add.91), channel_id=1, source_target_pairs={{0,8},{2,10},{4,12},{6,14},{24,16},{26,18},{28,20},{30,22},{1,9},{... | collective-permute-start | bytes 393224 | tf_op jit(solution)/shard_map/ppermute | solution.py:258
  177.6 6.6 %copy-start.21 = (f32[3,128,256]{2,1,0:T(8,128)}, f32[3,128,256]{2,1,0:T(8,128)S(1)}, u32[]{:S(2)}) copy-start(f32[3,128,256]{2,1,0:T(8,128)S(1)} %collective-permute-done.32) | copy-start | bytes 1179652
  177.6 8.9 %collective-permute-start.24 = (f32[2,128,256]{2,1,0:T(8,128)S(1)}, f32[2,128,256]{2,1,0:T(8,128)S(1)}, u32[]{:S(2)}, u32[]{:S(2)}) collective-permute-start(f32[2,128,256]{2,1,0:T(8,128)S(1)} %get-tuple-element.85), channel_id=1, source_target_pairs={{0,2},{2,0},{4,6},{6,4},{8,10},{10,8},{12,14},{14,12},{16,18},{18,... | collective-permute-start | bytes 786440 | tf_op jit(solution)/shard_map/ppermute | solution.py:267
  179.3 11.7 %collective-permute-start.25 = (f32[2,128,256]{2,1,0:T(8,128)S(1)}, f32[2,128,256]{2,1,0:T(8,128)S(1)}, u32[]{:S(2)}, u32[]{:S(2)}) collective-permute-start(f32[2,128,256]{2,1,0:T(8,128)S(1)} %get-tuple-element.86), channel_id=1, source_target_pairs={{0,4},{2,6},{4,0},{6,2},{8,12},{10,14},{12,8},{14,10},{16,20},{18,... | collective-permute-start | bytes 786440 | tf_op jit(solution)/shard_map/ppermute | solution.py:267
  179.8 31.5 %collective-permute-start.35 = (f32[4,128,256]{2,1,0:T(8,128)}, f32[4,128,256]{2,1,0:T(8,128)}, u32[]{:S(2)}, u32[]{:S(2)}) collective-permute-start(f32[4,128,256]{2,1,0:T(8,128)} %add.89), channel_id=1, source_target_pairs={{8,16},{10,18},{12,20},{14,22},{16,8},{18,10},{20,12},{22,14},{9,1... | collective-permute-start | bytes 1572872 | tf_op jit(solution)/shard_map/ppermute | solution.py:258
  181.3 14.2 %collective-permute-start.26 = (f32[2,128,256]{2,1,0:T(8,128)S(1)}, f32[2,128,256]{2,1,0:T(8,128)}, u32[]{:S(2)}, u32[]{:S(2)}) collective-permute-start(f32[2,128,256]{2,1,0:T(8,128)S(1)} %get-tuple-element.87), channel_id=1, source_target_pairs={{0,6},{2,4},{4,2},{6,0},{8,14},{10,12},{12,10},{14,8},{16,22},{18,... | collective-permute-start | bytes 786440 | tf_op jit(solution)/shard_map/ppermute | solution.py:267
  182.8 10.2 %collective-permute-start.38 = (f32[1,128,256]{2,1,0:T(8,128)S(1)}, f32[1,128,256]{2,1,0:T(8,128)}, u32[]{:S(2)}, u32[]{:S(2)}) collective-permute-start(f32[1,128,256]{2,1,0:T(8,128)S(1)} %add.92), channel_id=1, source_target_pairs={{8,16},{10,18},{12,20},{14,22},{16,8},{18,10},{20,12},{22,14},{9,1... | collective-permute-start | bytes 393224 | tf_op jit(solution)/shard_map/ppermute | solution.py:258
  185.7 8.6 %copy-start.2 = (s32[1024,1]{0,1:T(1,128)S(1)}, s32[1024,1]{0,1:T(1,128)}, u32[]{:S(2)}) copy-start(s32[1024,1]{0,1:T(1,128)} %param.7) | copy-start | bytes 12292
  187.2 24.1 %collective-permute-start.43 = (f32[2,128,256]{2,1,0:T(8,128)}, f32[2,128,256]{2,1,0:T(8,128)}, u32[]{:S(2)}, u32[]{:S(2)}) collective-permute-start(f32[2,128,256]{2,1,0:T(8,128)} %add.96), channel_id=1, source_target_pairs={{8,0},{10,2},{12,4},{14,6},{16,24},{18,26},{20,28},{22,30},{9,1},{... | collective-permute-start | bytes 786440 | tf_op jit(solution)/shard_map/ppermute | solution.py:258
  191.7 19.6 %collective-permute-start.47 = (f32[2,128,256]{2,1,0:T(8,128)}, f32[2,128,256]{2,1,0:T(8,128)}, u32[]{:S(2)}, u32[]{:S(2)}) collective-permute-start(f32[2,128,256]{2,1,0:T(8,128)} %add.99), channel_id=1, source_target_pairs={{8,0},{10,2},{12,4},{14,6},{16,24},{18,26},{20,28},{22,30},{9,1},{... | collective-permute-start | bytes 786440 | tf_op jit(solution)/shard_map/ppermute | solution.py:258
  193.0 18.3 %collective-permute-start.51 = (f32[2,128,256]{2,1,0:T(8,128)}, f32[2,128,256]{2,1,0:T(8,128)}, u32[]{:S(2)}, u32[]{:S(2)}) collective-permute-start(f32[2,128,256]{2,1,0:T(8,128)} %add.102), channel_id=1, source_target_pairs={{8,0},{10,2},{12,4},{14,6},{16,24},{18,26},{20,28},{22,30},{9,1},{... | collective-permute-start | bytes 786440 | tf_op jit(solution)/shard_map/ppermute | solution.py:258
  195.5 15.8 %collective-permute-start.39 = (f32[1,128,256]{2,1,0:T(8,128)S(1)}, f32[1,128,256]{2,1,0:T(8,128)S(1)}, u32[]{:S(2)}, u32[]{:S(2)}) collective-permute-start(f32[1,128,256]{2,1,0:T(8,128)S(1)} %add.93), channel_id=1, source_target_pairs={{8,0},{10,2},{12,4},{14,6},{16,24},{18,26},{20,28},{22,30},{9,1},{... | collective-permute-start | bytes 393224 | tf_op jit(solution)/shard_map/ppermute | solution.py:258
  199.7 11.6 %copy-start.15 = (f32[7,1,128,256]{3,2,1,0:T(8,128)S(1)}, f32[7,1,128,256]{3,2,1,0:T(8,128)}, u32[]{:S(2)}) copy-start(f32[7,1,128,256]{3,2,1,0:T(8,128)} %param.11) | copy-start | bytes 2752516
  199.7 11.6 %copy-start.17 = (f32[7,128,256]{2,1,0:T(8,128)S(1)}, f32[7,128,256]{2,1,0:T(8,128)}, u32[]{:S(2)}) copy-start(f32[7,128,256]{2,1,0:T(8,128)} %copy-done.16) | copy-start | bytes 2752516
  199.7 11.7 %copy-start.19 = (f32[7,128,256]{2,1,0:T(8,128)S(1)}, f32[7,128,256]{2,1,0:T(8,128)}, u32[]{:S(2)}) copy-start(f32[7,128,256]{2,1,0:T(8,128)} %copy-done.18) | copy-start | bytes 2752516
  199.7 11.7 %copy-start.22 = (f32[3,128,256]{2,1,0:T(8,128)S(1)}, f32[3,128,256]{2,1,0:T(8,128)}, u32[]{:S(2)}) copy-start(f32[3,128,256]{2,1,0:T(8,128)} %copy-done.21) | copy-start | bytes 1179652
  211.4 2.7 %copy-start.20 = (f32[7,1,128,256]{3,2,1,0:T(8,128)S(1)}, f32[7,1,128,256]{3,2,1,0:T(8,128)}, u32[]{:S(2)}) copy-start(f32[7,1,128,256]{3,2,1,0:T(8,128)} %param.10) | copy-start | bytes 2752516
  (11 other events, 12.4 us)
where the time goes:
time: 217 us; the launch traced here: 216 us
  waiting for transfers between devices  80.2 us (37%)
  starting transfers between devices  74 us (34%)
  Pallas kernels  40.1 us (18%)
  other arithmetic  12 us (6%)
  local copies, waits for them, and re-layouts  8.29 us (4%)
    ppermute x22, waiting for transfers between devices, along(): return lax.ppermute(value, 'expert', plane_pairs(pairs))  52.3 us
    ppermute x22, starting transfers between devices, along(): return lax.ppermute(value, 'expert', plane_pairs(pairs))  49.1 us
    ppermute x18, waiting for transfers between devices, exchange(): lax.ppermute(values[mask], 'expert', [(e, e ^ mask) for e in range(groups)])  27.9 us
    pallas_call x4, Pallas kernels, step_call(): pl.pallas_call(functools.partial(step_body, size, cap, layers, chunks, al...  27.7 us
    ppermute x18, starting transfers between devices, exchange(): lax.ppermute(values[mask], 'expert', [(e, e ^ mask) for e in range(groups)])  23.1 us
    unnamed x47, local copies, waits for them, and re-layouts  8.21 us
    pallas_call x1, Pallas kernels, unpack(): pl.pallas_call(functools.partial(unpack_body, size, cap, groups), out_sha...  7.02 us
    pallas_call x2, Pallas kernels, pack(): pl.pallas_call(functools.partial(pack_body, size, cap, groups, steps), ou...  5.38 us
  transfers between devices with their start and end apart: 52, of which 15 were waited for; matrix products, arithmetic and copies ran while one was open for 4% of the time, Pallas kernels for 19%

commit v1 on v0

--- a/solution.py
+++ b/solution.py
@@ -49,7 +49,25 @@
     return jnp.right_shift(at, size.bit_length() - 1), jnp.bitwise_and(at, size - 1)
 
 
-def pack_body(size, cap, groups, steps, route_ref, rows_ref, cots_ref, *outs):
+def slot_column(size, cap, groups, route):
+    count = route.shape[0]
+    plane, column = position(size)
+    hot = (lax.broadcasted_iota(jnp.int32, (count, groups), 1) == route).astype(F32)
+    ahead = (
+        lax.broadcasted_iota(jnp.int32, (count, count), 1)
+        < lax.broadcasted_iota(jnp.int32, (count, count), 0)
+    ).astype(F32).astype(BF16)
+    before = dot(ahead, hot.astype(BF16), NN)
+    rank = jnp.sum(before * hot, axis=1, keepdims=True).astype(jnp.int32)
+    return slots_of(route, rank, plane, column, size, cap)
+
+
+def pack_body(size, cap, groups, steps, with_column, *refs):
+    route_ref, rows_ref, cots_ref = refs[:3]
+    outs = refs[3:]
+    if with_column:
+        outs[-1][...] = slot_column(size, cap, groups, outs[0][...])
+        outs = outs[1:-1]
     count, _ = rows_ref.shape
     plane, column = position(size)
     route = route_ref[...]
@@ -73,37 +91,41 @@
                 outs[part * size + mask][kind] = rows[mask * cap : (mask + 1) * cap]
 
 
-def pack(route_row, rows, cots, size, cap, groups, steps):
+def pack(route_row, rows, cots, size, cap, groups, steps, route_col=None):
     count, width = rows.shape
+    with_column = route_col is not None
+    column = [pltpu.HBM((count, 1), jnp.int32)] if with_column else []
+    rows, cots = (pltpu.with_memory_space_constraint(v, pltpu.HBM) for v in (rows, cots))
+    row_spec = pl.BlockSpec((count, width), lambda i: (0, 0))
+    out_spec = pl.BlockSpec((2, cap, width), lambda i: (0, 0, 0))
+    in_specs = [pl.BlockSpec((1, count), lambda i: (0, 0)), row_spec, row_spec]
+    col_spec = pl.BlockSpec((count, 1), lambda i: (0, 0))
     made = pl.pallas_call(
-        functools.partial(pack_body, size, cap, groups, steps),
-        out_shape=[jax.ShapeDtypeStruct((2, cap, width), F32)] * (len(steps) * size),
+        functools.partial(pack_body, size, cap, groups, steps, with_column),
+        grid=(1,),
+        in_specs=in_specs + [col_spec] * with_column,
+        out_specs=[out_spec] * (len(steps) * size) + [col_spec] * with_column,
+        out_shape=[
+            (pltpu.HBM if m == 0 else jax.ShapeDtypeStruct)((2, cap, width), F32)
+            for m in list(range(size)) * len(steps)
+        ]
+        + column,
         compiler_params=pltpu.CompilerParams(vmem_limit_bytes=48 * 2**20),
         cost_estimate=pl.CostEstimate(
             flops=8 * count * count * width, bytes_accessed=12 * count * width, transcendentals=0
         ),
         name="pack",
-    )(route_row, rows, cots)
-    return [made[i * size : (i + 1) * size] for i in range(len(steps))]
-
-
-def unpack_body(size, cap, groups, route_ref, *refs):
+    )(route_row, rows, cots, *([route_col] if with_column else []))
+    return [made[i * size : (i + 1) * size] for i in range(len(steps))], made[-1]
+
+
+def unpack_body(size, cap, steps, added, slot_ref, *refs):
     out_ref = refs[-1]
     count = out_ref.shape[0]
-    plane, column = position(size)
-    route = route_ref[...]
-    hot = (lax.broadcasted_iota(jnp.int32, (count, groups), 1) == route).astype(F32)
-    ahead = (
-        lax.broadcasted_iota(jnp.int32, (count, count), 1)
-        < lax.broadcasted_iota(jnp.int32, (count, count), 0)
-    ).astype(F32).astype(BF16)
-    before = dot(ahead, hot.astype(BF16), NN)
-    rank = jnp.sum(before * hot, axis=1, keepdims=True).astype(jnp.int32)
-    slot = slots_of(route, rank, plane, column, size, cap)
-    total = None
-    for index, step in enumerate(sum(PAIRS, ())):
-        pair, which = divmod(index, 2)
-        rows = jnp.concatenate([refs[pair * size + m][which] for m in range(size)], axis=0)
+    slot = slot_ref[...]
+    total = refs[size][...] if added else None
+    for which, step in enumerate(steps):
+        rows = jnp.concatenate([refs[m][which] for m in range(size)], axis=0)
         high, low = split(rows)
         at = lax.broadcasted_iota(jnp.int32, (count, size * cap), 1) + step * size * cap
         pick = (at == slot).astype(F32).astype(BF16)
@@ -112,18 +134,58 @@
     out_ref[...] = total
 
 
-def unpack(route_col, pieces, size, cap, groups):
-    count = route_col.shape[0]
+def unpack(slot_col, pieces, before, steps, cap):
+    size = len(pieces)
+    count = slot_col.shape[0]
     width = pieces[0].shape[-1]
+    added = before is not None
     return pl.pallas_call(
-        functools.partial(unpack_body, size, cap, groups),
+        functools.partial(unpack_body, size, cap, steps, added),
         out_shape=jax.ShapeDtypeStruct((count, width), F32),
         compiler_params=pltpu.CompilerParams(vmem_limit_bytes=48 * 2**20),
         cost_estimate=pl.CostEstimate(
-            flops=8 * count * count * width, bytes_accessed=12 * count * width, transcendentals=0
+            flops=4 * count * count * width, bytes_accessed=12 * count * width, transcendentals=0
         ),
         name="unpack",
-    )(route_col, *pieces)
+    )(slot_col, *pieces, *([before] if added else []))
+
+
+def adam_body(w_ref, one_ref, two_ref, base_ref, mid_ref, far_ref, *refs):
+    new_w, new_one, new_two = refs[-3:]
+    grad = base_ref[0] + (mid_ref[0] + far_ref[0])
+    one = 0.9 * one_ref[0, 0] + 0.1 * grad
+    two = 0.999 * two_ref[0, 0] + 0.001 * grad * grad
+    new_one[0, 0] = one
+    new_two[0, 0] = two
+    new_w[0, 0] = w_ref[0, 0] - 0.01 * (one / CORR_ONE) / (jnp.sqrt(two / CORR_TWO) + 1e-08)
+
+
+def adam(weights, moment_one, moment_two, base, mid, far, chunk, mid_low, buffers):
+    _, _, shard, width = weights.shape
+    low = min(chunk)
+    whole = pl.BlockSpec((1, 1, shard, width), lambda i: (low + i, 0, 0, 0))
+    aliased = buffers is not None
+    return pl.pallas_call(
+        adam_body,
+        grid=(len(chunk),),
+        in_specs=[whole] * 3
+        + [
+            pl.BlockSpec((1, shard, width), lambda i: (low + i, 0, 0)),
+            pl.BlockSpec((1, shard, width), lambda i: (low - mid_low + i, 0, 0)),
+            pl.BlockSpec((1, shard, width), lambda i: (i, 0, 0)),
+        ]
+        + [pl.BlockSpec(memory_space=pl.ANY)] * (3 if aliased else 0),
+        out_specs=[whole] * 3,
+        out_shape=[jax.ShapeDtypeStruct(weights.shape, F32)] * 3,
+        input_output_aliases={6 + i: i for i in range(3)} if aliased else {},
+        compiler_params=pltpu.CompilerParams(vmem_limit_bytes=48 * 2**20),
+        cost_estimate=pl.CostEstimate(
+            flops=20 * len(chunk) * shard * width,
+            bytes_accessed=36 * len(chunk) * shard * width,
+            transcendentals=len(chunk) * shard * width,
+        ),
+        name="adam",
+    )(weights, moment_one, moment_two, base, mid, far, *(buffers or ()))
 
 
 def step_body(size, cap, layers, chunks, aliased, *refs):
@@ -192,7 +254,7 @@
     items = size * cap
     row_spec = pl.BlockSpec((2, cap, width), lambda i: (0, 0, 0))
     weight_spec = pl.BlockSpec((layers, shard, width), lambda i: (0, 0, 0))
-    outs = [jax.ShapeDtypeStruct((2, cap, width), F32)] * size
+    outs = [pltpu.HBM((2, cap, width), F32)] * size
     out_specs = [pl.BlockSpec((1, cap, width), lambda i: (which, 0, 0))] * size
     grads = [jax.ShapeDtypeStruct((len(c), shard, width), F32) for c in chunks] * 2
     grad_specs = [pl.BlockSpec((len(c), shard, width), lambda i: (0, 0, 0)) for c in chunks] * 2
@@ -229,18 +291,11 @@
 PAIRS = ((1, 2), (0, 3))
 
 
-def chunks_of(layers, parts):
+def chunks_of(layers, step):
     order = list(range(layers - 1, -1, -1))
-    parts = min(parts, layers)
-    sizes = [layers // parts + (1 if i < layers % parts else 0) for i in range(parts)]
-    cut, at = [], 0
-    for n in sizes:
-        cut.append(order[at : at + n])
-        at += n
-    return cut
-
-
-PARTS = {0: 1, 1: 1, 2: 2, 3: 4}
+    first, second = layers - layers // 3 * 2, layers // 3
+    cut = [order[:first], order[first : first + second], order[first + second :]]
+    return cut if step > 1 else [order]
 
 
 def on_device(samples, routes, cotangent, weights, moment_one, moment_two):
@@ -272,59 +327,70 @@
     MIDDLE = [(1, 2), (2, 1)]
     OUTWARD = [(1, 0), (2, 3)]
     INWARD = [(0, 1), (3, 2)]
+    FAR = [(1, 3), (2, 0)]
+    plane, _ = position(size)
+    inner = jnp.logical_and(plane > 0, plane < PLANES - 1)
 
     own = weights[:, 0]
     side = along(own, SIDES)
     middle = along(own, MIDDLE)
     own_other = swap_core(own)
     arrived = {}
-    for steps in PAIRS:
-        packed = pack(route_row, samples, cotangent, size, cap, groups, steps)
+    for i, steps in enumerate(PAIRS):
+        packed, slot_col = pack(
+            route_row, samples, cotangent, size, cap, groups, steps, routes if i else None
+        )
         for step, values in zip(steps, packed):
             arrived[step] = exchange(values)
     side_in = along(side, MIDDLE)
     middle_out = along(middle, OUTWARD)
-    side_out = along(side_in, OUTWARD)
     second = middle + middle_out
-    third = side_in + side_out
-    mats = [
-        (own, own_other),
-        (side, swap_core(side)),
-        (second, swap_core(second)),
-        (third, swap_core(third)),
-    ]
+
+    mats = {
+        0: lambda: (own, own_other),
+        1: lambda: (side, swap_core(side)),
+        2: lambda: (second, swap_core(second)),
+        3: lambda: (third, swap_core(third)),
+    }
     outputs = {}
     sums = {}
     for i, steps in enumerate(PAIRS):
         buffers = None
         for which, step in enumerate(steps):
+            if step == 3:
+                late, _ = lax.optimization_barrier((p3, buffers[0]))
+                third = jnp.where(inner, side_in, late)
+            pair = mats[step]()
             buffers, keeps, sends = step_call(
-                arrived[step], *mats[step], buffers, which, chunks_of(layers, PARTS[step])
+                arrived[step], *pair, buffers, which, chunks_of(layers, step)
             )
             sums[step] = [keep + swap_core(send) for keep, send in zip(keeps, sends)]
+            if step == 1:
+                one = sums[1][0]
+                p3 = along(jnp.where(inner, side_in, one), SIDES)
         outputs[i] = exchange(buffers)
 
-    zero, one = sums[0][0], sums[1][0]
-    first_in = along(one, INWARD)
-    second_mid = [along(value + along(value, INWARD), MIDDLE) for value in sums[2]]
-    third_out = []
-    cut = chunks_of(layers, PARTS[3])
-    held = lax.optimization_barrier([one[min(c) : max(c) + 1] for c in cut])
-    for j, value in enumerate(sums[3]):
-        inward = value + along(value, INWARD)
-        passed = held[j] + along(inward, MIDDLE)
-        third_out.append(along(passed, OUTWARD))
-    grad = (
-        zero
-        + first_in
-        + jnp.concatenate(second_mid[::-1], axis=0)
-        + jnp.concatenate(third_out[::-1], axis=0)
-    )[:, None]
-    new_one = 0.9 * moment_one + 0.1 * grad
-    new_two = 0.999 * moment_two + 0.001 * grad * grad
-    new_w = weights - 0.01 * (new_one / CORR_ONE) / (jnp.sqrt(new_two / CORR_TWO) + 1e-08)
-    result = unpack(routes, outputs[0] + outputs[1], size, cap, groups)
-    return (result, new_w, new_one, new_two)
+    zero = sums[0][0]
+    cut_two, cut_three = chunks_of(layers, 2), chunks_of(layers, 3)
+    p4, mid = [], []
+    for value, c in zip(sums[2], cut_two):
+        back = along(jnp.where(inner, one[min(c) : max(c) + 1], value), SIDES)
+        p4.append(back)
+        mid.append(along(value + back, MIDDLE))
+    kept, sides, *late = lax.optimization_barrier((zero, p3, *p4))
+    base = kept + jnp.where(inner, sides, jnp.concatenate(late[::-1], axis=0))
+    updated = None
+    for value, c in zip(sums[3], cut_three):
+        passed = value + along(value, INWARD)
+        far = along(passed, FAR)
+        k = next(k for k, d in enumerate(cut_two) if min(c) in d)
+        updated = adam(
+            weights, moment_one, moment_two, base, mid[k], far, c, min(cut_two[k]), updated
+        )
+    result = None
+    for i, steps in enumerate(PAIRS):
+        result = unpack(slot_col, outputs[i], result, steps, cap)
+    return (result, *updated)
 
 
 def solution(mesh):

time: 217 us -> 226 us (1.041)
  waiting for transfers between devices: 80.2 us -> 99.2 us
  other arithmetic: 12 us -> 3.94 us
  Pallas kernels: 40.1 us -> 47.9 us
  starting transfers between devices: 74 us -> 68.7 us
  local copies, waits for them, and re-layouts: 8.29 us -> 4.64 us
    ppermute x22 -> x17, waiting for transfers between devices: 52.3 us -> 65.1 us  [along(): return lax.ppermute(value, 'expert', plane_pairs(pairs))]
    ppermute x22 -> x17, starting transfers between devices: 49.1 us -> 42.9 us  [along(): return lax.ppermute(value, 'expert', plane_pairs(pairs))]
    pallas_call x3 -> x7, Pallas kernels: 12.4 us -> 17.9 us  [the longest x2 10.7 us: pack(): pl.pallas_call(functools.partial(pack_body, size, cap, groups, steps, wit...]
    add x11 -> x7, other arithmetic: 5.81 us -> 0.43 us  [the longest x1 0.18 us: on_device(): base = kept + jnp.where(inner, sides, jnp.concatenate(late[::-1], axis=0))]
    ppermute x18, waiting for transfers between devices: 27.9 us -> 32.5 us  [exchange(): lax.ppermute(values[mask], 'expert', [(e, e ^ mask) for e in range(groups)])]
    unnamed x2 -> x0, other arithmetic: 4.48 us -> none
    unnamed x47 -> x45, local copies, waits for them, and re-layouts: 8.21 us -> 4.64 us
    pallas_call x4, Pallas kernels: 27.7 us -> 30.1 us  [step_call(): pl.pallas_call(functools.partial(step_body, size, cap, layers, chunks, al...]
  transfers between devices with their start and end apart: 52 -> 47, of which waited for: 15 -> 17; matrix products, arithmetic and copies ran while one was open for 4% -> 2% of each run, Pallas kernels for 19% -> 21%
where the time goes in v1:
time: 226 us
  waiting for transfers between devices  99.2 us (44%)
  starting transfers between devices  68.7 us (30%)
  Pallas kernels  47.9 us (21%)
  local copies, waits for them, and re-layouts  4.64 us (2%)
  other arithmetic  3.94 us (2%)
    ppermute x17, waiting for transfers between devices, along(): return lax.ppermute(value, 'expert', plane_pairs(pairs))  65.1 us
    ppermute x17, starting transfers between devices, along(): return lax.ppermute(value, 'expert', plane_pairs(pairs))  42.9 us
    ppermute x18, waiting for transfers between devices, exchange(): lax.ppermute(values[mask], 'expert', [(e, e ^ mask) for e in range(groups)])  32.5 us
    pallas_call x4, Pallas kernels, step_call(): pl.pallas_call(functools.partial(step_body, size, cap, layers, chunks, al...  30.1 us
    ppermute x18, starting transfers between devices, exchange(): lax.ppermute(values[mask], 'expert', [(e, e ^ mask) for e in range(groups)])  23.5 us
    pallas_call x2, Pallas kernels, pack(): pl.pallas_call(functools.partial(pack_body, size, cap, groups, steps, wit...  10.7 us
    unnamed x45, local copies, waits for them, and re-layouts  4.64 us
  transfers between devices with their start and end apart: 47, of which 17 were waited for; matrix products, arithmetic and copies ran while one was open for 2% of the time, Pallas kernels for 21%

profile of v1, /device:TPU:0, one launch (start us, length us, event | category | flops | bytes accessed | tf_op | source)
XLA Modules:
  0.0 225.5 jit_solution(933136157810747050)
XLA Ops:
  0.6 3.1 %collective-permute-start.3 = (f32[7,128,256]{2,1,0:T(8,128)}, f32[7,128,256]{2,1,0:T(8,128)}, u32[]{:S(2)}, u32[]{:S(2)}) collective-permute-start(f32[7,128,256]{2,1,0:T(8,128)} %bitcast.2), channel_id=1, source_target_pairs={{0,8},{2,10},{4,12},{6,14},{8,0},{10,2},{12,4},{14,6},{16,24},{18,... | collective-permute-start | bytes 2752520 | tf_op jit(solution)/shard_map/ppermute | solution.py:313
  3.7 20.7 %collective-permute-done.3.refs_4_ = f32[7,128,256]{2,1,0:T(8,128)} collective-permute-done((f32[7,128,256]{2,1,0:T(8,128)}, f32[7,128,256]{2,1,0:T(8,128)}, u32[]{:S(2)}, u32[]{:S(2)}) %collective-permute-start.3) | collective-permute-done | bytes 917536 | tf_op jit(solution)/shard_map/ppermute | solution.py:313
  24.4 0.7 copy-done.3
  25.1 5.0 %pack.3 = (f32[2,128,256]{2,1,0:T(8,128)}, f32[2,128,256]{2,1,0:T(8,128)S(1)}, f32[2,128,256]{2,1,0:T(8,128)S(1)}, f32[2,128,256]{2,1,0:T(8,128)S(1)}, f32[2,128...) custom-call(s32[1,1024]{1,0:T(1,128)S(1)} %bitcast.6, ...), custom_call_target="tpu_custom_call" | custom-call | flops 2147483648 | bytes 3145728 | tf_op jit(solution)/shard_map/pack/pallas_call | solution.py:103
  30.1 0.7 copy-done.5
  30.8 0.7 copy-done.7
  31.6 1.7 collective-permute-start.5
  33.2 1.5 collective-permute-start.6
  35.1 1.6 collective-permute-start.22
  36.6 4.1 %collective-permute-done.5.refs_1_ = f32[2,128,256]{2,1,0:T(8,128)S(1)} collective-permute-done((f32[2,128,256]{2,1,0:T(8,128)S(1)}, f32[2,128,256]{2,1,0:T(8,128)S(1)}, u32[]{:S(2)}, u32[]{:S(2)}) %collective-permute-start.5) | collective-permute-done | bytes 262176 | tf_op jit(solution)/shard_map/ppermute | solution.py:322
  40.7 1.6 collective-permute-start.4
  42.4 4.9 %collective-permute-done.6.refs_2_ = f32[2,128,256]{2,1,0:T(8,128)S(1)} collective-permute-done((f32[2,128,256]{2,1,0:T(8,128)S(1)}, f32[2,128,256]{2,1,0:T(8,128)S(1)}, u32[]{:S(2)}, u32[]{:S(2)}) %collective-permute-start.6) | collective-permute-done | bytes 262176 | tf_op jit(solution)/shard_map/ppermute | solution.py:322
  47.3 0.9 copy-done.15
  48.2 9.0 %step.4 = (f32[2,128,256]{2,1,0:T(8,128)}, f32[2,128,256]{2,1,0:T(8,128)}, f32[2,128,256]{2,1,0:T(8,128)}, f32[2,128,256]{2,1,0:T(8,128)}, f32[7,128,256]{2,1,0:T(8,128)S(1)}, /*index=5*/f32[7,128,256]{2,1,0:T(8,128)}) custom-call(f32[2,128,256]{2,1,0:T(8,128)S(1)} %copy-done.15, f32[2,128,256]{2,1,0:T(8,128)S(1)} %collective-permute-done.5.refs_1_, ...), custom_call_target="tpu_custom_call" | custom-call | flops 4227858432 | bytes 5242880 | tf_op jit(solution)/shard_map/step/pallas_call | solution.py:262
  57.2 1.3 collective-permute-start.23
  59.4 0.7 collective-permute-done.9
  60.1 1.4 broadcast_select_fusion.1
  61.4 20.7 %collective-permute-start.10 = (f32[7,128,256]{2,1,0:T(8,128)S(1)}, f32[7,128,256]{2,1,0:T(8,128)S(1)}, u32[]{:S(2)}, u32[]{:S(2)}) collective-permute-start(f32[7,128,256]{2,1,0:T(8,128)S(1)} %get-tuple-element.138), channel_id=1, source_target_pairs={{0,8},{2,10},{4,12},{6,14},{8,0},{10,2},{12,4},{14,6},{16,24},{18,... | collective-permute-start | bytes 2752520 | tf_op jit(solution)/shard_map/ppermute | solution.py:313
  82.1 5.7 %pack.2 = (f32[2,128,256]{2,1,0:T(8,128)}, f32[2,128,256]{2,1,0:T(8,128)S(1)}, f32[2,128,256]{2,1,0:T(8,128)S(1)}, f32[2,128,256]{2,1,0:T(8,128)S(1)}, f32[2,128...) custom-call(s32[1,1024]{1,0:T(1,128)S(1)} %bitcast.7, ...), custom_call_target="tpu_custom_call" | custom-call | flops 2147483648 | bytes 3145728 | tf_op jit(solution)/shard_map/pack/pallas_call | solution.py:103
  87.8 1.5 collective-permute-start.11
  89.2 1.5 collective-permute-start.12
  91.3 1.6 add.49.refs_4_
  92.9 4.0 %collective-permute-done.11.refs_1_ = f32[2,128,256]{2,1,0:T(8,128)S(1)} collective-permute-done((f32[2,128,256]{2,1,0:T(8,128)S(1)}, f32[2,128,256]{2,1,0:T(8,128)S(1)}, u32[]{:S(2)}, u32[]{:S(2)}) %collective-permute-start.11) | collective-permute-done | bytes 262176 | tf_op jit(solution)/shard_map/ppermute | solution.py:322
  96.9 4.4 %collective-permute-done.12.refs_2_ = f32[2,128,256]{2,1,0:T(8,128)S(1)} collective-permute-done((f32[2,128,256]{2,1,0:T(8,128)S(1)}, f32[2,128,256]{2,1,0:T(8,128)S(1)}, u32[]{:S(2)}, u32[]{:S(2)}) %collective-permute-start.12) | collective-permute-done | bytes 262176 | tf_op jit(solution)/shard_map/ppermute | solution.py:322
  101.4 2.1 collective-permute-start.20
  103.4 1.4 collective-permute-start.21
  104.8 7.1 %step.5 = (f32[2,128,256]{2,1,0:T(8,128)}, f32[2,128,256]{2,1,0:T(8,128)}, f32[2,128,256]{2,1,0:T(8,128)}, f32[2,128,256]{2,1,0:T(8,128)}, f32[7,128,256]{2,1,0:T(8,128)S(1)}, /*index=5*/f32[7,128,256]{2,1,0:T(8,128)S(1)}) custom-call(f32[2,128,256]{2,1,0:T(8,128)S(1)} %copy-done.13, f32[2,128,256]{2,1,0:T(8,128)S(1)} %collective-permute-done.11.refs_1_, ...), custom_call_target="tpu_custom_call" | custom-call | flops 4227858432 | bytes 5242880 | tf_op jit(solution)/shard_map/step/pallas_call | solution.py:262
  112.9 6.9 %step.7 = (f32[2,128,256]{2,1,0:T(8,128)}, f32[2,128,256]{2,1,0:T(8,128)}, f32[2,128,256]{2,1,0:T(8,128)}, f32[2,128,256]{2,1,0:T(8,128)}, f32[3,128,256]{2,1,0:...) custom-call(f32[2,128,256]{2,1,0:T(8,128)S(1)} %copy-done.14, ...), custom_call_target="tpu_custom_call", output_to_operand_aliasing={{0}: (6, {}), {1}: (7, {}), {2}: (8, {}), {3}: (9, {})} | custom-call | flops 4227858432 | bytes 5242880 | tf_op jit(solution)/shard_map/step/pallas_call | solution.py:262
  120.4 1.2 collective-permute-start
  121.6 1.3 collective-permute-start.1
  122.9 0.9 collective-permute-start.2
  124.0 5.6 %collective-permute-done.refs_1_ = f32[2,128,256]{2,1,0:T(8,128)S(1)} collective-permute-done((f32[2,128,256]{2,1,0:T(8,128)S(1)}, f32[2,128,256]{2,1,0:T(8,128)S(1)}, u32[]{:S(2)}, u32[]{:S(2)}) %collective-permute-start) | collective-permute-done | bytes 262176 | tf_op jit(solution)/shard_map/ppermute | solution.py:322
  129.5 1.2 collective-permute-start.25
  130.8 3.9 %collective-permute-done.1.refs_2_ = f32[2,128,256]{2,1,0:T(8,128)S(1)} collective-permute-done((f32[2,128,256]{2,1,0:T(8,128)S(1)}, f32[2,128,256]{2,1,0:T(8,128)S(1)}, u32[]{:S(2)}, u32[]{:S(2)}) %collective-permute-start.1) | collective-permute-done | bytes 262176 | tf_op jit(solution)/shard_map/ppermute | solution.py:322
  134.6 2.6 %collective-permute-start.26 = (f32[2,128,256]{2,1,0:T(8,128)S(1)}, f32[2,128,256]{2,1,0:T(8,128)S(1)}, u32[]{:S(2)}, u32[]{:S(2)}) collective-permute-start(f32[2,128,256]{2,1,0:T(8,128)S(1)} %copy-done.17), channel_id=1, source_target_pairs={{0,4},{2,6},{4,0},{6,2},{8,12},{10,14},{12,8},{14,10},{16,20},{18,... | collective-permute-start | bytes 786440 | tf_op jit(solution)/shard_map/ppermute | solution.py:322
  137.8 7.1 %step.6 = (f32[2,128,256]{2,1,0:T(8,128)}, f32[2,128,256]{2,1,0:T(8,128)}, f32[2,128,256]{2,1,0:T(8,128)}, f32[2,128,256]{2,1,0:T(8,128)}, f32[3,128,256]{2,1,0:...) custom-call(f32[2,128,256]{2,1,0:T(8,128)S(1)} %copy-done.12, ...), custom_call_target="tpu_custom_call", output_to_operand_aliasing={{0}: (6, {}), {1}: (7, {}), {2}: (8, {}), {3}: (9, {})} | custom-call | flops 4227858432 | bytes 5242880 | tf_op jit(solution)/shard_map/step/pallas_call | solution.py:262
  145.3 1.0 collective-permute-start.30
  147.1 0.8 collective-permute-done.36
  147.9 1.0 collective-permute-start.34
  149.0 5.2 %collective-permute-done.27.refs_3_ = f32[2,128,256]{2,1,0:T(8,128)S(1)} collective-permute-done((f32[2,128,256]{2,1,0:T(8,128)S(1)}, f32[2,128,256]{2,1,0:T(8,128)S(1)}, u32[]{:S(2)}, u32[]{:S(2)}) %collective-permute-start.27) | collective-permute-done | bytes 262176 | tf_op jit(solution)/shard_map/ppermute | solution.py:322
  154.7 3.4 %collective-permute-start.37 = (f32[2,128,256]{2,1,0:T(8,128)S(1)}, f32[2,128,256]{2,1,0:T(8,128)S(1)}, u32[]{:S(2)}, u32[]{:S(2)}) collective-permute-start(f32[2,128,256]{2,1,0:T(8,128)S(1)} %add.56), channel_id=1, source_target_pairs={{0,8},{2,10},{4,12},{6,14},{24,16},{26,18},{28,20},{30,22},{1,9},{... | collective-permute-start | bytes 786440 | tf_op jit(solution)/shard_map/ppermute | solution.py:313
  158.2 1.3 collective-permute-start.41
  159.6 1.3 collective-permute-start.45
  161.0 2.0 collective-permute-done.34
  163.0 0.7 collective-permute-start.43
  163.6 3.8 %collective-permute-done.32 = f32[2,128,256]{2,1,0:T(8,128)S(1)} collective-permute-done((f32[2,128,256]{2,1,0:T(8,128)S(1)}, f32[2,128,256]{2,1,0:T(8,128)S(1)}, u32[]{:S(2)}, u32[]{:S(2)}) %collective-permute-start.32) | collective-permute-done | bytes 262176 | tf_op jit(solution)/shard_map/ppermute | solution.py:313
  167.4 1.2 collective-permute-start.16
  168.6 4.1 %collective-permute-done.37 = f32[2,128,256]{2,1,0:T(8,128)S(1)} collective-permute-done((f32[2,128,256]{2,1,0:T(8,128)S(1)}, f32[2,128,256]{2,1,0:T(8,128)S(1)}, u32[]{:S(2)}, u32[]{:S(2)}) %collective-permute-start.37) | collective-permute-done | bytes 262176 | tf_op jit(solution)/shard_map/ppermute | solution.py:313
  172.7 2.0 collective-permute-start.17
  174.7 3.7 %collective-permute-done.41 = f32[2,128,256]{2,1,0:T(8,128)S(1)} collective-permute-done((f32[2,128,256]{2,1,0:T(8,128)S(1)}, f32[2,128,256]{2,1,0:T(8,128)S(1)}, u32[]{:S(2)}, u32[]{:S(2)}) %collective-permute-start.41) | collective-permute-done | bytes 262176 | tf_op jit(solution)/shard_map/ppermute | solution.py:313
  178.4 2.1 collective-permute-start.18
  180.6 0.9 copy-done.9
  181.5 1.3 unpack.2.refs_4_
  183.0 2.6 %collective-permute-done.45 = f32[3,128,256]{2,1,0:T(8,128)S(1)} collective-permute-done((f32[3,128,256]{2,1,0:T(8,128)S(1)}, f32[3,128,256]{2,1,0:T(8,128)S(1)}, u32[]{:S(2)}, u32[]{:S(2)}) %collective-permute-start.45) | collective-permute-done | bytes 393248 | tf_op jit(solution)/shard_map/ppermute | solution.py:313
  185.6 0.7 collective-permute-start.35
  186.4 0.8 collective-permute-start.39
  187.2 1.3 collective-permute-start.38
  188.5 1.3 collective-permute-start.42
  189.8 1.3 collective-permute-start.46
  191.4 2.3 %unpack.3 = f32[1024,256]{1,0:T(8,128)} custom-call(s32[1024,1]{1,0:T(8,128)S(1)} %copy-done.9, f32[2,128,256]{2,1,0:T(8,128)S(1)} %copy-done.10, f32[2,128,256]{2,1,0:T(8,128)S(1)} %collective-permute-done.16.refs_1_, f32[2,128,256]{2,1,0:T(8,128)S(1)} %collective-permute-done.17.refs_2_, f32[2,128,256]{2,1,0:T(8,128)S(1)} %collective-permute-done.18.refs_3_, ...), custom_call_target="tpu_custom_call" | custom-call | flops 1073741824 | bytes 3145728 | tf_op jit(solution)/shard_map/unpack/pallas_call | solution.py:142
  193.6 28.3 %collective-permute-done.46.far_ref = f32[3,128,256]{2,1,0:T(8,128)S(1)} collective-permute-done((f32[3,128,256]{2,1,0:T(8,128)S(1)}, f32[3,128,256]{2,1,0:T(8,128)S(1)}, u32[]{:S(2)}, u32[]{:S(2)}) %collective-permute-start.46) | collective-permute-done | bytes 393248 | tf_op jit(solution)/shard_map/ppermute | solution.py:313
  221.9 1.6 adam.3
  223.5 1.0 adam.4
  224.5 1.0 adam.5
  (102 shorter events, 6.2 us)
Async XLA Ops:
  0.6 23.8 %collective-permute-start.3 = (f32[7,128,256]{2,1,0:T(8,128)}, f32[7,128,256]{2,1,0:T(8,128)}, u32[]{:S(2)}, u32[]{:S(2)}) collective-permute-start(f32[7,128,256]{2,1,0:T(8,128)} %bitcast.2), channel_id=1, source_target_pairs={{0,8},{2,10},{4,12},{6,14},{8,0},{10,2},{12,4},{14,6},{16,24},{18,... | collective-permute-start | bytes 2752520 | tf_op jit(solution)/shard_map/ppermute | solution.py:313
  24.4 22.9 %collective-permute-start.8 = (f32[7,128,256]{2,1,0:T(8,128)}, f32[7,128,256]{2,1,0:T(8,128)S(1)}, u32[]{:S(2)}, u32[]{:S(2)}) collective-permute-start(f32[7,128,256]{2,1,0:T(8,128)} %collective-permute-done.3.refs_4_), channel_id=1, source_target_pairs={{0,1},{1,0},{2,3},{3,2},{4,5},{5,4},{6,7},{7,6},{8,9},{9,8},{10,11... | collective-permute-start | bytes 2752520 | tf_op jit(solution)/shard_map/ppermute | solution.py:316
  25.1 9.9 %copy-start = (f32[7,1,128,256]{3,2,1,0:T(8,128)S(1)}, f32[7,1,128,256]{3,2,1,0:T(8,128)}, u32[]{:S(2)}) copy-start(f32[7,1,128,256]{3,2,1,0:T(8,128)} %w_ref.5) | copy-start | bytes 2752516
  31.6 9.2 %collective-permute-start.5 = (f32[2,128,256]{2,1,0:T(8,128)S(1)}, f32[2,128,256]{2,1,0:T(8,128)S(1)}, u32[]{:S(2)}, u32[]{:S(2)}) collective-permute-start(f32[2,128,256]{2,1,0:T(8,128)S(1)} %get-tuple-element.74), channel_id=1, source_target_pairs={{0,2},{2,0},{4,6},{6,4},{8,10},{10,8},{12,14},{14,12},{16,18},{18,... | collective-permute-start | bytes 786440 | tf_op jit(solution)/shard_map/ppermute | solution.py:322
  33.2 14.1 %collective-permute-start.6 = (f32[2,128,256]{2,1,0:T(8,128)S(1)}, f32[2,128,256]{2,1,0:T(8,128)S(1)}, u32[]{:S(2)}, u32[]{:S(2)}) collective-permute-start(f32[2,128,256]{2,1,0:T(8,128)S(1)} %get-tuple-element.75), channel_id=1, source_target_pairs={{0,4},{2,6},{4,0},{6,2},{8,12},{10,14},{12,8},{14,10},{16,20},{18,... | collective-permute-start | bytes 786440 | tf_op jit(solution)/shard_map/ppermute | solution.py:322
  34.7 12.5 %collective-permute-start.7 = (f32[2,128,256]{2,1,0:T(8,128)S(1)}, f32[2,128,256]{2,1,0:T(8,128)S(1)}, u32[]{:S(2)}, u32[]{:S(2)}) collective-permute-start(f32[2,128,256]{2,1,0:T(8,128)S(1)} %get-tuple-element.76), channel_id=1, source_target_pairs={{0,6},{2,4},{4,2},{6,0},{8,14},{10,12},{12,10},{14,8},{16,22},{18,... | collective-permute-start | bytes 786440 | tf_op jit(solution)/shard_map/ppermute | solution.py:322
  35.1 22.2 %collective-permute-start.22 = (f32[7,128,256]{2,1,0:T(8,128)S(1)}, f32[7,128,256]{2,1,0:T(8,128)}, u32[]{:S(2)}, u32[]{:S(2)}) collective-permute-start(f32[7,128,256]{2,1,0:T(8,128)S(1)} %bitcast.3), channel_id=1, source_target_pairs={{8,16},{10,18},{12,20},{14,22},{16,8},{18,10},{20,12},{22,14},{9,1... | collective-permute-start | bytes 2752520 | tf_op jit(solution)/shard_map/ppermute | solution.py:313
  40.7 18.6 %collective-permute-start.4 = (f32[7,128,256]{2,1,0:T(8,128)}, f32[7,128,256]{2,1,0:T(8,128)}, u32[]{:S(2)}, u32[]{:S(2)}) collective-permute-start(f32[7,128,256]{2,1,0:T(8,128)} %collective-permute-done.3.refs_4_), channel_id=1, source_target_pairs={{8,16},{10,18},{12,20},{14,22},{16,8},{18,10},{20,12},{22,14},{9,1... | collective-permute-start | bytes 2752520 | tf_op jit(solution)/shard_map/ppermute | solution.py:313
  48.2 10.9 %copy-start.4 = (s32[1024,1]{0,1:T(1,128)S(1)}, s32[1024,1]{0,1:T(1,128)}, u32[]{:S(2)}) copy-start(s32[1024,1]{0,1:T(1,128)} %param.7) | copy-start | bytes 12292
  57.2 2.8 %collective-permute-start.9 = (f32[7,128,256]{2,1,0:T(8,128)}, f32[7,128,256]{2,1,0:T(8,128)}, u32[]{:S(2)}, u32[]{:S(2)}) collective-permute-start(f32[7,128,256]{2,1,0:T(8,128)} %get-tuple-element.78), channel_id=1, source_target_pairs={{0,1},{1,0},{2,3},{3,2},{4,5},{5,4},{6,7},{7,6},{8,9},{9,8},{10,11... | collective-permute-start | bytes 2752520 | tf_op jit(solution)/shard_map/ppermute | solution.py:316
  57.2 33.5 %collective-permute-start.23 = (f32[7,128,256]{2,1,0:T(8,128)}, f32[7,128,256]{2,1,0:T(8,128)}, u32[]{:S(2)}, u32[]{:S(2)}) collective-permute-start(f32[7,128,256]{2,1,0:T(8,128)} %collective-permute-done.22), channel_id=1, source_target_pairs={{8,0},{10,2},{12,4},{14,6},{16,24},{18,26},{20,28},{22,30},{9,1},{... | collective-permute-start | bytes 2752520 | tf_op jit(solution)/shard_map/ppermute | solution.py:313
  58.5 44.9 %collective-permute-start.14 = (f32[7,128,256]{2,1,0:T(8,128)S(1)}, f32[7,128,256]{2,1,0:T(8,128)S(1)}, u32[]{:S(2)}, u32[]{:S(2)}) collective-permute-start(f32[7,128,256]{2,1,0:T(8,128)S(1)} %bitcast.4), channel_id=1, source_target_pairs={{0,1},{1,0},{2,3},{3,2},{4,5},{5,4},{6,7},{7,6},{8,9},{9,8},{10,11... | collective-permute-start | bytes 2752520 | tf_op jit(solution)/shard_map/ppermute | solution.py:316
  61.4 50.5 %collective-permute-start.10 = (f32[7,128,256]{2,1,0:T(8,128)S(1)}, f32[7,128,256]{2,1,0:T(8,128)S(1)}, u32[]{:S(2)}, u32[]{:S(2)}) collective-permute-start(f32[7,128,256]{2,1,0:T(8,128)S(1)} %get-tuple-element.138), channel_id=1, source_target_pairs={{0,8},{2,10},{4,12},{6,14},{8,0},{10,2},{12,4},{14,6},{16,24},{18,... | collective-permute-start | bytes 2752520 | tf_op jit(solution)/shard_map/ppermute | solution.py:313
  87.8 9.2 %collective-permute-start.11 = (f32[2,128,256]{2,1,0:T(8,128)S(1)}, f32[2,128,256]{2,1,0:T(8,128)S(1)}, u32[]{:S(2)}, u32[]{:S(2)}) collective-permute-start(f32[2,128,256]{2,1,0:T(8,128)S(1)} %get-tuple-element.80), channel_id=1, source_target_pairs={{0,2},{2,0},{4,6},{6,4},{8,10},{10,8},{12,14},{14,12},{16,18},{18,... | collective-permute-start | bytes 786440 | tf_op jit(solution)/shard_map/ppermute | solution.py:322
  89.2 12.1 %collective-permute-start.12 = (f32[2,128,256]{2,1,0:T(8,128)S(1)}, f32[2,128,256]{2,1,0:T(8,128)S(1)}, u32[]{:S(2)}, u32[]{:S(2)}) collective-permute-start(f32[2,128,256]{2,1,0:T(8,128)S(1)} %get-tuple-element.81), channel_id=1, source_target_pairs={{0,4},{2,6},{4,0},{6,2},{8,12},{10,14},{12,8},{14,10},{16,20},{18,... | collective-permute-start | bytes 786440 | tf_op jit(solution)/shard_map/ppermute | solution.py:322
  90.8 10.6 %copy-start.8 = (f32[2,128,256]{2,1,0:T(8,128)S(1)}, f32[2,128,256]{2,1,0:T(8,128)}, u32[]{:S(2)}) copy-start(f32[2,128,256]{2,1,0:T(8,128)} %copy-done.7) | copy-start | bytes 786436
  90.8 10.6 %copy-start.6 = (f32[2,128,256]{2,1,0:T(8,128)S(1)}, f32[2,128,256]{2,1,0:T(8,128)}, u32[]{:S(2)}) copy-start(f32[2,128,256]{2,1,0:T(8,128)} %copy-done.5) | copy-start | bytes 786436
  90.8 14.1 %copy-start.13 = (f32[2,128,256]{2,1,0:T(8,128)S(1)}, f32[2,128,256]{2,1,0:T(8,128)}, u32[]{:S(2)}) copy-start(f32[2,128,256]{2,1,0:T(8,128)} %get-tuple-element.79.refs_0_) | copy-start | bytes 786436
  90.8 10.6 %collective-permute-start.13 = (f32[2,128,256]{2,1,0:T(8,128)S(1)}, f32[2,128,256]{2,1,0:T(8,128)S(1)}, u32[]{:S(2)}, u32[]{:S(2)}) collective-permute-start(f32[2,128,256]{2,1,0:T(8,128)S(1)} %get-tuple-element.82), channel_id=1, source_target_pairs={{0,6},{2,4},{4,2},{6,0},{8,14},{10,12},{12,10},{14,8},{16,22},{18,... | collective-permute-start | bytes 786440 | tf_op jit(solution)/shard_map/ppermute | solution.py:322
  96.9 15.6 %collective-permute-start.24 = (f32[7,128,256]{2,1,0:T(8,128)S(1)}, f32[7,128,256]{2,1,0:T(8,128)S(1)}, u32[]{:S(2)}, u32[]{:S(2)}) collective-permute-start(f32[7,128,256]{2,1,0:T(8,128)S(1)} %add.49.refs_4_), channel_id=1, source_target_pairs={{0,1},{1,0},{2,3},{3,2},{4,5},{5,4},{6,7},{7,6},{8,9},{9,8},{10,11... | collective-permute-start | bytes 2752520 | tf_op jit(solution)/shard_map/ppermute | solution.py:316
  101.3 10.8 %collective-permute-start.19 = (f32[2,128,256]{2,1,0:T(8,128)S(1)}, f32[2,128,256]{2,1,0:T(8,128)S(1)}, u32[]{:S(2)}, u32[]{:S(2)}) collective-permute-start(f32[2,128,256]{2,1,0:T(8,128)S(1)} %copy-done.8), channel_id=1, source_target_pairs={{0,2},{2,0},{4,6},{6,4},{8,10},{10,8},{12,14},{14,12},{16,18},{18,... | collective-permute-start | bytes 786440 | tf_op jit(solution)/shard_map/ppermute | solution.py:322
  101.4 11.2 %collective-permute-start.20 = (f32[2,128,256]{2,1,0:T(8,128)S(1)}, f32[2,128,256]{2,1,0:T(8,128)S(1)}, u32[]{:S(2)}, u32[]{:S(2)}) collective-permute-start(f32[2,128,256]{2,1,0:T(8,128)S(1)} %copy-done.6), channel_id=1, source_target_pairs={{0,4},{2,6},{4,0},{6,2},{8,12},{10,14},{12,8},{14,10},{16,20},{18,... | collective-permute-start | bytes 786440 | tf_op jit(solution)/shard_map/ppermute | solution.py:322
  103.4 9.1 %collective-permute-start.21 = (f32[2,128,256]{2,1,0:T(8,128)S(1)}, f32[2,128,256]{2,1,0:T(8,128)S(1)}, u32[]{:S(2)}, u32[]{:S(2)}) collective-permute-start(f32[2,128,256]{2,1,0:T(8,128)S(1)} %get-tuple-element.95), channel_id=1, source_target_pairs={{0,6},{2,4},{4,2},{6,0},{8,14},{10,12},{12,10},{14,8},{16,22},{18,... | collective-permute-start | bytes 786440 | tf_op jit(solution)/shard_map/ppermute | solution.py:322
  112.1 25.2 %collective-permute-start.15 = (f32[7,128,256]{2,1,0:T(8,128)S(1)}, f32[7,128,256]{2,1,0:T(8,128)S(1)}, u32[]{:S(2)}, u32[]{:S(2)}) collective-permute-start(f32[7,128,256]{2,1,0:T(8,128)S(1)} %broadcast_select_fusion.refs_4_), channel_id=1, source_target_pairs={{0,1},{1,0},{2,3},{3,2},{4,5},{5,4},{6,7},{7,6},{8,9},{9,8},{10,11... | collective-permute-start | bytes 2752520 | tf_op jit(solution)/shard_map/ppermute | solution.py:316
  119.8 3.1 %collective-permute-start.29 = (f32[3,128,256]{2,1,0:T(8,128)S(1)}, f32[3,128,256]{2,1,0:T(8,128)S(1)}, u32[]{:S(2)}, u32[]{:S(2)}) collective-permute-start(f32[3,128,256]{2,1,0:T(8,128)S(1)} %get-tuple-element.107), channel_id=1, source_target_pairs={{0,1},{1,0},{2,3},{3,2},{4,5},{5,4},{6,7},{7,6},{8,9},{9,8},{10,11... | collective-permute-start | bytes 1179656 | tf_op jit(solution)/shard_map/ppermute | solution.py:316
  119.9 25.0 %collective-permute-start.28 = (f32[7,128,256]{2,1,0:T(8,128)S(1)}, f32[7,128,256]{2,1,0:T(8,128)S(1)}, u32[]{:S(2)}, u32[]{:S(2)}) collective-permute-start(f32[7,128,256]{2,1,0:T(8,128)S(1)} %get-tuple-element.105), channel_id=1, source_target_pairs={{0,1},{1,0},{2,3},{3,2},{4,5},{5,4},{6,7},{7,6},{8,9},{9,8},{10,11... | collective-permute-start | bytes 2752520 | tf_op jit(solution)/shard_map/ppermute | solution.py:316
  120.4 9.2 %collective-permute-start = (f32[2,128,256]{2,1,0:T(8,128)S(1)}, f32[2,128,256]{2,1,0:T(8,128)S(1)}, u32[]{:S(2)}, u32[]{:S(2)}) collective-permute-start(f32[2,128,256]{2,1,0:T(8,128)S(1)} %get-tuple-element.70), channel_id=1, source_target_pairs={{0,2},{2,0},{4,6},{6,4},{8,10},{10,8},{12,14},{14,12},{16,18},{18,... | collective-permute-start | bytes 786440 | tf_op jit(solution)/shard_map/ppermute | solution.py:322
  121.6 13.0 %collective-permute-start.1 = (f32[2,128,256]{2,1,0:T(8,128)S(1)}, f32[2,128,256]{2,1,0:T(8,128)S(1)}, u32[]{:S(2)}, u32[]{:S(2)}) collective-permute-start(f32[2,128,256]{2,1,0:T(8,128)S(1)} %get-tuple-element.71), channel_id=1, source_target_pairs={{0,4},{2,6},{4,0},{6,2},{8,12},{10,14},{12,8},{14,10},{16,20},{18,... | collective-permute-start | bytes 786440 | tf_op jit(solution)/shard_map/ppermute | solution.py:322
  122.9 14.3 %collective-permute-start.2 = (f32[2,128,256]{2,1,0:T(8,128)S(1)}, f32[2,128,256]{2,1,0:T(8,128)S(1)}, u32[]{:S(2)}, u32[]{:S(2)}) collective-permute-start(f32[2,128,256]{2,1,0:T(8,128)S(1)} %get-tuple-element.72), channel_id=1, source_target_pairs={{0,6},{2,4},{4,2},{6,0},{8,14},{10,12},{12,10},{14,8},{16,22},{18,... | collective-permute-start | bytes 786440 | tf_op jit(solution)/shard_map/ppermute | solution.py:322
  123.9 5.7 %copy-start.16 = (f32[2,128,256]{2,1,0:T(8,128)S(1)}, f32[2,128,256]{2,1,0:T(8,128)}, u32[]{:S(2)}) copy-start(f32[2,128,256]{2,1,0:T(8,128)} %get-tuple-element.101) | copy-start | bytes 786436
  123.9 10.8 %copy-start.17 = (f32[2,128,256]{2,1,0:T(8,128)S(1)}, f32[2,128,256]{2,1,0:T(8,128)}, u32[]{:S(2)}) copy-start(f32[2,128,256]{2,1,0:T(8,128)} %get-tuple-element.102) | copy-start | bytes 786436
  123.9 13.9 %copy-start.12 = (f32[2,128,256]{2,1,0:T(8,128)S(1)}, f32[2,128,256]{2,1,0:T(8,128)}, u32[]{:S(2)}) copy-start(f32[2,128,256]{2,1,0:T(8,128)} %get-tuple-element.69.refs_0_) | copy-start | bytes 786436
  129.5 15.8 %collective-permute-start.25 = (f32[2,128,256]{2,1,0:T(8,128)S(1)}, f32[2,128,256]{2,1,0:T(8,128)S(1)}, u32[]{:S(2)}, u32[]{:S(2)}) collective-permute-start(f32[2,128,256]{2,1,0:T(8,128)S(1)} %copy-done.16), channel_id=1, source_target_pairs={{0,2},{2,0},{4,6},{6,4},{8,10},{10,8},{12,14},{14,12},{16,18},{18,... | collective-permute-start | bytes 786440 | tf_op jit(solution)/shard_map/ppermute | solution.py:322
  134.6 11.7 %collective-permute-start.26 = (f32[2,128,256]{2,1,0:T(8,128)S(1)}, f32[2,128,256]{2,1,0:T(8,128)S(1)}, u32[]{:S(2)}, u32[]{:S(2)}) collective-permute-start(f32[2,128,256]{2,1,0:T(8,128)S(1)} %copy-done.17), channel_id=1, source_target_pairs={{0,4},{2,6},{4,0},{6,2},{8,12},{10,14},{12,8},{14,10},{16,20},{18,... | collective-permute-start | bytes 786440 | tf_op jit(solution)/shard_map/ppermute | solution.py:322
  137.3 9.1 %collective-permute-start.31 = (f32[2,128,256]{2,1,0:T(8,128)S(1)}, f32[2,128,256]{2,1,0:T(8,128)S(1)}, u32[]{:S(2)}, u32[]{:S(2)}) collective-permute-start(f32[2,128,256]{2,1,0:T(8,128)S(1)} %get-tuple-element.109), channel_id=1, source_target_pairs={{0,1},{1,0},{2,3},{3,2},{4,5},{5,4},{6,7},{7,6},{8,9},{9,8},{10,11... | collective-permute-start | bytes 786440 | tf_op jit(solution)/shard_map/ppermute | solution.py:316
  137.3 9.6 %collective-permute-start.33 = (f32[2,128,256]{2,1,0:T(8,128)S(1)}, f32[2,128,256]{2,1,0:T(8,128)S(1)}, u32[]{:S(2)}, u32[]{:S(2)}) collective-permute-start(f32[2,128,256]{2,1,0:T(8,128)S(1)} %get-tuple-element.111), channel_id=1, source_target_pairs={{0,1},{1,0},{2,3},{3,2},{4,5},{5,4},{6,7},{7,6},{8,9},{9,8},{10,11... | collective-permute-start | bytes 786440 | tf_op jit(solution)/shard_map/ppermute | solution.py:316
  137.8 7.1 %copy-start.18 = (f32[2,128,256]{2,1,0:T(8,128)S(1)}, f32[2,128,256]{2,1,0:T(8,128)}, u32[]{:S(2)}) copy-start(f32[2,128,256]{2,1,0:T(8,128)} %get-tuple-element.103) | copy-start | bytes 786436
  144.9 9.3 %collective-permute-start.27 = (f32[2,128,256]{2,1,0:T(8,128)S(1)}, f32[2,128,256]{2,1,0:T(8,128)S(1)}, u32[]{:S(2)}, u32[]{:S(2)}) collective-permute-start(f32[2,128,256]{2,1,0:T(8,128)S(1)} %copy-done.18), channel_id=1, source_target_pairs={{0,6},{2,4},{4,2},{6,0},{8,14},{10,12},{12,10},{14,8},{16,22},{18,... | collective-permute-start | bytes 786440 | tf_op jit(solution)/shard_map/ppermute | solution.py:322
  145.3 14.2 %collective-permute-start.30 = (f32[3,128,256]{2,1,0:T(8,128)S(1)}, f32[3,128,256]{2,1,0:T(8,128)S(1)}, u32[]{:S(2)}, u32[]{:S(2)}) collective-permute-start(f32[3,128,256]{2,1,0:T(8,128)S(1)} %get-tuple-element.136), channel_id=1, source_target_pairs={{0,8},{2,10},{4,12},{6,14},{8,0},{10,2},{12,4},{14,6},{16,24},{18,... | collective-permute-start | bytes 1179656 | tf_op jit(solution)/shard_map/ppermute | solution.py:313
  146.4 1.5 collective-permute-start.36
  146.4 8.3 %collective-permute-start.40 = (f32[2,128,256]{2,1,0:T(8,128)S(1)}, f32[2,128,256]{2,1,0:T(8,128)S(1)}, u32[]{:S(2)}, u32[]{:S(2)}) collective-permute-start(f32[2,128,256]{2,1,0:T(8,128)S(1)} %get-tuple-element.120), channel_id=1, source_target_pairs={{0,1},{1,0},{2,3},{3,2},{4,5},{5,4},{6,7},{7,6},{8,9},{9,8},{10,11... | collective-permute-start | bytes 786440 | tf_op jit(solution)/shard_map/ppermute | solution.py:316
  146.9 11.3 %collective-permute-start.44 = (f32[3,128,256]{2,1,0:T(8,128)S(1)}, f32[3,128,256]{2,1,0:T(8,128)S(1)}, u32[]{:S(2)}, u32[]{:S(2)}) collective-permute-start(f32[3,128,256]{2,1,0:T(8,128)S(1)} %get-tuple-element.122), channel_id=1, source_target_pairs={{0,1},{1,0},{2,3},{3,2},{4,5},{5,4},{6,7},{7,6},{8,9},{9,8},{10,11... | collective-permute-start | bytes 1179656 | tf_op jit(solution)/shard_map/ppermute | solution.py:316
  147.9 15.0 %collective-permute-start.34 = (f32[2,128,256]{2,1,0:T(8,128)S(1)}, f32[2,128,256]{2,1,0:T(8,128)S(1)}, u32[]{:S(2)}, u32[]{:S(2)}) collective-permute-start(f32[2,128,256]{2,1,0:T(8,128)S(1)} %get-tuple-element.132), channel_id=1, source_target_pairs={{0,8},{2,10},{4,12},{6,14},{8,0},{10,2},{12,4},{14,6},{16,24},{18,... | collective-permute-start | bytes 786440 | tf_op jit(solution)/shard_map/ppermute | solution.py:313
  154.2 13.2 %collective-permute-start.32 = (f32[2,128,256]{2,1,0:T(8,128)S(1)}, f32[2,128,256]{2,1,0:T(8,128)S(1)}, u32[]{:S(2)}, u32[]{:S(2)}) collective-permute-start(f32[2,128,256]{2,1,0:T(8,128)S(1)} %get-tuple-element.140), channel_id=1, source_target_pairs={{0,8},{2,10},{4,12},{6,14},{8,0},{10,2},{12,4},{14,6},{16,24},{18,... | collective-permute-start | bytes 786440 | tf_op jit(solution)/shard_map/ppermute | solution.py:313
  154.7 18.0 %collective-permute-start.37 = (f32[2,128,256]{2,1,0:T(8,128)S(1)}, f32[2,128,256]{2,1,0:T(8,128)S(1)}, u32[]{:S(2)}, u32[]{:S(2)}) collective-permute-start(f32[2,128,256]{2,1,0:T(8,128)S(1)} %add.56), channel_id=1, source_target_pairs={{0,8},{2,10},{4,12},{6,14},{24,16},{26,18},{28,20},{30,22},{1,9},{... | collective-permute-start | bytes 786440 | tf_op jit(solution)/shard_map/ppermute | solution.py:313
  158.2 20.2 %collective-permute-start.41 = (f32[2,128,256]{2,1,0:T(8,128)S(1)}, f32[2,128,256]{2,1,0:T(8,128)S(1)}, u32[]{:S(2)}, u32[]{:S(2)}) collective-permute-start(f32[2,128,256]{2,1,0:T(8,128)S(1)} %add.59), channel_id=1, source_target_pairs={{0,8},{2,10},{4,12},{6,14},{24,16},{26,18},{28,20},{30,22},{1,9},{... | collective-permute-start | bytes 786440 | tf_op jit(solution)/shard_map/ppermute | solution.py:313
  159.6 26.1 %collective-permute-start.45 = (f32[3,128,256]{2,1,0:T(8,128)S(1)}, f32[3,128,256]{2,1,0:T(8,128)S(1)}, u32[]{:S(2)}, u32[]{:S(2)}) collective-permute-start(f32[3,128,256]{2,1,0:T(8,128)S(1)} %add.62), channel_id=1, source_target_pairs={{0,8},{2,10},{4,12},{6,14},{24,16},{26,18},{28,20},{30,22},{1,9},{... | collective-permute-start | bytes 1179656 | tf_op jit(solution)/shard_map/ppermute | solution.py:313
  160.9 6.5 %copy-start.19 = (f32[2,128,256]{2,1,0:T(8,128)S(1)}, f32[2,128,256]{2,1,0:T(8,128)}, u32[]{:S(2)}) copy-start(f32[2,128,256]{2,1,0:T(8,128)} %get-tuple-element.89) | copy-start | bytes 786436
  160.9 11.8 %copy-start.20 = (f32[2,128,256]{2,1,0:T(8,128)S(1)}, f32[2,128,256]{2,1,0:T(8,128)}, u32[]{:S(2)}) copy-start(f32[2,128,256]{2,1,0:T(8,128)} %get-tuple-element.90) | copy-start | bytes 786436
  160.9 17.5 %copy-start.21 = (f32[2,128,256]{2,1,0:T(8,128)S(1)}, f32[2,128,256]{2,1,0:T(8,128)}, u32[]{:S(2)}) copy-start(f32[2,128,256]{2,1,0:T(8,128)} %get-tuple-element.91) | copy-start | bytes 786436
  163.0 23.4 %collective-permute-start.43 = (f32[3,128,256]{2,1,0:T(8,128)S(1)}, f32[3,128,256]{2,1,0:T(8,128)S(1)}, u32[]{:S(2)}, u32[]{:S(2)}) collective-permute-start(f32[3,128,256]{2,1,0:T(8,128)S(1)} %add.61), channel_id=1, source_target_pairs={{8,16},{10,18},{12,20},{14,22},{16,8},{18,10},{20,12},{22,14},{9,1... | collective-permute-start | bytes 1179656 | tf_op jit(solution)/shard_map/ppermute | solution.py:313
  167.4 19.8 %collective-permute-start.16 = (f32[2,128,256]{2,1,0:T(8,128)S(1)}, f32[2,128,256]{2,1,0:T(8,128)S(1)}, u32[]{:S(2)}, u32[]{:S(2)}) collective-permute-start(f32[2,128,256]{2,1,0:T(8,128)S(1)} %copy-done.19), channel_id=1, source_target_pairs={{0,2},{2,0},{4,6},{6,4},{8,10},{10,8},{12,14},{14,12},{16,18},{18,... | collective-permute-start | bytes 786440 | tf_op jit(solution)/shard_map/ppermute | solution.py:322
  172.7 15.8 %collective-permute-start.17 = (f32[2,128,256]{2,1,0:T(8,128)S(1)}, f32[2,128,256]{2,1,0:T(8,128)S(1)}, u32[]{:S(2)}, u32[]{:S(2)}) collective-permute-start(f32[2,128,256]{2,1,0:T(8,128)S(1)} %copy-done.20), channel_id=1, source_target_pairs={{0,4},{2,6},{4,0},{6,2},{8,12},{10,14},{12,8},{14,10},{16,20},{18,... | collective-permute-start | bytes 786440 | tf_op jit(solution)/shard_map/ppermute | solution.py:322
  178.4 11.5 %collective-permute-start.18 = (f32[2,128,256]{2,1,0:T(8,128)S(1)}, f32[2,128,256]{2,1,0:T(8,128)S(1)}, u32[]{:S(2)}, u32[]{:S(2)}) collective-permute-start(f32[2,128,256]{2,1,0:T(8,128)S(1)} %copy-done.21), channel_id=1, source_target_pairs={{0,6},{2,4},{4,2},{6,0},{8,14},{10,12},{12,10},{14,8},{16,22},{18,... | collective-permute-start | bytes 786440 | tf_op jit(solution)/shard_map/ppermute | solution.py:322
  180.4 1.0 copy-start.9
  180.4 1.1 copy-start.11
  185.6 38.9 %collective-permute-start.35 = (f32[2,128,256]{2,1,0:T(8,128)S(1)}, f32[2,128,256]{2,1,0:T(8,128)S(1)}, u32[]{:S(2)}, u32[]{:S(2)}) collective-permute-start(f32[2,128,256]{2,1,0:T(8,128)S(1)} %add.55), channel_id=1, source_target_pairs={{8,16},{10,18},{12,20},{14,22},{16,8},{18,10},{20,12},{22,14},{9,1... | collective-permute-start | bytes 786440 | tf_op jit(solution)/shard_map/ppermute | solution.py:313
  186.4 5.0 %copy-start.10 = (f32[2,128,256]{2,1,0:T(8,128)S(1)}, f32[2,128,256]{2,1,0:T(8,128)}, u32[]{:S(2)}) copy-start(f32[2,128,256]{2,1,0:T(8,128)} %get-tuple-element.88.refs_0_) | copy-start | bytes 786436
  186.4 37.1 %collective-permute-start.39 = (f32[2,128,256]{2,1,0:T(8,128)S(1)}, f32[2,128,256]{2,1,0:T(8,128)S(1)}, u32[]{:S(2)}, u32[]{:S(2)}) collective-permute-start(f32[2,128,256]{2,1,0:T(8,128)S(1)} %add.58), channel_id=1, source_target_pairs={{8,16},{10,18},{12,20},{14,22},{16,8},{18,10},{20,12},{22,14},{9,1... | collective-permute-start | bytes 786440 | tf_op jit(solution)/shard_map/ppermute | solution.py:313
  187.2 37.3 %collective-permute-start.38 = (f32[2,128,256]{2,1,0:T(8,128)S(1)}, f32[2,128,256]{2,1,0:T(8,128)S(1)}, u32[]{:S(2)}, u32[]{:S(2)}) collective-permute-start(f32[2,128,256]{2,1,0:T(8,128)S(1)} %add.57), channel_id=1, source_target_pairs={{8,24},{10,26},{12,28},{14,30},{16,0},{18,2},{20,4},{22,6},{9,25},... | collective-permute-start | bytes 786440 | tf_op jit(solution)/shard_map/ppermute | solution.py:313
  188.5 35.0 %collective-permute-start.42 = (f32[2,128,256]{2,1,0:T(8,128)S(1)}, f32[2,128,256]{2,1,0:T(8,128)S(1)}, u32[]{:S(2)}, u32[]{:S(2)}) collective-permute-start(f32[2,128,256]{2,1,0:T(8,128)S(1)} %add.60), channel_id=1, source_target_pairs={{8,24},{10,26},{12,28},{14,30},{16,0},{18,2},{20,4},{22,6},{9,25},... | collective-permute-start | bytes 786440 | tf_op jit(solution)/shard_map/ppermute | solution.py:313
  189.8 32.0 %collective-permute-start.46 = (f32[3,128,256]{2,1,0:T(8,128)S(1)}, f32[3,128,256]{2,1,0:T(8,128)S(1)}, u32[]{:S(2)}, u32[]{:S(2)}) collective-permute-start(f32[3,128,256]{2,1,0:T(8,128)S(1)} %add.63), channel_id=1, source_target_pairs={{8,24},{10,26},{12,28},{14,30},{16,0},{18,2},{20,4},{22,6},{9,25},... | collective-permute-start | bytes 1179656 | tf_op jit(solution)/shard_map/ppermute | solution.py:313
  191.3 30.5 %copy-start.1 = (f32[7,1,128,256]{3,2,1,0:T(8,128)S(1)}, f32[7,1,128,256]{3,2,1,0:T(8,128)}, u32[]{:S(2)}) copy-start(f32[7,1,128,256]{3,2,1,0:T(8,128)} %one_ref.5) | copy-start | bytes 2752516
  191.3 30.5 %copy-start.2 = (f32[7,1,128,256]{3,2,1,0:T(8,128)S(1)}, f32[7,1,128,256]{3,2,1,0:T(8,128)}, u32[]{:S(2)}) copy-start(f32[7,1,128,256]{3,2,1,0:T(8,128)} %two_ref.5) | copy-start | bytes 2752516
  (5 other events, 4.0 us)

commit v2 on v1

--- a/solution.py
+++ b/solution.py
@@ -150,9 +150,9 @@
     )(slot_col, *pieces, *([before] if added else []))
 
 
-def adam_body(w_ref, one_ref, two_ref, base_ref, mid_ref, far_ref, *refs):
+def adam_body(w_ref, one_ref, two_ref, base_ref, far_ref, last_ref, *refs):
     new_w, new_one, new_two = refs[-3:]
-    grad = base_ref[0] + (mid_ref[0] + far_ref[0])
+    grad = base_ref[0] + (far_ref[0] + last_ref[0])
     one = 0.9 * one_ref[0, 0] + 0.1 * grad
     two = 0.999 * two_ref[0, 0] + 0.001 * grad * grad
     new_one[0, 0] = one
@@ -160,7 +160,7 @@
     new_w[0, 0] = w_ref[0, 0] - 0.01 * (one / CORR_ONE) / (jnp.sqrt(two / CORR_TWO) + 1e-08)
 
 
-def adam(weights, moment_one, moment_two, base, mid, far, chunk, mid_low, buffers):
+def adam(weights, moment_one, moment_two, base, far, last, chunk, buffers):
     _, _, shard, width = weights.shape
     low = min(chunk)
     whole = pl.BlockSpec((1, 1, shard, width), lambda i: (low + i, 0, 0, 0))
@@ -169,9 +169,8 @@
         adam_body,
         grid=(len(chunk),),
         in_specs=[whole] * 3
+        + [pl.BlockSpec((1, shard, width), lambda i: (low + i, 0, 0))] * 2
         + [
-            pl.BlockSpec((1, shard, width), lambda i: (low + i, 0, 0)),
-            pl.BlockSpec((1, shard, width), lambda i: (low - mid_low + i, 0, 0)),
             pl.BlockSpec((1, shard, width), lambda i: (i, 0, 0)),
         ]
         + [pl.BlockSpec(memory_space=pl.ANY)] * (3 if aliased else 0),
@@ -181,19 +180,24 @@
         compiler_params=pltpu.CompilerParams(vmem_limit_bytes=48 * 2**20),
         cost_estimate=pl.CostEstimate(
             flops=20 * len(chunk) * shard * width,
-            bytes_accessed=36 * len(chunk) * shard * width,
+            bytes_accessed=32 * len(chunk) * shard * width,
             transcendentals=len(chunk) * shard * width,
         ),
         name="adam",
-    )(weights, moment_one, moment_two, base, mid, far, *(buffers or ()))
-
-
-def step_body(size, cap, layers, chunks, aliased, *refs):
+    )(weights, moment_one, moment_two, base, far, last, *(buffers or ()))
+
+
+def step_body(size, cap, layers, chunks, aliased, forwarded, *refs):
     sent = refs[:size]
     mine, other = refs[size : size + 2]
-    at = size + 2 + (size if aliased else 0)
+    at = size + 2
+    passed = refs[at] if forwarded else None
+    at += int(forwarded) + (size if aliased else 0)
     outs = refs[at : at + size]
     at += size
+    back_out = refs[at] if forwarded else None
+    at += int(forwarded)
+    items = size * cap
     keeps = refs[at : at + len(chunks)]
     sends = refs[at + len(chunks) : at + 2 * len(chunks)]
     at += 2 * len(chunks)
@@ -208,6 +212,10 @@
         high, low = split(sent[m][0])
         ah[0, m * cap : (m + 1) * cap] = high
         al[0, m * cap : (m + 1) * cap] = low
+        if forwarded:
+            high, low = split(passed[m, 0])
+            ah[0, items + m * cap : items + (m + 1) * cap] = high
+            al[0, items + m * cap : items + (m + 1) * cap] = low
 
     def weights(layer):
         high, low = split(mine[layer])
@@ -233,9 +241,13 @@
     result = dot3(ah[last], al[last], wh[last], wl[last], NN)
     for m in range(size):
         outs[m][0] = result[m * cap : (m + 1) * cap]
-
-    delta = jnp.concatenate([sent[m][1] for m in range(size)], axis=0)
-    dh, dl = split(delta)
+        if forwarded:
+            back_out[m] = result[items + m * cap : items + (m + 1) * cap]
+
+    delta = [sent[m][1] for m in range(size)]
+    if forwarded:
+        delta += [passed[m, 1] for m in range(size)]
+    dh, dl = split(jnp.concatenate(delta, axis=0))
     for keep, send, chunk in zip(keeps, sends, chunks):
         for layer in chunk:
             place = layer - min(chunk)
@@ -247,27 +259,33 @@
                 dh, dl = split(back * slope[layer - 1])
 
 
-def step_call(sent, mine, other, buffers, which, chunks):
+def step_call(sent, mine, other, buffers, which, chunks, passed=None):
     size = len(sent)
     cap, width = sent[0].shape[1:]
     layers, shard = mine.shape[:2]
-    items = size * cap
+    forwarded = passed is not None
+    aliased = buffers is not None
+    items = size * cap * (2 if forwarded else 1)
     row_spec = pl.BlockSpec((2, cap, width), lambda i: (0, 0, 0))
+    pass_spec = pl.BlockSpec((size, 2, cap, width), lambda i: (0, 0, 0, 0))
+    back_spec = pl.BlockSpec((size, cap, width), lambda i: (0, 0, 0))
     weight_spec = pl.BlockSpec((layers, shard, width), lambda i: (0, 0, 0))
     outs = [pltpu.HBM((2, cap, width), F32)] * size
     out_specs = [pl.BlockSpec((1, cap, width), lambda i: (which, 0, 0))] * size
+    back = [jax.ShapeDtypeStruct((size, cap, width), F32)] * forwarded
     grads = [jax.ShapeDtypeStruct((len(c), shard, width), F32) for c in chunks] * 2
     grad_specs = [pl.BlockSpec((len(c), shard, width), lambda i: (0, 0, 0)) for c in chunks] * 2
-    aliased = buffers is not None
+    first = size + 2 + int(forwarded)
     result = pl.pallas_call(
-        functools.partial(step_body, size, cap, layers, chunks, aliased),
+        functools.partial(step_body, size, cap, layers, chunks, aliased, forwarded),
         grid=(1,),
         in_specs=[row_spec] * size
         + [weight_spec] * 2
+        + [pass_spec] * forwarded
         + [pl.BlockSpec(memory_space=pl.ANY)] * (size if aliased else 0),
-        out_specs=out_specs + grad_specs,
-        out_shape=outs + grads,
-        input_output_aliases={size + 2 + m: m for m in range(size)} if aliased else {},
+        out_specs=out_specs + [back_spec] * forwarded + grad_specs,
+        out_shape=outs + back + grads,
+        input_output_aliases={first + m: m for m in range(size)} if aliased else {},
         scratch_shapes=[
             pltpu.VMEM((layers, width, width), BF16),
             pltpu.VMEM((layers, width, width), BF16),
@@ -283,19 +301,20 @@
             transcendentals=layers * items * width,
         ),
         name="step",
-    )(*sent, mine, other, *(buffers or ()))
+    )(*sent, mine, other, *([passed] if forwarded else []), *(buffers or ()))
     n = len(chunks)
-    return result[:size], result[size : size + n], result[size + n :]
-
-
-PAIRS = ((1, 2), (0, 3))
+    at = size + int(forwarded)
+    return result[:at], result[at : at + n], result[at + n :]
+
+
+LEAVING = (3, 1, 0, 2)
 
 
 def chunks_of(layers, step):
     order = list(range(layers - 1, -1, -1))
     first, second = layers - layers // 3 * 2, layers // 3
     cut = [order[:first], order[first : first + second], order[first + second :]]
-    return cut if step > 1 else [order]
+    return cut if step == 2 else [order]
 
 
 def on_device(samples, routes, cotangent, weights, moment_one, moment_two):
@@ -336,59 +355,52 @@
     middle = along(own, MIDDLE)
     own_other = swap_core(own)
     arrived = {}
-    for i, steps in enumerate(PAIRS):
-        packed, slot_col = pack(
-            route_row, samples, cotangent, size, cap, groups, steps, routes if i else None
+    packed, slot_col = pack(
+        route_row, samples, cotangent, size, cap, groups, LEAVING, routes
+    )
+    for step, values in zip(LEAVING, packed):
+        arrived[step] = exchange(values)
+    beyond = along(side, MIDDLE)
+    middle_out = along(middle, OUTWARD)
+    passed = along(jnp.stack(arrived[3]), INWARD)
+    second = middle + middle_out
+    mats = {0: (own, own_other)}
+    for step, value in ((1, side), (3, beyond), (2, second)):
+        mats[step] = (value, swap_core(value))
+
+    sums = {}
+
+    def run(step, buffers, which, extra=None):
+        outs, keeps, sends = step_call(
+            arrived[step], *mats[step], buffers, which, chunks_of(layers, step), extra
         )
-        for step, values in zip(steps, packed):
-            arrived[step] = exchange(values)
-    side_in = along(side, MIDDLE)
-    middle_out = along(middle, OUTWARD)
-    second = middle + middle_out
-
-    mats = {
-        0: lambda: (own, own_other),
-        1: lambda: (side, swap_core(side)),
-        2: lambda: (second, swap_core(second)),
-        3: lambda: (third, swap_core(third)),
-    }
-    outputs = {}
-    sums = {}
-    for i, steps in enumerate(PAIRS):
-        buffers = None
-        for which, step in enumerate(steps):
-            if step == 3:
-                late, _ = lax.optimization_barrier((p3, buffers[0]))
-                third = jnp.where(inner, side_in, late)
-            pair = mats[step]()
-            buffers, keeps, sends = step_call(
-                arrived[step], *pair, buffers, which, chunks_of(layers, step)
-            )
-            sums[step] = [keep + swap_core(send) for keep, send in zip(keeps, sends)]
-            if step == 1:
-                one = sums[1][0]
-                p3 = along(jnp.where(inner, side_in, one), SIDES)
-        outputs[i] = exchange(buffers)
-
-    zero = sums[0][0]
-    cut_two, cut_three = chunks_of(layers, 2), chunks_of(layers, 3)
-    p4, mid = [], []
-    for value, c in zip(sums[2], cut_two):
-        back = along(jnp.where(inner, one[min(c) : max(c) + 1], value), SIDES)
-        p4.append(back)
-        mid.append(along(value + back, MIDDLE))
-    kept, sides, *late = lax.optimization_barrier((zero, p3, *p4))
-    base = kept + jnp.where(inner, sides, jnp.concatenate(late[::-1], axis=0))
+        sums[step] = []
+        for keep, send in zip(keeps, sends):
+            sums[step].append(keep + swap_core(send))
+        return outs
+
+    near = run(1, None, 0)
+    rest = run(0, None, 0)
+    *rest, back = run(3, rest, 1, passed)
+    near = run(2, near, 1)
+    back = along(back, OUTWARD)
+    rest = [
+        jnp.stack([value[0], jnp.where(inner, value[1], back[m])])
+        for m, value in enumerate(rest)
+    ]
+    outputs = [exchange(near), exchange(rest)]
+
+    zero, one, three = sums[0][0], sums[1][0], sums[3][0]
+    from_side = along(one, SIDES)
+    from_far = along(three, FAR)
+    base = zero + from_side
     updated = None
-    for value, c in zip(sums[3], cut_three):
-        passed = value + along(value, INWARD)
-        far = along(passed, FAR)
-        k = next(k for k, d in enumerate(cut_two) if min(c) in d)
-        updated = adam(
-            weights, moment_one, moment_two, base, mid[k], far, c, min(cut_two[k]), updated
-        )
+    for value, c in zip(sums[2], chunks_of(layers, 2)):
+        joined = value + along(value, INWARD)
+        last = along(joined, MIDDLE)
+        updated = adam(weights, moment_one, moment_two, base, from_far, last, c, updated)
     result = None
-    for i, steps in enumerate(PAIRS):
+    for i, steps in enumerate(((1, 2), (0, 3))):
         result = unpack(slot_col, outputs[i], result, steps, cap)
     return (result, *updated)
 

time: 226 us -> 205 us (0.907)
  the two profiles are of different devices: /device:TPU:0 before, /device:TPU:10 now
where the time goes in v2:
time: 205 us
  waiting for transfers between devices  87.5 us (43%)
  starting transfers between devices  52.7 us (26%)
  Pallas kernels  51.1 us (25%)
  other arithmetic  7.77 us (4%)
  local copies, waits for them, and re-layouts  4.53 us (2%)
    ppermute x14, waiting for transfers between devices, along(): return lax.ppermute(value, 'expert', plane_pairs(pairs))  50.9 us
    ppermute x18, waiting for transfers between devices, exchange(): lax.ppermute(values[mask], 'expert', [(e, e ^ mask) for e in range(groups)])  36.6 us
    pallas_call x4, Pallas kernels, step_call(): pl.pallas_call(functools.partial(step_body, size, cap, layers, chunks, al...  34.9 us
    ppermute x14, starting transfers between devices, along(): return lax.ppermute(value, 'expert', plane_pairs(pairs))  28.7 us
    ppermute x18, starting transfers between devices, exchange(): lax.ppermute(values[mask], 'expert', [(e, e ^ mask) for e in range(groups)])  22.7 us
    pallas_call x1, Pallas kernels, pack(): pl.pallas_call(functools.partial(pack_body, size, cap, groups, steps, wit...  8.03 us
    pallas_call x2, Pallas kernels, unpack(): pl.pallas_call(functools.partial(unpack_body, size, cap, steps, added), o...  4.58 us
    unnamed x53, local copies, waits for them, and re-layouts  4.53 us
  transfers between devices with their start and end apart: 42, of which 15 were waited for; matrix products, arithmetic and copies ran while one was open for 4% of the time, Pallas kernels for 24%

profile of v2, /device:TPU:10, one launch (start us, length us, event | category | flops | bytes accessed | tf_op | source)
XLA Modules:
  0.0 204.8 jit_solution(8903381238581204007)
XLA Ops:
  0.6 3.5 %collective-permute-start.18 = (f32[7,128,256]{2,1,0:T(8,128)}, f32[7,128,256]{2,1,0:T(8,128)}, u32[]{:S(2)}, u32[]{:S(2)}) collective-permute-start(f32[7,128,256]{2,1,0:T(8,128)} %bitcast.6), channel_id=1, source_target_pairs={{8,16},{10,18},{12,20},{14,22},{16,8},{18,10},{20,12},{22,14},{9,1... | collective-permute-start | bytes 2752520 | tf_op jit(solution)/shard_map/ppermute | solution.py:332
  4.2 0.9 copy.24.refs_3_
  5.1 8.0 %pack.1 = (f32[2,128,256]{2,1,0:T(8,128)}, f32[2,128,256]{2,1,0:T(8,128)S(1)}, f32[2,128,256]{2,1,0:T(8,128)S(1)}, f32[2,128,256]{2,1,0:T(8,128)S(1)}, f32[2,128...) custom-call(s32[1,1024]{1,0:T(1,128)S(1)} %bitcast.14, ...), custom_call_target="tpu_custom_call" | custom-call | flops 2147483648 | bytes 3145728 | tf_op jit(solution)/shard_map/pack/pallas_call | solution.py:103
  13.2 0.5 collective-permute-start.21
  13.7 1.5 collective-permute-start.22
  15.2 9.7 %collective-permute-done.18 = f32[7,128,256]{2,1,0:T(8,128)} collective-permute-done((f32[7,128,256]{2,1,0:T(8,128)}, f32[7,128,256]{2,1,0:T(8,128)}, u32[]{:S(2)}, u32[]{:S(2)}) %collective-permute-start.18) | collective-permute-done | bytes 917536 | tf_op jit(solution)/shard_map/ppermute | solution.py:332
  24.9 1.3 collective-permute-start.19
  26.3 1.6 collective-permute-start.23
  27.8 1.5 collective-permute-start.7
  29.3 0.5 collective-permute-start.8
  29.8 6.6 %collective-permute-done.23.refs_3_ = f32[2,128,256]{2,1,0:T(8,128)S(1)} collective-permute-done((f32[2,128,256]{2,1,0:T(8,128)S(1)}, f32[2,128,256]{2,1,0:T(8,128)S(1)}, u32[]{:S(2)}, u32[]{:S(2)}) %collective-permute-start.23) | collective-permute-done | bytes 262176 | tf_op jit(solution)/shard_map/ppermute | solution.py:341
  36.5 3.5 %collective-permute-start.4 = (f32[7,128,256]{2,1,0:T(8,128)S(1)}, f32[7,128,256]{2,1,0:T(8,128)S(1)}, u32[]{:S(2)}, u32[]{:S(2)}) collective-permute-start(f32[7,128,256]{2,1,0:T(8,128)S(1)} %collective-permute-done.3.refs_4_), channel_id=1, source_target_pairs={{8,16},{10,18},{12,20},{14,22},{16,8},{18,10},{20,12},{22,14},{9,1... | collective-permute-start | bytes 2752520 | tf_op jit(solution)/shard_map/ppermute | solution.py:332
  40.2 0.5 collective-permute-start
  40.7 1.4 collective-permute-start.1
  42.1 6.4 %collective-permute-done.refs_1_ = f32[2,128,256]{2,1,0:T(8,128)S(1)} collective-permute-done((f32[2,128,256]{2,1,0:T(8,128)S(1)}, f32[2,128,256]{2,1,0:T(8,128)S(1)}, u32[]{:S(2)}, u32[]{:S(2)}) %collective-permute-start) | collective-permute-done | bytes 262176 | tf_op jit(solution)/shard_map/ppermute | solution.py:341
  48.7 2.4 %collective-permute-start.2 = (f32[2,128,256]{2,1,0:T(8,128)S(1)}, f32[2,128,256]{2,1,0:T(8,128)S(1)}, u32[]{:S(2)}, u32[]{:S(2)}) collective-permute-start(f32[2,128,256]{2,1,0:T(8,128)S(1)} %get-tuple-element.63), channel_id=1, source_target_pairs={{0,6},{2,4},{4,2},{6,0},{8,14},{10,12},{12,10},{14,8},{16,22},{18,... | collective-permute-start | bytes 786440 | tf_op jit(solution)/shard_map/ppermute | solution.py:341
  51.2 0.5 collective-permute-start.9
  51.7 1.3 add.33.refs_4_
  53.0 5.8 %collective-permute-done.2.refs_3_ = f32[2,128,256]{2,1,0:T(8,128)S(1)} collective-permute-done((f32[2,128,256]{2,1,0:T(8,128)S(1)}, f32[2,128,256]{2,1,0:T(8,128)S(1)}, u32[]{:S(2)}, u32[]{:S(2)}) %collective-permute-start.2) | collective-permute-done | bytes 262176 | tf_op jit(solution)/shard_map/ppermute | solution.py:341
  58.9 4.8 %collective-permute-done.9.refs_3_ = f32[2,128,256]{2,1,0:T(8,128)S(1)} collective-permute-done((f32[2,128,256]{2,1,0:T(8,128)S(1)}, f32[2,128,256]{2,1,0:T(8,128)S(1)}, u32[]{:S(2)}, u32[]{:S(2)}) %collective-permute-start.9) | collective-permute-done | bytes 262176 | tf_op jit(solution)/shard_map/ppermute | solution.py:341
  63.7 0.5 collective-permute-start.15
  64.3 1.5 collective-permute-start.6
  65.8 6.9 %step.4 = (f32[2,128,256]{2,1,0:T(8,128)}, f32[2,128,256]{2,1,0:T(8,128)}, f32[2,128,256]{2,1,0:T(8,128)}, f32[2,128,256]{2,1,0:T(8,128)}, f32[7,128,256]{2,1,0:T(8,128)S(1)}, /*index=5*/f32[7,128,256]{2,1,0:T(8,128)S(1)}) custom-call(f32[2,128,256]{2,1,0:T(8,128)S(1)} %copy-done.14, f32[2,128,256]{2,1,0:T(8,128)S(1)} %collective-permute-done.7.refs_1_, ...), custom_call_target="tpu_custom_call" | custom-call | flops 4227858432 | bytes 5242880 | tf_op jit(solution)/shard_map/step/pallas_call | solution.py:279
  72.8 1.0 copy-done.6
  73.7 1.5 collective-permute-start.16
  75.2 1.4 collective-permute-start.17
  76.7 6.9 %step.6 = (f32[2,128,256]{2,1,0:T(8,128)}, f32[2,128,256]{2,1,0:T(8,128)}, f32[2,128,256]{2,1,0:T(8,128)}, f32[2,128,256]{2,1,0:T(8,128)}, f32[7,128,256]{2,1,0:T(8,128)S(1)}, /*index=5*/f32[7,128,256]{2,1,0:T(8,128)S(1)}) custom-call(f32[2,128,256]{2,1,0:T(8,128)S(1)} %copy-done.13, f32[2,128,256]{2,1,0:T(8,128)S(1)} %collective-permute-done.21.refs_1_, ...), custom_call_target="tpu_custom_call" | custom-call | flops 4227858432 | bytes 5242880 | tf_op jit(solution)/shard_map/step/pallas_call | solution.py:279
  83.6 0.9 copy-done.3
  84.5 3.5 %collective-permute-done.16.refs_2_ = f32[2,128,256]{2,1,0:T(8,128)S(1)} collective-permute-done((f32[2,128,256]{2,1,0:T(8,128)S(1)}, f32[2,128,256]{2,1,0:T(8,128)S(1)}, u32[]{:S(2)}, u32[]{:S(2)}) %collective-permute-start.16) | collective-permute-done | bytes 262176 | tf_op jit(solution)/shard_map/ppermute | solution.py:341
  88.0 6.9 %step.7 = (f32[2,128,256]{2,1,0:T(8,128)}, f32[2,128,256]{2,1,0:T(8,128)}, f32[2,128,256]{2,1,0:T(8,128)}, f32[2,128,256]{2,1,0:T(8,128)}, f32[3,128,256]{2,1,0:...) custom-call(f32[2,128,256]{2,1,0:T(8,128)S(1)} %copy-done.12, ...), custom_call_target="tpu_custom_call", output_to_operand_aliasing={{0}: (6, {}), {1}: (7, {}), {2}: (8, {}), {3}: (9, {})} | custom-call | flops 4227858432 | bytes 5242880 | tf_op jit(solution)/shard_map/step/pallas_call | solution.py:279
  94.9 0.6 collective-permute-start.39
  95.6 1.0 copy-done.24
  96.6 14.2 %step.5 = (f32[2,128,256]{2,1,0:T(8,128)}, f32[2,128,256]{2,1,0:T(8,128)}, f32[2,128,256]{2,1,0:T(8,128)}, f32[2,128,256]{2,1,0:T(8,128)}, f32[4,128,256]{2,1,0:...) custom-call(f32[2,128,256]{2,1,0:T(8,128)S(1)} %copy-done.4, ...), custom_call_target="tpu_custom_call", output_to_operand_aliasing={{0}: (7, {}), {1}: (8, {}), {2}: (9, {}), {3}: (10, {})} | custom-call | flops 8455716864 | bytes 6815744 | tf_op jit(solution)/shard_map/step/pallas_call | solution.py:279
  111.3 1.6 collective-permute-start.25
  112.9 5.4 %collective-permute-start.11 = (f32[4,128,256]{2,1,0:T(8,128)}, f32[4,128,256]{2,1,0:T(8,128)}, u32[]{:S(2)}, u32[]{:S(2)}) collective-permute-start(f32[4,128,256]{2,1,0:T(8,128)} %get-tuple-element.73), channel_id=1, source_target_pairs={{8,0},{10,2},{12,4},{14,6},{16,24},{18,26},{20,28},{22,30},{9,1},{... | collective-permute-start | bytes 1572872 | tf_op jit(solution)/shard_map/ppermute | solution.py:332
  118.3 0.8 add.40
  119.1 1.5 collective-permute-start.26
  120.6 0.7 copy-done.8
  121.3 1.9 collective-permute-start.27
  123.2 1.3 collective-permute-start.37
  124.6 1.6 add.35
  126.4 6.7 %collective-permute-done.26.refs_2_ = f32[2,128,256]{2,1,0:T(8,128)} collective-permute-done((f32[2,128,256]{2,1,0:T(8,128)}, f32[2,128,256]{2,1,0:T(8,128)}, u32[]{:S(2)}, u32[]{:S(2)}) %collective-permute-start.26) | collective-permute-done | bytes 262176 | tf_op jit(solution)/shard_map/ppermute | solution.py:341
  133.4 1.3 collective-permute-start.34
  134.7 1.3 collective-permute-start.40
  136.0 1.2 slice_select_fusion
  137.3 1.7 collective-permute-start.14
  139.0 1.3 add.37
  140.3 21.7 %collective-permute-done.34 = f32[2,128,256]{2,1,0:T(8,128)S(1)} collective-permute-done((f32[2,128,256]{2,1,0:T(8,128)S(1)}, f32[2,128,256]{2,1,0:T(8,128)S(1)}, u32[]{:S(2)}, u32[]{:S(2)}) %collective-permute-start.34) | collective-permute-done | bytes 262176 | tf_op jit(solution)/shard_map/ppermute | solution.py:332
  162.0 1.4 collective-permute-start.32
  163.5 6.4 %collective-permute-done.40 = f32[3,128,256]{2,1,0:T(8,128)S(1)} collective-permute-done((f32[3,128,256]{2,1,0:T(8,128)S(1)}, f32[3,128,256]{2,1,0:T(8,128)S(1)}, u32[]{:S(2)}, u32[]{:S(2)}) %collective-permute-start.40) | collective-permute-done | bytes 393248 | tf_op jit(solution)/shard_map/ppermute | solution.py:332
  169.9 1.5 collective-permute-start.13
  171.4 0.5 collective-permute-start.12
  172.0 2.3 %unpack.2.refs_4_ = f32[1024,256]{1,0:T(8,128)S(1)} custom-call(s32[1024,1]{1,0:T(8,128)S(1)} %copy-done.10, f32[2,128,256]{2,1,0:T(8,128)S(1)} %copy-done.11, f32[2,128,256]{2,1,0:T(8,128)S(1)} %copy-done.9, f32[2,128,256]{2,1,0:T(8,128)} %collective-permute-done.26.refs_2_, f32[2,128,256]{2,1,0:T(8,128)} %collective-permute-done.27.refs_3_), custom_call_target="tpu_custom_call" | custom-call | flops 1073741824 | bytes 3145728 | tf_op jit(solution)/shard_map/unpack/pallas_call | solution.py:142
  174.3 1.1 add.41
  175.5 2.2 %collective-permute-done.13.refs_2_ = f32[2,128,256]{2,1,0:T(8,128)S(1)} collective-permute-done((f32[2,128,256]{2,1,0:T(8,128)S(1)}, f32[2,128,256]{2,1,0:T(8,128)S(1)}, u32[]{:S(2)}, u32[]{:S(2)}) %collective-permute-start.13) | collective-permute-done | bytes 262176 | tf_op jit(solution)/shard_map/ppermute | solution.py:341
  177.7 2.3 %collective-permute-start.38 = (f32[2,128,256]{2,1,0:T(8,128)S(1)}, f32[2,128,256]{2,1,0:T(8,128)S(1)}, u32[]{:S(2)}, u32[]{:S(2)}) collective-permute-start(f32[2,128,256]{2,1,0:T(8,128)S(1)} %add.41), channel_id=1, source_target_pairs={{8,16},{10,18},{12,20},{14,22},{16,8},{18,10},{20,12},{22,14},{9,1... | collective-permute-start | bytes 786440 | tf_op jit(solution)/shard_map/ppermute | solution.py:332
  180.1 3.5 %collective-permute-start.41 = (f32[3,128,256]{2,1,0:T(8,128)S(1)}, f32[3,128,256]{2,1,0:T(8,128)S(1)}, u32[]{:S(2)}, u32[]{:S(2)}) collective-permute-start(f32[3,128,256]{2,1,0:T(8,128)S(1)} %add.43), channel_id=1, source_target_pairs={{8,16},{10,18},{12,20},{14,22},{16,8},{18,10},{20,12},{22,14},{9,1... | collective-permute-start | bytes 1179656 | tf_op jit(solution)/shard_map/ppermute | solution.py:332
  183.6 2.3 %unpack.3 = f32[1024,256]{1,0:T(8,128)} custom-call(s32[1024,1]{1,0:T(8,128)S(1)} %copy-done.10, f32[2,128,256]{2,1,0:T(8,128)S(1)} %pad_maximum_fusion.1.refs_0_, f32[2,128,256]{2,1,0:T(8,128)S(1)} %collective-permute-done.12.refs_1_, f32[2,128,256]{2,1,0:T(8,128)S(1)} %collective-permute-done.13.refs_2_, ...), custom_call_target="tpu_custom_call" | custom-call | flops 1073741824 | bytes 3145728 | tf_op jit(solution)/shard_map/unpack/pallas_call | solution.py:142
  185.8 2.3 %collective-permute-start.35 = (f32[2,128,256]{2,1,0:T(8,128)S(1)}, f32[2,128,256]{2,1,0:T(8,128)S(1)}, u32[]{:S(2)}, u32[]{:S(2)}) collective-permute-start(f32[2,128,256]{2,1,0:T(8,128)S(1)} %add.39), channel_id=1, source_target_pairs={{8,16},{10,18},{12,20},{14,22},{16,8},{18,10},{20,12},{22,14},{9,1... | collective-permute-start | bytes 786440 | tf_op jit(solution)/shard_map/ppermute | solution.py:332
  188.4 11.7 %collective-permute-done.41.last_ref = f32[3,128,256]{2,1,0:T(8,128)S(1)} collective-permute-done((f32[3,128,256]{2,1,0:T(8,128)S(1)}, f32[3,128,256]{2,1,0:T(8,128)S(1)}, u32[]{:S(2)}, u32[]{:S(2)}) %collective-permute-start.41) | collective-permute-done | bytes 393248 | tf_op jit(solution)/shard_map/ppermute | solution.py:332
  200.2 1.6 adam.3
  201.8 1.0 adam.4
  202.8 1.1 collective-permute-done.35.last_ref
  203.9 0.9 adam.5
  (99 shorter events, 2.1 us)
Async XLA Ops:
  0.6 4.5 %copy-start.5 = (s32[1024,1]{0,1:T(1,128)S(1)}, s32[1024,1]{0,1:T(1,128)}, u32[]{:S(2)}) copy-start(s32[1024,1]{0,1:T(1,128)} %param.7) | copy-start | bytes 12292
  0.6 24.3 %collective-permute-start.18 = (f32[7,128,256]{2,1,0:T(8,128)}, f32[7,128,256]{2,1,0:T(8,128)}, u32[]{:S(2)}, u32[]{:S(2)}) collective-permute-start(f32[7,128,256]{2,1,0:T(8,128)} %bitcast.6), channel_id=1, source_target_pairs={{8,16},{10,18},{12,20},{14,22},{16,8},{18,10},{20,12},{22,14},{9,1... | collective-permute-start | bytes 2752520 | tf_op jit(solution)/shard_map/ppermute | solution.py:332
  4.1 32.3 %collective-permute-start.3 = (f32[7,128,256]{2,1,0:T(8,128)}, f32[7,128,256]{2,1,0:T(8,128)S(1)}, u32[]{:S(2)}, u32[]{:S(2)}) collective-permute-start(f32[7,128,256]{2,1,0:T(8,128)} %bitcast.7), channel_id=1, source_target_pairs={{0,8},{2,10},{4,12},{6,14},{8,0},{10,2},{12,4},{14,6},{16,24},{18,... | collective-permute-start | bytes 2752520 | tf_op jit(solution)/shard_map/ppermute | solution.py:332
  5.1 31.3 %copy-start = (f32[7,1,128,256]{3,2,1,0:T(8,128)S(1)}, f32[7,1,128,256]{3,2,1,0:T(8,128)}, u32[]{:S(2)}) copy-start(f32[7,1,128,256]{3,2,1,0:T(8,128)} %w_ref.5) | copy-start | bytes 2752516
  13.2 14.7 %collective-permute-start.21 = (f32[2,128,256]{2,1,0:T(8,128)S(1)}, f32[2,128,256]{2,1,0:T(8,128)S(1)}, u32[]{:S(2)}, u32[]{:S(2)}) collective-permute-start(f32[2,128,256]{2,1,0:T(8,128)S(1)} %get-tuple-element.82), channel_id=1, source_target_pairs={{0,2},{2,0},{4,6},{6,4},{8,10},{10,8},{12,14},{14,12},{16,18},{18,... | collective-permute-start | bytes 786440 | tf_op jit(solution)/shard_map/ppermute | solution.py:341
  13.7 15.6 %collective-permute-start.22 = (f32[2,128,256]{2,1,0:T(8,128)S(1)}, f32[2,128,256]{2,1,0:T(8,128)S(1)}, u32[]{:S(2)}, u32[]{:S(2)}) collective-permute-start(f32[2,128,256]{2,1,0:T(8,128)S(1)} %get-tuple-element.83), channel_id=1, source_target_pairs={{0,4},{2,6},{4,0},{6,2},{8,12},{10,14},{12,8},{14,10},{16,20},{18,... | collective-permute-start | bytes 786440 | tf_op jit(solution)/shard_map/ppermute | solution.py:341
  24.9 26.2 %collective-permute-start.19 = (f32[7,128,256]{2,1,0:T(8,128)}, f32[7,128,256]{2,1,0:T(8,128)S(1)}, u32[]{:S(2)}, u32[]{:S(2)}) collective-permute-start(f32[7,128,256]{2,1,0:T(8,128)} %collective-permute-done.18), channel_id=1, source_target_pairs={{8,0},{10,2},{12,4},{14,6},{16,24},{18,26},{20,28},{22,30},{9,1},{... | collective-permute-start | bytes 2752520 | tf_op jit(solution)/shard_map/ppermute | solution.py:332
  26.3 10.2 %collective-permute-start.23 = (f32[2,128,256]{2,1,0:T(8,128)S(1)}, f32[2,128,256]{2,1,0:T(8,128)S(1)}, u32[]{:S(2)}, u32[]{:S(2)}) collective-permute-start(f32[2,128,256]{2,1,0:T(8,128)S(1)} %get-tuple-element.84), channel_id=1, source_target_pairs={{0,6},{2,4},{4,2},{6,0},{8,14},{10,12},{12,10},{14,8},{16,22},{18,... | collective-permute-start | bytes 786440 | tf_op jit(solution)/shard_map/ppermute | solution.py:341
  27.8 12.3 %collective-permute-start.7 = (f32[2,128,256]{2,1,0:T(8,128)S(1)}, f32[2,128,256]{2,1,0:T(8,128)S(1)}, u32[]{:S(2)}, u32[]{:S(2)}) collective-permute-start(f32[2,128,256]{2,1,0:T(8,128)S(1)} %get-tuple-element.65), channel_id=1, source_target_pairs={{0,2},{2,0},{4,6},{6,4},{8,10},{10,8},{12,14},{14,12},{16,18},{18,... | collective-permute-start | bytes 786440 | tf_op jit(solution)/shard_map/ppermute | solution.py:341
  29.3 11.4 %collective-permute-start.8 = (f32[2,128,256]{2,1,0:T(8,128)S(1)}, f32[2,128,256]{2,1,0:T(8,128)S(1)}, u32[]{:S(2)}, u32[]{:S(2)}) collective-permute-start(f32[2,128,256]{2,1,0:T(8,128)S(1)} %get-tuple-element.66), channel_id=1, source_target_pairs={{0,4},{2,6},{4,0},{6,2},{8,12},{10,14},{12,8},{14,10},{16,20},{18,... | collective-permute-start | bytes 786440 | tf_op jit(solution)/shard_map/ppermute | solution.py:341
  36.5 27.8 %collective-permute-start.10 = (f32[7,128,256]{2,1,0:T(8,128)S(1)}, f32[7,128,256]{2,1,0:T(8,128)S(1)}, u32[]{:S(2)}, u32[]{:S(2)}) collective-permute-start(f32[7,128,256]{2,1,0:T(8,128)S(1)} %bitcast.8), channel_id=1, source_target_pairs={{0,1},{1,0},{2,3},{3,2},{4,5},{5,4},{6,7},{7,6},{8,9},{9,8},{10,11... | collective-permute-start | bytes 2752520 | tf_op jit(solution)/shard_map/ppermute | solution.py:335
  36.5 29.2 %collective-permute-start.4 = (f32[7,128,256]{2,1,0:T(8,128)S(1)}, f32[7,128,256]{2,1,0:T(8,128)S(1)}, u32[]{:S(2)}, u32[]{:S(2)}) collective-permute-start(f32[7,128,256]{2,1,0:T(8,128)S(1)} %collective-permute-done.3.refs_4_), channel_id=1, source_target_pairs={{8,16},{10,18},{12,20},{14,22},{16,8},{18,10},{20,12},{22,14},{9,1... | collective-permute-start | bytes 2752520 | tf_op jit(solution)/shard_map/ppermute | solution.py:332
  40.2 8.3 %collective-permute-start = (f32[2,128,256]{2,1,0:T(8,128)S(1)}, f32[2,128,256]{2,1,0:T(8,128)S(1)}, u32[]{:S(2)}, u32[]{:S(2)}) collective-permute-start(f32[2,128,256]{2,1,0:T(8,128)S(1)} %get-tuple-element.61), channel_id=1, source_target_pairs={{0,2},{2,0},{4,6},{6,4},{8,10},{10,8},{12,14},{14,12},{16,18},{18,... | collective-permute-start | bytes 786440 | tf_op jit(solution)/shard_map/ppermute | solution.py:341
  40.7 8.0 %collective-permute-start.1 = (f32[2,128,256]{2,1,0:T(8,128)S(1)}, f32[2,128,256]{2,1,0:T(8,128)S(1)}, u32[]{:S(2)}, u32[]{:S(2)}) collective-permute-start(f32[2,128,256]{2,1,0:T(8,128)S(1)} %get-tuple-element.62), channel_id=1, source_target_pairs={{0,4},{2,6},{4,0},{6,2},{8,12},{10,14},{12,8},{14,10},{16,20},{18,... | collective-permute-start | bytes 786440 | tf_op jit(solution)/shard_map/ppermute | solution.py:341
  48.5 26.8 %collective-permute-start.24 = (f32[7,128,256]{2,1,0:T(8,128)S(1)}, f32[7,128,256]{2,1,0:T(8,128)S(1)}, u32[]{:S(2)}, u32[]{:S(2)}) collective-permute-start(f32[7,128,256]{2,1,0:T(8,128)S(1)} %collective-permute-done.3.refs_4_), channel_id=1, source_target_pairs={{0,1},{1,0},{2,3},{3,2},{4,5},{5,4},{6,7},{7,6},{8,9},{9,8},{10,11... | collective-permute-start | bytes 2752520 | tf_op jit(solution)/shard_map/ppermute | solution.py:335
  48.7 10.1 %collective-permute-start.2 = (f32[2,128,256]{2,1,0:T(8,128)S(1)}, f32[2,128,256]{2,1,0:T(8,128)S(1)}, u32[]{:S(2)}, u32[]{:S(2)}) collective-permute-start(f32[2,128,256]{2,1,0:T(8,128)S(1)} %get-tuple-element.63), channel_id=1, source_target_pairs={{0,6},{2,4},{4,2},{6,0},{8,14},{10,12},{12,10},{14,8},{16,22},{18,... | collective-permute-start | bytes 786440 | tf_op jit(solution)/shard_map/ppermute | solution.py:341
  51.2 7.6 %copy-start.4 = (f32[2,128,256]{2,1,0:T(8,128)S(1)}, f32[2,128,256]{2,1,0:T(8,128)}, u32[]{:S(2)}) copy-start(f32[2,128,256]{2,1,0:T(8,128)} %get-tuple-element.60.refs_0_) | copy-start | bytes 786436
  51.2 12.5 %collective-permute-start.9 = (f32[2,128,256]{2,1,0:T(8,128)S(1)}, f32[2,128,256]{2,1,0:T(8,128)S(1)}, u32[]{:S(2)}, u32[]{:S(2)}) collective-permute-start(f32[2,128,256]{2,1,0:T(8,128)S(1)} %get-tuple-element.67), channel_id=1, source_target_pairs={{0,6},{2,4},{4,2},{6,0},{8,14},{10,12},{12,10},{14,8},{16,22},{18,... | collective-permute-start | bytes 786440 | tf_op jit(solution)/shard_map/ppermute | solution.py:341
  58.8 29.2 %collective-permute-start.20 = (f32[7,128,256]{2,1,0:T(8,128)S(1)}, f32[7,128,256]{2,1,0:T(8,128)S(1)}, u32[]{:S(2)}, u32[]{:S(2)}) collective-permute-start(f32[7,128,256]{2,1,0:T(8,128)S(1)} %add.33.refs_4_), channel_id=1, source_target_pairs={{0,1},{1,0},{2,3},{3,2},{4,5},{5,4},{6,7},{7,6},{8,9},{9,8},{10,11... | collective-permute-start | bytes 2752520 | tf_op jit(solution)/shard_map/ppermute | solution.py:335
  58.8 7.0 %copy-start.14 = (f32[2,128,256]{2,1,0:T(8,128)S(1)}, f32[2,128,256]{2,1,0:T(8,128)}, u32[]{:S(2)}) copy-start(f32[2,128,256]{2,1,0:T(8,128)} %get-tuple-element.64.refs_0_) | copy-start | bytes 786436
  63.7 10.0 %collective-permute-start.15 = (f32[2,128,256]{2,1,0:T(8,128)S(1)}, f32[2,128,256]{2,1,0:T(8,128)S(1)}, u32[]{:S(2)}, u32[]{:S(2)}) collective-permute-start(f32[2,128,256]{2,1,0:T(8,128)S(1)} %get-tuple-element.78), channel_id=1, source_target_pairs={{0,2},{2,0},{4,6},{6,4},{8,10},{10,8},{12,14},{14,12},{16,18},{18,... | collective-permute-start | bytes 786440 | tf_op jit(solution)/shard_map/ppermute | solution.py:341
  64.3 31.3 %collective-permute-start.6 = (f32[4,2,128,256]{3,2,1,0:T(8,128)S(1)}, f32[4,2,128,256]{3,2,1,0:T(8,128)S(1)}, u32[]{:S(2)}, u32[]{:S(2)}) collective-permute-start(f32[4,2,128,256]{3,2,1,0:T(8,128)S(1)} %pad_maximum_fusion), channel_id=1, source_target_pairs={{0,8},{2,10},{4,12},{6,14},{24,16},{26,18},{28,20},{30,22},{1,9},{... | collective-permute-start | bytes 3145736 | tf_op jit(solution)/shard_map/ppermute | solution.py:332
  65.7 29.9 %collective-permute-start.5 = (f32[7,128,256]{2,1,0:T(8,128)S(1)}, f32[7,128,256]{2,1,0:T(8,128)S(1)}, u32[]{:S(2)}, u32[]{:S(2)}) collective-permute-start(f32[7,128,256]{2,1,0:T(8,128)S(1)} %collective-permute-done.4.refs_4_), channel_id=1, source_target_pairs={{0,1},{1,0},{2,3},{3,2},{4,5},{5,4},{6,7},{7,6},{8,9},{9,8},{10,11... | collective-permute-start | bytes 2752520 | tf_op jit(solution)/shard_map/ppermute | solution.py:335
  65.8 10.8 %copy-start.13 = (f32[2,128,256]{2,1,0:T(8,128)S(1)}, f32[2,128,256]{2,1,0:T(8,128)}, u32[]{:S(2)}) copy-start(f32[2,128,256]{2,1,0:T(8,128)} %get-tuple-element.81.refs_0_) | copy-start | bytes 786436
  73.7 14.3 %collective-permute-start.16 = (f32[2,128,256]{2,1,0:T(8,128)S(1)}, f32[2,128,256]{2,1,0:T(8,128)S(1)}, u32[]{:S(2)}, u32[]{:S(2)}) collective-permute-start(f32[2,128,256]{2,1,0:T(8,128)S(1)} %get-tuple-element.79), channel_id=1, source_target_pairs={{0,4},{2,6},{4,0},{6,2},{8,12},{10,14},{12,8},{14,10},{16,20},{18,... | collective-permute-start | bytes 786440 | tf_op jit(solution)/shard_map/ppermute | solution.py:341
  75.2 12.8 %collective-permute-start.17 = (f32[2,128,256]{2,1,0:T(8,128)S(1)}, f32[2,128,256]{2,1,0:T(8,128)S(1)}, u32[]{:S(2)}, u32[]{:S(2)}) collective-permute-start(f32[2,128,256]{2,1,0:T(8,128)S(1)} %get-tuple-element.80), channel_id=1, source_target_pairs={{0,6},{2,4},{4,2},{6,0},{8,14},{10,12},{12,10},{14,8},{16,22},{18,... | collective-permute-start | bytes 786440 | tf_op jit(solution)/shard_map/ppermute | solution.py:341
  76.7 11.4 %copy-start.12 = (f32[2,128,256]{2,1,0:T(8,128)S(1)}, f32[2,128,256]{2,1,0:T(8,128)}, u32[]{:S(2)}) copy-start(f32[2,128,256]{2,1,0:T(8,128)} %get-tuple-element.77.refs_0_) | copy-start | bytes 786436
  88.0 23.3 %collective-permute-start.29 = (f32[7,128,256]{2,1,0:T(8,128)S(1)}, f32[7,128,256]{2,1,0:T(8,128)S(1)}, u32[]{:S(2)}, u32[]{:S(2)}) collective-permute-start(f32[7,128,256]{2,1,0:T(8,128)S(1)} %get-tuple-element.96), channel_id=1, source_target_pairs={{0,1},{1,0},{2,3},{3,2},{4,5},{5,4},{6,7},{7,6},{8,9},{9,8},{10,11... | collective-permute-start | bytes 2752520 | tf_op jit(solution)/shard_map/ppermute | solution.py:335
  94.9 28.3 %collective-permute-start.39 = (f32[3,128,256]{2,1,0:T(8,128)S(1)}, f32[3,128,256]{2,1,0:T(8,128)S(1)}, u32[]{:S(2)}, u32[]{:S(2)}) collective-permute-start(f32[3,128,256]{2,1,0:T(8,128)S(1)} %get-tuple-element.104), channel_id=1, source_target_pairs={{0,1},{1,0},{2,3},{3,2},{4,5},{5,4},{6,7},{7,6},{8,9},{9,8},{10,11... | collective-permute-start | bytes 1179656 | tf_op jit(solution)/shard_map/ppermute | solution.py:335
  95.5 17.4 %collective-permute-start.36 = (f32[2,128,256]{2,1,0:T(8,128)S(1)}, f32[2,128,256]{2,1,0:T(8,128)S(1)}, u32[]{:S(2)}, u32[]{:S(2)}) collective-permute-start(f32[2,128,256]{2,1,0:T(8,128)S(1)} %get-tuple-element.102), channel_id=1, source_target_pairs={{0,1},{1,0},{2,3},{3,2},{4,5},{5,4},{6,7},{7,6},{8,9},{9,8},{10,11... | collective-permute-start | bytes 786440 | tf_op jit(solution)/shard_map/ppermute | solution.py:335
  96.6 14.8 %copy-start.25 = (f32[2,128,256]{2,1,0:T(8,128)S(1)}, f32[2,128,256]{2,1,0:T(8,128)}, u32[]{:S(2)}) copy-start(f32[2,128,256]{2,1,0:T(8,128)} %get-tuple-element.90) | copy-start | bytes 786436
  110.8 26.5 %collective-permute-start.31 = (f32[7,128,256]{2,1,0:T(8,128)}, f32[7,128,256]{2,1,0:T(8,128)}, u32[]{:S(2)}, u32[]{:S(2)}) collective-permute-start(f32[7,128,256]{2,1,0:T(8,128)} %get-tuple-element.98), channel_id=1, source_target_pairs={{0,1},{1,0},{2,3},{3,2},{4,5},{5,4},{6,7},{7,6},{8,9},{9,8},{10,11... | collective-permute-start | bytes 2752520 | tf_op jit(solution)/shard_map/ppermute | solution.py:335
  111.3 7.8 %collective-permute-start.33 = (f32[2,128,256]{2,1,0:T(8,128)S(1)}, f32[2,128,256]{2,1,0:T(8,128)S(1)}, u32[]{:S(2)}, u32[]{:S(2)}) collective-permute-start(f32[2,128,256]{2,1,0:T(8,128)S(1)} %get-tuple-element.100), channel_id=1, source_target_pairs={{0,1},{1,0},{2,3},{3,2},{4,5},{5,4},{6,7},{7,6},{8,9},{9,8},{10,11... | collective-permute-start | bytes 786440 | tf_op jit(solution)/shard_map/ppermute | solution.py:335
  111.3 11.9 %copy-start.15 = (f32[7,128,256]{2,1,0:T(8,128)}, f32[7,128,256]{2,1,0:T(8,128)S(1)}, u32[]{:S(2)}) copy-start(f32[7,128,256]{2,1,0:T(8,128)S(1)} %collective-permute-done.29) | copy-start | bytes 2752516
  111.3 9.3 %collective-permute-start.25 = (f32[2,128,256]{2,1,0:T(8,128)S(1)}, f32[2,128,256]{2,1,0:T(8,128)S(1)}, u32[]{:S(2)}, u32[]{:S(2)}) collective-permute-start(f32[2,128,256]{2,1,0:T(8,128)S(1)} %copy-done.25), channel_id=1, source_target_pairs={{0,2},{2,0},{4,6},{6,4},{8,10},{10,8},{12,14},{14,12},{16,18},{18,... | collective-permute-start | bytes 786440 | tf_op jit(solution)/shard_map/ppermute | solution.py:341
  112.9 21.8 %collective-permute-start.11 = (f32[4,128,256]{2,1,0:T(8,128)}, f32[4,128,256]{2,1,0:T(8,128)}, u32[]{:S(2)}, u32[]{:S(2)}) collective-permute-start(f32[4,128,256]{2,1,0:T(8,128)} %get-tuple-element.73), channel_id=1, source_target_pairs={{8,0},{10,2},{12,4},{14,6},{16,24},{18,26},{20,28},{22,30},{9,1},{... | collective-permute-start | bytes 1572872 | tf_op jit(solution)/shard_map/ppermute | solution.py:332
  119.1 5.5 %copy-start.18 = (f32[2,128,256]{2,1,0:T(8,128)}, f32[2,128,256]{2,1,0:T(8,128)S(1)}, u32[]{:S(2)}) copy-start(f32[2,128,256]{2,1,0:T(8,128)S(1)} %collective-permute-done.33) | copy-start | bytes 786436
  119.1 14.0 %collective-permute-start.26 = (f32[2,128,256]{2,1,0:T(8,128)}, f32[2,128,256]{2,1,0:T(8,128)}, u32[]{:S(2)}, u32[]{:S(2)}) collective-permute-start(f32[2,128,256]{2,1,0:T(8,128)} %get-tuple-element.91), channel_id=1, source_target_pairs={{0,4},{2,6},{4,0},{6,2},{8,12},{10,14},{12,8},{14,10},{16,20},{18,... | collective-permute-start | bytes 786440 | tf_op jit(solution)/shard_map/ppermute | solution.py:341
  121.3 11.8 %collective-permute-start.27 = (f32[2,128,256]{2,1,0:T(8,128)}, f32[2,128,256]{2,1,0:T(8,128)}, u32[]{:S(2)}, u32[]{:S(2)}) collective-permute-start(f32[2,128,256]{2,1,0:T(8,128)} %get-tuple-element.92), channel_id=1, source_target_pairs={{0,6},{2,4},{4,2},{6,0},{8,14},{10,12},{12,10},{14,8},{16,22},{18,... | collective-permute-start | bytes 786440 | tf_op jit(solution)/shard_map/ppermute | solution.py:341
  123.2 1.3 copy-start.16
  123.2 10.2 %collective-permute-start.37 = (f32[2,128,256]{2,1,0:T(8,128)}, f32[2,128,256]{2,1,0:T(8,128)}, u32[]{:S(2)}, u32[]{:S(2)}) collective-permute-start(f32[2,128,256]{2,1,0:T(8,128)} %add.40), channel_id=1, source_target_pairs={{0,8},{2,10},{4,12},{6,14},{24,16},{26,18},{28,20},{30,22},{1,9},{... | collective-permute-start | bytes 786440 | tf_op jit(solution)/shard_map/ppermute | solution.py:332
  124.6 1.7 copy-start.19
  124.6 1.7 copy-start.17
  126.2 6.9 %copy-start.7 = (f32[7,128,256]{2,1,0:T(8,128)S(1)}, f32[7,128,256]{2,1,0:T(8,128)}, u32[]{:S(2)}) copy-start(f32[7,128,256]{2,1,0:T(8,128)} %copy-done.6) | copy-start | bytes 2752516
  126.3 9.7 %copy-start.20 = (f32[2,128,256]{2,1,0:T(8,128)S(1)}, f32[2,128,256]{2,1,0:T(8,128)}, u32[]{:S(2)}) copy-start(f32[2,128,256]{2,1,0:T(8,128)} %get-tuple-element.72) | copy-start | bytes 786436
  126.3 9.7 %copy-start.21 = (f32[2,128,256]{2,1,0:T(8,128)S(1)}, f32[2,128,256]{2,1,0:T(8,128)}, u32[]{:S(2)}) copy-start(f32[2,128,256]{2,1,0:T(8,128)} %get-tuple-element.74) | copy-start | bytes 786436
  126.3 9.7 %copy-start.22 = (f32[2,128,256]{2,1,0:T(8,128)S(1)}, f32[2,128,256]{2,1,0:T(8,128)}, u32[]{:S(2)}) copy-start(f32[2,128,256]{2,1,0:T(8,128)} %get-tuple-element.75) | copy-start | bytes 786436
  126.3 9.7 %copy-start.23 = (f32[2,128,256]{2,1,0:T(8,128)S(1)}, f32[2,128,256]{2,1,0:T(8,128)}, u32[]{:S(2)}) copy-start(f32[2,128,256]{2,1,0:T(8,128)} %get-tuple-element.76) | copy-start | bytes 786436
  133.1 52.7 %collective-permute-start.28 = (f32[7,128,256]{2,1,0:T(8,128)S(1)}, f32[7,128,256]{2,1,0:T(8,128)S(1)}, u32[]{:S(2)}, u32[]{:S(2)}) collective-permute-start(f32[7,128,256]{2,1,0:T(8,128)S(1)} %copy-done.7), channel_id=1, source_target_pairs={{0,1},{1,0},{2,3},{3,2},{4,5},{5,4},{6,7},{7,6},{8,9},{9,8},{10,11... | collective-permute-start | bytes 2752520 | tf_op jit(solution)/shard_map/ppermute | solution.py:335
  133.1 55.1 %collective-permute-start.30 = (f32[7,128,256]{2,1,0:T(8,128)S(1)}, f32[7,128,256]{2,1,0:T(8,128)S(1)}, u32[]{:S(2)}, u32[]{:S(2)}) collective-permute-start(f32[7,128,256]{2,1,0:T(8,128)S(1)} %add.35), channel_id=1, source_target_pairs={{0,8},{2,10},{4,12},{6,14},{8,0},{10,2},{12,4},{14,6},{16,24},{18,... | collective-permute-start | bytes 2752520 | tf_op jit(solution)/shard_map/ppermute | solution.py:332
  133.4 28.6 %collective-permute-start.34 = (f32[2,128,256]{2,1,0:T(8,128)S(1)}, f32[2,128,256]{2,1,0:T(8,128)S(1)}, u32[]{:S(2)}, u32[]{:S(2)}) collective-permute-start(f32[2,128,256]{2,1,0:T(8,128)S(1)} %add.38), channel_id=1, source_target_pairs={{0,8},{2,10},{4,12},{6,14},{24,16},{26,18},{28,20},{30,22},{1,9},{... | collective-permute-start | bytes 786440 | tf_op jit(solution)/shard_map/ppermute | solution.py:332
  134.7 35.2 %collective-permute-start.40 = (f32[3,128,256]{2,1,0:T(8,128)S(1)}, f32[3,128,256]{2,1,0:T(8,128)S(1)}, u32[]{:S(2)}, u32[]{:S(2)}) collective-permute-start(f32[3,128,256]{2,1,0:T(8,128)S(1)} %add.42), channel_id=1, source_target_pairs={{0,8},{2,10},{4,12},{6,14},{24,16},{26,18},{28,20},{30,22},{1,9},{... | collective-permute-start | bytes 1179656 | tf_op jit(solution)/shard_map/ppermute | solution.py:332
  137.3 34.2 %collective-permute-start.14 = (f32[2,128,256]{2,1,0:T(8,128)S(1)}, f32[2,128,256]{2,1,0:T(8,128)S(1)}, u32[]{:S(2)}, u32[]{:S(2)}) collective-permute-start(f32[2,128,256]{2,1,0:T(8,128)S(1)} %pad_maximum_fusion.4), channel_id=1, source_target_pairs={{0,6},{2,4},{4,2},{6,0},{8,14},{10,12},{12,10},{14,8},{16,22},{18,... | collective-permute-start | bytes 786440 | tf_op jit(solution)/shard_map/ppermute | solution.py:341
  162.0 38.1 %collective-permute-start.32 = (f32[7,128,256]{2,1,0:T(8,128)S(1)}, f32[7,128,256]{2,1,0:T(8,128)S(1)}, u32[]{:S(2)}, u32[]{:S(2)}) collective-permute-start(f32[7,128,256]{2,1,0:T(8,128)S(1)} %add.37), channel_id=1, source_target_pairs={{8,24},{10,26},{12,28},{14,30},{16,0},{18,2},{20,4},{22,6},{9,25},... | collective-permute-start | bytes 2752520 | tf_op jit(solution)/shard_map/ppermute | solution.py:332
  163.4 8.6 %copy-start.10 = (s32[1024,1]{1,0:T(8,128)S(1)}, s32[1024,1]{1,0:T(8,128)}, u32[]{:S(2)}) copy-start(s32[1024,1]{1,0:T(8,128)} %get-tuple-element.59.slot_ref) | copy-start | bytes 12292
  163.4 8.5 %copy-start.9 = (f32[2,128,256]{2,1,0:T(8,128)S(1)}, f32[2,128,256]{2,1,0:T(8,128)}, u32[]{:S(2)}) copy-start(f32[2,128,256]{2,1,0:T(8,128)} %copy-done.8) | copy-start | bytes 786436
  163.5 8.5 %copy-start.11 = (f32[2,128,256]{2,1,0:T(8,128)S(1)}, f32[2,128,256]{2,1,0:T(8,128)}, u32[]{:S(2)}) copy-start(f32[2,128,256]{2,1,0:T(8,128)} %get-tuple-element.89.refs_0_) | copy-start | bytes 786436
  169.9 7.8 %collective-permute-start.13 = (f32[2,128,256]{2,1,0:T(8,128)S(1)}, f32[2,128,256]{2,1,0:T(8,128)S(1)}, u32[]{:S(2)}, u32[]{:S(2)}) collective-permute-start(f32[2,128,256]{2,1,0:T(8,128)S(1)} %pad_maximum_fusion.3), channel_id=1, source_target_pairs={{0,4},{2,6},{4,0},{6,2},{8,12},{10,14},{12,8},{14,10},{16,20},{18,... | collective-permute-start | bytes 786440 | tf_op jit(solution)/shard_map/ppermute | solution.py:341
  171.4 8.6 %collective-permute-start.12 = (f32[2,128,256]{2,1,0:T(8,128)S(1)}, f32[2,128,256]{2,1,0:T(8,128)S(1)}, u32[]{:S(2)}, u32[]{:S(2)}) collective-permute-start(f32[2,128,256]{2,1,0:T(8,128)S(1)} %pad_maximum_fusion.2), channel_id=1, source_target_pairs={{0,2},{2,0},{4,6},{6,4},{8,10},{10,8},{12,14},{14,12},{16,18},{18,... | collective-permute-start | bytes 786440 | tf_op jit(solution)/shard_map/ppermute | solution.py:341
  177.7 24.1 %collective-permute-start.38 = (f32[2,128,256]{2,1,0:T(8,128)S(1)}, f32[2,128,256]{2,1,0:T(8,128)S(1)}, u32[]{:S(2)}, u32[]{:S(2)}) collective-permute-start(f32[2,128,256]{2,1,0:T(8,128)S(1)} %add.41), channel_id=1, source_target_pairs={{8,16},{10,18},{12,20},{14,22},{16,8},{18,10},{20,12},{22,14},{9,1... | collective-permute-start | bytes 786440 | tf_op jit(solution)/shard_map/ppermute | solution.py:332
  180.1 20.1 %collective-permute-start.41 = (f32[3,128,256]{2,1,0:T(8,128)S(1)}, f32[3,128,256]{2,1,0:T(8,128)S(1)}, u32[]{:S(2)}, u32[]{:S(2)}) collective-permute-start(f32[3,128,256]{2,1,0:T(8,128)S(1)} %add.43), channel_id=1, source_target_pairs={{8,16},{10,18},{12,20},{14,22},{16,8},{18,10},{20,12},{22,14},{9,1... | collective-permute-start | bytes 1179656 | tf_op jit(solution)/shard_map/ppermute | solution.py:332
  185.8 18.0 %collective-permute-start.35 = (f32[2,128,256]{2,1,0:T(8,128)S(1)}, f32[2,128,256]{2,1,0:T(8,128)S(1)}, u32[]{:S(2)}, u32[]{:S(2)}) collective-permute-start(f32[2,128,256]{2,1,0:T(8,128)S(1)} %add.39), channel_id=1, source_target_pairs={{8,16},{10,18},{12,20},{14,22},{16,8},{18,10},{20,12},{22,14},{9,1... | collective-permute-start | bytes 786440 | tf_op jit(solution)/shard_map/ppermute | solution.py:332
  188.2 12.0 %copy-start.1 = (f32[7,1,128,256]{3,2,1,0:T(8,128)S(1)}, f32[7,1,128,256]{3,2,1,0:T(8,128)}, u32[]{:S(2)}) copy-start(f32[7,1,128,256]{3,2,1,0:T(8,128)} %one_ref.5) | copy-start | bytes 2752516
  188.2 11.9 %copy-start.2 = (f32[7,1,128,256]{3,2,1,0:T(8,128)S(1)}, f32[7,1,128,256]{3,2,1,0:T(8,128)}, u32[]{:S(2)}) copy-start(f32[7,1,128,256]{3,2,1,0:T(8,128)} %two_ref.5) | copy-start | bytes 2752516
  (4 other events, 3.6 us)

commit v3 on v1

--- a/solution.py
+++ b/solution.py
@@ -293,7 +293,7 @@
 
 def chunks_of(layers, step):
     order = list(range(layers - 1, -1, -1))
-    first, second = layers - layers // 3 * 2, layers // 3
+    first, second = layers // 2, layers - 1 - layers // 2
     cut = [order[:first], order[first : first + second], order[first + second :]]
     return cut if step > 1 else [order]
 
@@ -376,7 +376,8 @@
     for value, c in zip(sums[2], cut_two):
         back = along(jnp.where(inner, one[min(c) : max(c) + 1], value), SIDES)
         p4.append(back)
-        mid.append(along(value + back, MIDDLE))
+        joined = value + back
+        mid.append(along(joined, MIDDLE))
     kept, sides, *late = lax.optimization_barrier((zero, p3, *p4))
     base = kept + jnp.where(inner, sides, jnp.concatenate(late[::-1], axis=0))
     updated = None

time: 226 us -> 234 us (1.035)
  starting transfers between devices: 68.7 us -> 71.5 us
  waiting for transfers between devices: 99.2 us -> 102 us
  other arithmetic: 3.94 us -> 6.39 us
    ppermute x18, waiting for transfers between devices: 32.5 us -> 42.7 us  [exchange(): lax.ppermute(values[mask], 'expert', [(e, e ^ mask) for e in range(groups)])]
    ppermute x17, waiting for transfers between devices: 65.1 us -> 57.2 us  [along(): return lax.ppermute(value, 'expert', plane_pairs(pairs))]
    ppermute x17, starting transfers between devices: 42.9 us -> 48.1 us  [along(): return lax.ppermute(value, 'expert', plane_pairs(pairs))]
  transfers between devices with their start and end apart: 47 -> 47, of which waited for: 17 -> 17; matrix products, arithmetic and copies ran while one was open for 2% -> 3% of each run, Pallas kernels for 21% -> 21%
where the time goes in v3:
time: 234 us; the launch traced here: 233 us
  waiting for transfers between devices  102 us (44%)
  starting transfers between devices  71.5 us (31%)
  Pallas kernels  49 us (21%)
  other arithmetic  6.39 us (3%)
  local copies, waits for them, and re-layouts  3.3 us (1%)
    ppermute x17, waiting for transfers between devices, along(): return lax.ppermute(value, 'expert', plane_pairs(pairs))  57.2 us
    ppermute x17, starting transfers between devices, along(): return lax.ppermute(value, 'expert', plane_pairs(pairs))  48.1 us
    ppermute x18, waiting for transfers between devices, exchange(): lax.ppermute(values[mask], 'expert', [(e, e ^ mask) for e in range(groups)])  42.7 us
    pallas_call x4, Pallas kernels, step_call(): pl.pallas_call(functools.partial(step_body, size, cap, layers, chunks, al...  30.7 us
    ppermute x18, starting transfers between devices, exchange(): lax.ppermute(values[mask], 'expert', [(e, e ^ mask) for e in range(groups)])  21.7 us
    pallas_call x2, Pallas kernels, pack(): pl.pallas_call(functools.partial(pack_body, size, cap, groups, steps, wit...  10.7 us
  transfers between devices with their start and end apart: 47, of which 17 were waited for; matrix products, arithmetic and copies ran while one was open for 3% of the time, Pallas kernels for 21%

profile of v3, /device:TPU:0, one launch (start us, length us, event | category | flops | bytes accessed | tf_op | source)
XLA Modules:
  0.0 233.5 jit_solution(17556235396944544352)
XLA Ops:
  0.6 3.1 %collective-permute-start.3 = (f32[7,128,256]{2,1,0:T(8,128)}, f32[7,128,256]{2,1,0:T(8,128)S(1)}, u32[]{:S(2)}, u32[]{:S(2)}) collective-permute-start(f32[7,128,256]{2,1,0:T(8,128)} %bitcast.2), channel_id=1, source_target_pairs={{0,8},{2,10},{4,12},{6,14},{8,0},{10,2},{12,4},{14,6},{16,24},{18,... | collective-permute-start | bytes 2752520 | tf_op jit(solution)/shard_map/ppermute | solution.py:313
  3.7 20.6 %collective-permute-done.3.refs_4_ = f32[7,128,256]{2,1,0:T(8,128)S(1)} collective-permute-done((f32[7,128,256]{2,1,0:T(8,128)}, f32[7,128,256]{2,1,0:T(8,128)S(1)}, u32[]{:S(2)}, u32[]{:S(2)}) %collective-permute-start.3) | collective-permute-done | bytes 917536 | tf_op jit(solution)/shard_map/ppermute | solution.py:313
  24.3 0.7 copy-done.3
  25.0 5.0 %pack.3 = (f32[2,128,256]{2,1,0:T(8,128)}, f32[2,128,256]{2,1,0:T(8,128)S(1)}, f32[2,128,256]{2,1,0:T(8,128)S(1)}, f32[2,128,256]{2,1,0:T(8,128)S(1)}, f32[2,128...) custom-call(s32[1,1024]{1,0:T(1,128)S(1)} %bitcast.6, ...), custom_call_target="tpu_custom_call" | custom-call | flops 2147483648 | bytes 3145728 | tf_op jit(solution)/shard_map/pack/pallas_call | solution.py:103
  30.0 1.7 collective-permute-start.5
  31.7 1.5 collective-permute-start.6
  33.5 1.6 collective-permute-start.22
  35.1 4.1 %collective-permute-done.5.refs_1_ = f32[2,128,256]{2,1,0:T(8,128)S(1)} collective-permute-done((f32[2,128,256]{2,1,0:T(8,128)S(1)}, f32[2,128,256]{2,1,0:T(8,128)S(1)}, u32[]{:S(2)}, u32[]{:S(2)}) %collective-permute-start.5) | collective-permute-done | bytes 262176 | tf_op jit(solution)/shard_map/ppermute | solution.py:322
  39.2 1.6 collective-permute-start.4
  40.8 4.9 %collective-permute-done.6.refs_2_ = f32[2,128,256]{2,1,0:T(8,128)S(1)} collective-permute-done((f32[2,128,256]{2,1,0:T(8,128)S(1)}, f32[2,128,256]{2,1,0:T(8,128)S(1)}, u32[]{:S(2)}, u32[]{:S(2)}) %collective-permute-start.6) | collective-permute-done | bytes 262176 | tf_op jit(solution)/shard_map/ppermute | solution.py:322
  45.7 0.9 copy-done.11
  46.7 7.8 %step.4 = (f32[2,128,256]{2,1,0:T(8,128)}, f32[2,128,256]{2,1,0:T(8,128)}, f32[2,128,256]{2,1,0:T(8,128)}, f32[2,128,256]{2,1,0:T(8,128)}, f32[7,128,256]{2,1,0:T(8,128)S(1)}, /*index=5*/f32[7,128,256]{2,1,0:T(8,128)}) custom-call(f32[2,128,256]{2,1,0:T(8,128)S(1)} %copy-done.11, f32[2,128,256]{2,1,0:T(8,128)S(1)} %collective-permute-done.5.refs_1_, ...), custom_call_target="tpu_custom_call" | custom-call | flops 4227858432 | bytes 5242880 | tf_op jit(solution)/shard_map/step/pallas_call | solution.py:262
  54.5 1.3 collective-permute-start.23
  55.8 0.6 collective-permute-start.14
  56.4 0.9 collective-permute-done.9
  57.3 2.6 %broadcast_select_fusion.1 = (f32[7,128,256]{2,1,0:T(8,128)}, f32[7,128,256]{2,1,0:T(8,128)}) fusion(f32[7,128,256]{2,1,0:T(8,128)} %collective-permute-done.4, pred[]{:T(512)S(6)} %and.4, f32[7,128,256]{2,1,0:T(8,128)S(1)} %get-tuple-element.77, f32[7,128,256]{2,1,0:T(8,128)} %collective-permute-done.9), kind=kLoop, calls=%fused_computation.3 | loop fusion | flops 458752 | bytes 4587521 | tf_op jit(solution)/shard_map/jit(_where)/select_n | solution.py:370
  59.9 21.8 %collective-permute-start.10 = (f32[7,128,256]{2,1,0:T(8,128)}, f32[7,128,256]{2,1,0:T(8,128)}, u32[]{:S(2)}, u32[]{:S(2)}) collective-permute-start(f32[7,128,256]{2,1,0:T(8,128)} %get-tuple-element.138), channel_id=1, source_target_pairs={{0,8},{2,10},{4,12},{6,14},{8,0},{10,2},{12,4},{14,6},{16,24},{18,... | collective-permute-start | bytes 2752520 | tf_op jit(solution)/shard_map/ppermute | solution.py:313
  81.9 5.7 %pack.2 = (f32[2,128,256]{2,1,0:T(8,128)}, f32[2,128,256]{2,1,0:T(8,128)S(1)}, f32[2,128,256]{2,1,0:T(8,128)S(1)}, f32[2,128,256]{2,1,0:T(8,128)S(1)}, f32[2,128...) custom-call(s32[1,1024]{1,0:T(1,128)S(1)} %bitcast.7, ...), custom_call_target="tpu_custom_call" | custom-call | flops 2147483648 | bytes 3145728 | tf_op jit(solution)/shard_map/pack/pallas_call | solution.py:103
  87.6 1.5 collective-permute-start.11
  89.1 1.5 collective-permute-start.12
  91.1 1.6 add.49.refs_4_
  92.7 4.1 %collective-permute-done.11.refs_1_ = f32[2,128,256]{2,1,0:T(8,128)S(1)} collective-permute-done((f32[2,128,256]{2,1,0:T(8,128)S(1)}, f32[2,128,256]{2,1,0:T(8,128)S(1)}, u32[]{:S(2)}, u32[]{:S(2)}) %collective-permute-start.11) | collective-permute-done | bytes 262176 | tf_op jit(solution)/shard_map/ppermute | solution.py:322
  96.8 4.4 %collective-permute-done.12.refs_2_ = f32[2,128,256]{2,1,0:T(8,128)S(1)} collective-permute-done((f32[2,128,256]{2,1,0:T(8,128)S(1)}, f32[2,128,256]{2,1,0:T(8,128)S(1)}, u32[]{:S(2)}, u32[]{:S(2)}) %collective-permute-start.12) | collective-permute-done | bytes 262176 | tf_op jit(solution)/shard_map/ppermute | solution.py:322
  101.2 8.3 %step.5 = (f32[2,128,256]{2,1,0:T(8,128)}, f32[2,128,256]{2,1,0:T(8,128)}, f32[2,128,256]{2,1,0:T(8,128)}, f32[2,128,256]{2,1,0:T(8,128)}, f32[7,128,256]{2,1,0:T(8,128)S(1)}, /*index=5*/f32[7,128,256]{2,1,0:T(8,128)S(1)}) custom-call(f32[2,128,256]{2,1,0:T(8,128)S(1)} %copy-done.9, f32[2,128,256]{2,1,0:T(8,128)S(1)} %collective-permute-done.11.refs_1_, ...), custom_call_target="tpu_custom_call" | custom-call | flops 4227858432 | bytes 5242880 | tf_op jit(solution)/shard_map/step/pallas_call | solution.py:262
  109.5 1.4 broadcast_select_fusion.refs_4_
  110.9 1.3 collective-permute-start.19
  112.2 0.8 collective-permute-start.20
  113.1 1.4 collective-permute-start.21
  114.5 5.7 %collective-permute-done.19.refs_1_ = f32[2,128,256]{2,1,0:T(8,128)S(1)} collective-permute-done((f32[2,128,256]{2,1,0:T(8,128)S(1)}, f32[2,128,256]{2,1,0:T(8,128)S(1)}, u32[]{:S(2)}, u32[]{:S(2)}) %collective-permute-start.19) | collective-permute-done | bytes 262176 | tf_op jit(solution)/shard_map/ppermute | solution.py:322
  120.2 1.2 collective-permute-start
  121.4 2.8 %collective-permute-done.20.refs_2_ = f32[2,128,256]{2,1,0:T(8,128)S(1)} collective-permute-done((f32[2,128,256]{2,1,0:T(8,128)S(1)}, f32[2,128,256]{2,1,0:T(8,128)S(1)}, u32[]{:S(2)}, u32[]{:S(2)}) %collective-permute-start.20) | collective-permute-done | bytes 262176 | tf_op jit(solution)/shard_map/ppermute | solution.py:322
  124.2 3.0 %collective-permute-start.1 = (f32[2,128,256]{2,1,0:T(8,128)S(1)}, f32[2,128,256]{2,1,0:T(8,128)S(1)}, u32[]{:S(2)}, u32[]{:S(2)}) collective-permute-start(f32[2,128,256]{2,1,0:T(8,128)S(1)} %get-tuple-element.71), channel_id=1, source_target_pairs={{0,4},{2,6},{4,0},{6,2},{8,12},{10,14},{12,8},{14,10},{16,20},{18,... | collective-permute-start | bytes 786440 | tf_op jit(solution)/shard_map/ppermute | solution.py:322
  127.2 1.2 collective-permute-start.2
  128.4 7.2 %step.7 = (f32[2,128,256]{2,1,0:T(8,128)}, f32[2,128,256]{2,1,0:T(8,128)}, f32[2,128,256]{2,1,0:T(8,128)}, f32[2,128,256]{2,1,0:T(8,128)}, f32[3,128,256]{2,1,0:...) custom-call(f32[2,128,256]{2,1,0:T(8,128)S(1)} %copy-done.10, ...), custom_call_target="tpu_custom_call", output_to_operand_aliasing={{0}: (6, {}), {1}: (7, {}), {2}: (8, {}), {3}: (9, {})} | custom-call | flops 4227858432 | bytes 5242880 | tf_op jit(solution)/shard_map/step/pallas_call | solution.py:262
  136.1 0.6 collective-permute-done.1.refs_2_
  136.7 0.7 collective-permute-done.2.refs_3_
  137.5 7.4 %step.6 = (f32[2,128,256]{2,1,0:T(8,128)}, f32[2,128,256]{2,1,0:T(8,128)}, f32[2,128,256]{2,1,0:T(8,128)}, f32[2,128,256]{2,1,0:T(8,128)}, f32[3,128,256]{2,1,0:...) custom-call(f32[2,128,256]{2,1,0:T(8,128)S(1)} %copy-done.8, ...), custom_call_target="tpu_custom_call", output_to_operand_aliasing={{0}: (6, {}), {1}: (7, {}), {2}: (8, {}), {3}: (9, {})} | custom-call | flops 4227858432 | bytes 5242880 | tf_op jit(solution)/shard_map/step/pallas_call | solution.py:262
  145.9 2.0 collective-permute-start.25
  147.9 2.0 collective-permute-start.26
  149.9 0.5 collective-permute-start.33
  150.5 1.3 collective-permute-done.33
  151.8 3.3 %collective-permute-done.25.refs_1_ = f32[2,128,256]{2,1,0:T(8,128)S(1)} collective-permute-done((f32[2,128,256]{2,1,0:T(8,128)S(1)}, f32[2,128,256]{2,1,0:T(8,128)S(1)}, u32[]{:S(2)}, u32[]{:S(2)}) %collective-permute-start.25) | collective-permute-done | bytes 262176 | tf_op jit(solution)/shard_map/ppermute | solution.py:322
  155.1 0.8 collective-permute-start.32
  155.9 5.8 %collective-permute-done.26.refs_2_ = f32[2,128,256]{2,1,0:T(8,128)S(1)} collective-permute-done((f32[2,128,256]{2,1,0:T(8,128)S(1)}, f32[2,128,256]{2,1,0:T(8,128)S(1)}, u32[]{:S(2)}, u32[]{:S(2)}) %collective-permute-start.26) | collective-permute-done | bytes 262176 | tf_op jit(solution)/shard_map/ppermute | solution.py:322
  161.7 3.0 %collective-permute-start.41 = (f32[3,128,256]{2,1,0:T(8,128)S(1)}, f32[3,128,256]{2,1,0:T(8,128)S(1)}, u32[]{:S(2)}, u32[]{:S(2)}) collective-permute-start(f32[3,128,256]{2,1,0:T(8,128)S(1)} %add.59), channel_id=1, source_target_pairs={{0,8},{2,10},{4,12},{6,14},{24,16},{26,18},{28,20},{30,22},{1,9},{... | collective-permute-start | bytes 1179656 | tf_op jit(solution)/shard_map/ppermute | solution.py:313
  165.0 4.1 %collective-permute-start.45 = (f32[3,128,256]{2,1,0:T(8,128)S(1)}, f32[3,128,256]{2,1,0:T(8,128)S(1)}, u32[]{:S(2)}, u32[]{:S(2)}) collective-permute-start(f32[3,128,256]{2,1,0:T(8,128)S(1)} %add.62), channel_id=1, source_target_pairs={{0,8},{2,10},{4,12},{6,14},{24,16},{26,18},{28,20},{30,22},{1,9},{... | collective-permute-start | bytes 1179656 | tf_op jit(solution)/shard_map/ppermute | solution.py:313
  169.1 0.7 collective-permute-start.43
  169.8 7.2 %collective-permute-done.34 = f32[1,128,256]{2,1,0:T(8,128)S(1)} collective-permute-done((f32[1,128,256]{2,1,0:T(8,128)S(1)}, f32[1,128,256]{2,1,0:T(8,128)S(1)}, u32[]{:S(2)}, u32[]{:S(2)}) %collective-permute-start.34) | collective-permute-done | bytes 131104 | tf_op jit(solution)/shard_map/ppermute | solution.py:313
  177.0 4.4 %collective-permute-start.37 = (f32[1,128,256]{2,1,0:T(8,128)S(1)}, f32[1,128,256]{2,1,0:T(8,128)S(1)}, u32[]{:S(2)}, u32[]{:S(2)}) collective-permute-start(f32[1,128,256]{2,1,0:T(8,128)S(1)} %add.56), channel_id=1, source_target_pairs={{0,8},{2,10},{4,12},{6,14},{24,16},{26,18},{28,20},{30,22},{1,9},{... | collective-permute-start | bytes 393224 | tf_op jit(solution)/shard_map/ppermute | solution.py:313
  181.4 6.3 %collective-permute-done.37 = f32[1,128,256]{2,1,0:T(8,128)S(1)} collective-permute-done((f32[1,128,256]{2,1,0:T(8,128)S(1)}, f32[1,128,256]{2,1,0:T(8,128)S(1)}, u32[]{:S(2)}, u32[]{:S(2)}) %collective-permute-start.37) | collective-permute-done | bytes 131104 | tf_op jit(solution)/shard_map/ppermute | solution.py:313
  187.7 1.7 collective-permute-start.17
  189.6 0.9 copy-done.5
  190.6 1.3 unpack.2.refs_4_
  192.1 0.7 collective-permute-start.35
  192.9 0.8 collective-permute-start.39
  193.7 1.3 collective-permute-start.38
  195.0 6.2 %collective-permute-done.17.refs_2_ = f32[2,128,256]{2,1,0:T(8,128)S(1)} collective-permute-done((f32[2,128,256]{2,1,0:T(8,128)S(1)}, f32[2,128,256]{2,1,0:T(8,128)S(1)}, u32[]{:S(2)}, u32[]{:S(2)}) %collective-permute-start.17) | collective-permute-done | bytes 262176 | tf_op jit(solution)/shard_map/ppermute | solution.py:322
  201.2 1.3 collective-permute-start.42
  202.5 1.3 collective-permute-start.46
  204.0 2.3 unpack.3
  206.3 23.1 %collective-permute-done.46.far_ref = f32[3,128,256]{2,1,0:T(8,128)S(1)} collective-permute-done((f32[3,128,256]{2,1,0:T(8,128)S(1)}, f32[3,128,256]{2,1,0:T(8,128)S(1)}, u32[]{:S(2)}, u32[]{:S(2)}) %collective-permute-start.46) | collective-permute-done | bytes 393248 | tf_op jit(solution)/shard_map/ppermute | solution.py:313
  229.4 1.6 adam.3
  231.0 1.6 adam.4
  232.7 0.8 adam.5
  (96 shorter events, 3.6 us)
Async XLA Ops:
  0.6 23.7 %collective-permute-start.3 = (f32[7,128,256]{2,1,0:T(8,128)}, f32[7,128,256]{2,1,0:T(8,128)S(1)}, u32[]{:S(2)}, u32[]{:S(2)}) collective-permute-start(f32[7,128,256]{2,1,0:T(8,128)} %bitcast.2), channel_id=1, source_target_pairs={{0,8},{2,10},{4,12},{6,14},{8,0},{10,2},{12,4},{14,6},{16,24},{18,... | collective-permute-start | bytes 2752520 | tf_op jit(solution)/shard_map/ppermute | solution.py:313
  24.3 21.4 %collective-permute-start.8 = (f32[7,128,256]{2,1,0:T(8,128)S(1)}, f32[7,128,256]{2,1,0:T(8,128)S(1)}, u32[]{:S(2)}, u32[]{:S(2)}) collective-permute-start(f32[7,128,256]{2,1,0:T(8,128)S(1)} %collective-permute-done.3.refs_4_), channel_id=1, source_target_pairs={{0,1},{1,0},{2,3},{3,2},{4,5},{5,4},{6,7},{7,6},{8,9},{9,8},{10,11... | collective-permute-start | bytes 2752520 | tf_op jit(solution)/shard_map/ppermute | solution.py:316
  25.0 8.5 %copy-start = (f32[7,1,128,256]{3,2,1,0:T(8,128)S(1)}, f32[7,1,128,256]{3,2,1,0:T(8,128)}, u32[]{:S(2)}) copy-start(f32[7,1,128,256]{3,2,1,0:T(8,128)} %w_ref.5) | copy-start | bytes 2752516
  30.0 9.2 %collective-permute-start.5 = (f32[2,128,256]{2,1,0:T(8,128)S(1)}, f32[2,128,256]{2,1,0:T(8,128)S(1)}, u32[]{:S(2)}, u32[]{:S(2)}) collective-permute-start(f32[2,128,256]{2,1,0:T(8,128)S(1)} %get-tuple-element.74), channel_id=1, source_target_pairs={{0,2},{2,0},{4,6},{6,4},{8,10},{10,8},{12,14},{14,12},{16,18},{18,... | collective-permute-start | bytes 786440 | tf_op jit(solution)/shard_map/ppermute | solution.py:322
  31.7 14.1 %collective-permute-start.6 = (f32[2,128,256]{2,1,0:T(8,128)S(1)}, f32[2,128,256]{2,1,0:T(8,128)S(1)}, u32[]{:S(2)}, u32[]{:S(2)}) collective-permute-start(f32[2,128,256]{2,1,0:T(8,128)S(1)} %get-tuple-element.75), channel_id=1, source_target_pairs={{0,4},{2,6},{4,0},{6,2},{8,12},{10,14},{12,8},{14,10},{16,20},{18,... | collective-permute-start | bytes 786440 | tf_op jit(solution)/shard_map/ppermute | solution.py:322
  33.2 12.5 %collective-permute-start.7 = (f32[2,128,256]{2,1,0:T(8,128)S(1)}, f32[2,128,256]{2,1,0:T(8,128)S(1)}, u32[]{:S(2)}, u32[]{:S(2)}) collective-permute-start(f32[2,128,256]{2,1,0:T(8,128)S(1)} %get-tuple-element.76), channel_id=1, source_target_pairs={{0,6},{2,4},{4,2},{6,0},{8,14},{10,12},{12,10},{14,8},{16,22},{18,... | collective-permute-start | bytes 786440 | tf_op jit(solution)/shard_map/ppermute | solution.py:322
  33.5 21.0 %collective-permute-start.22 = (f32[7,128,256]{2,1,0:T(8,128)S(1)}, f32[7,128,256]{2,1,0:T(8,128)}, u32[]{:S(2)}, u32[]{:S(2)}) collective-permute-start(f32[7,128,256]{2,1,0:T(8,128)S(1)} %bitcast.3), channel_id=1, source_target_pairs={{8,16},{10,18},{12,20},{14,22},{16,8},{18,10},{20,12},{22,14},{9,1... | collective-permute-start | bytes 2752520 | tf_op jit(solution)/shard_map/ppermute | solution.py:313
  39.2 17.2 %collective-permute-start.4 = (f32[7,128,256]{2,1,0:T(8,128)S(1)}, f32[7,128,256]{2,1,0:T(8,128)}, u32[]{:S(2)}, u32[]{:S(2)}) collective-permute-start(f32[7,128,256]{2,1,0:T(8,128)S(1)} %collective-permute-done.3.refs_4_), channel_id=1, source_target_pairs={{8,16},{10,18},{12,20},{14,22},{16,8},{18,10},{20,12},{22,14},{9,1... | collective-permute-start | bytes 2752520 | tf_op jit(solution)/shard_map/ppermute | solution.py:313
  45.7 1.0 copy-start.11
  54.5 2.8 %collective-permute-start.9 = (f32[7,128,256]{2,1,0:T(8,128)}, f32[7,128,256]{2,1,0:T(8,128)}, u32[]{:S(2)}, u32[]{:S(2)}) collective-permute-start(f32[7,128,256]{2,1,0:T(8,128)} %get-tuple-element.78), channel_id=1, source_target_pairs={{0,1},{1,0},{2,3},{3,2},{4,5},{5,4},{6,7},{7,6},{8,9},{9,8},{10,11... | collective-permute-start | bytes 2752520 | tf_op jit(solution)/shard_map/ppermute | solution.py:316
  54.5 36.1 %collective-permute-start.23 = (f32[7,128,256]{2,1,0:T(8,128)}, f32[7,128,256]{2,1,0:T(8,128)}, u32[]{:S(2)}, u32[]{:S(2)}) collective-permute-start(f32[7,128,256]{2,1,0:T(8,128)} %collective-permute-done.22), channel_id=1, source_target_pairs={{8,0},{10,2},{12,4},{14,6},{16,24},{18,26},{20,28},{22,30},{9,1},{... | collective-permute-start | bytes 2752520 | tf_op jit(solution)/shard_map/ppermute | solution.py:313
  55.8 45.4 %collective-permute-start.14 = (f32[7,128,256]{2,1,0:T(8,128)S(1)}, f32[7,128,256]{2,1,0:T(8,128)}, u32[]{:S(2)}, u32[]{:S(2)}) collective-permute-start(f32[7,128,256]{2,1,0:T(8,128)S(1)} %bitcast.4), channel_id=1, source_target_pairs={{0,1},{1,0},{2,3},{3,2},{4,5},{5,4},{6,7},{7,6},{8,9},{9,8},{10,11... | collective-permute-start | bytes 2752520 | tf_op jit(solution)/shard_map/ppermute | solution.py:316
  57.3 24.4 %copy-start.4 = (s32[1024,1]{0,1:T(1,128)S(1)}, s32[1024,1]{0,1:T(1,128)}, u32[]{:S(2)}) copy-start(s32[1024,1]{0,1:T(1,128)} %param.7) | copy-start | bytes 12292
  59.9 49.5 %collective-permute-start.10 = (f32[7,128,256]{2,1,0:T(8,128)}, f32[7,128,256]{2,1,0:T(8,128)}, u32[]{:S(2)}, u32[]{:S(2)}) collective-permute-start(f32[7,128,256]{2,1,0:T(8,128)} %get-tuple-element.138), channel_id=1, source_target_pairs={{0,8},{2,10},{4,12},{6,14},{8,0},{10,2},{12,4},{14,6},{16,24},{18,... | collective-permute-start | bytes 2752520 | tf_op jit(solution)/shard_map/ppermute | solution.py:313
  87.6 9.2 %collective-permute-start.11 = (f32[2,128,256]{2,1,0:T(8,128)S(1)}, f32[2,128,256]{2,1,0:T(8,128)S(1)}, u32[]{:S(2)}, u32[]{:S(2)}) collective-permute-start(f32[2,128,256]{2,1,0:T(8,128)S(1)} %get-tuple-element.80), channel_id=1, source_target_pairs={{0,2},{2,0},{4,6},{6,4},{8,10},{10,8},{12,14},{14,12},{16,18},{18,... | collective-permute-start | bytes 786440 | tf_op jit(solution)/shard_map/ppermute | solution.py:322
  89.1 12.1 %collective-permute-start.12 = (f32[2,128,256]{2,1,0:T(8,128)S(1)}, f32[2,128,256]{2,1,0:T(8,128)S(1)}, u32[]{:S(2)}, u32[]{:S(2)}) collective-permute-start(f32[2,128,256]{2,1,0:T(8,128)S(1)} %get-tuple-element.81), channel_id=1, source_target_pairs={{0,4},{2,6},{4,0},{6,2},{8,12},{10,14},{12,8},{14,10},{16,20},{18,... | collective-permute-start | bytes 786440 | tf_op jit(solution)/shard_map/ppermute | solution.py:322
  90.6 10.6 %copy-start.9 = (f32[2,128,256]{2,1,0:T(8,128)S(1)}, f32[2,128,256]{2,1,0:T(8,128)}, u32[]{:S(2)}) copy-start(f32[2,128,256]{2,1,0:T(8,128)} %get-tuple-element.79.refs_0_) | copy-start | bytes 786436
  90.6 10.5 %collective-permute-start.13 = (f32[2,128,256]{2,1,0:T(8,128)S(1)}, f32[2,128,256]{2,1,0:T(8,128)S(1)}, u32[]{:S(2)}, u32[]{:S(2)}) collective-permute-start(f32[2,128,256]{2,1,0:T(8,128)S(1)} %get-tuple-element.82), channel_id=1, source_target_pairs={{0,6},{2,4},{4,2},{6,0},{8,14},{10,12},{12,10},{14,8},{16,22},{18,... | collective-permute-start | bytes 786440 | tf_op jit(solution)/shard_map/ppermute | solution.py:322
  96.8 31.6 %collective-permute-start.24 = (f32[7,128,256]{2,1,0:T(8,128)S(1)}, f32[7,128,256]{2,1,0:T(8,128)S(1)}, u32[]{:S(2)}, u32[]{:S(2)}) collective-permute-start(f32[7,128,256]{2,1,0:T(8,128)S(1)} %add.49.refs_4_), channel_id=1, source_target_pairs={{0,1},{1,0},{2,3},{3,2},{4,5},{5,4},{6,7},{7,6},{8,9},{9,8},{10,11... | collective-permute-start | bytes 2752520 | tf_op jit(solution)/shard_map/ppermute | solution.py:316
  109.5 19.0 %copy-start.10 = (f32[2,128,256]{2,1,0:T(8,128)S(1)}, f32[2,128,256]{2,1,0:T(8,128)}, u32[]{:S(2)}) copy-start(f32[2,128,256]{2,1,0:T(8,128)} %get-tuple-element.92.refs_0_) | copy-start | bytes 786436
  110.8 26.6 %collective-permute-start.15 = (f32[7,128,256]{2,1,0:T(8,128)S(1)}, f32[7,128,256]{2,1,0:T(8,128)S(1)}, u32[]{:S(2)}, u32[]{:S(2)}) collective-permute-start(f32[7,128,256]{2,1,0:T(8,128)S(1)} %broadcast_select_fusion.refs_4_), channel_id=1, source_target_pairs={{0,1},{1,0},{2,3},{3,2},{4,5},{5,4},{6,7},{7,6},{8,9},{9,8},{10,11... | collective-permute-start | bytes 2752520 | tf_op jit(solution)/shard_map/ppermute | solution.py:316
  110.9 9.2 %collective-permute-start.19 = (f32[2,128,256]{2,1,0:T(8,128)S(1)}, f32[2,128,256]{2,1,0:T(8,128)S(1)}, u32[]{:S(2)}, u32[]{:S(2)}) collective-permute-start(f32[2,128,256]{2,1,0:T(8,128)S(1)} %get-tuple-element.93), channel_id=1, source_target_pairs={{0,2},{2,0},{4,6},{6,4},{8,10},{10,8},{12,14},{14,12},{16,18},{18,... | collective-permute-start | bytes 786440 | tf_op jit(solution)/shard_map/ppermute | solution.py:322
  112.2 12.0 %collective-permute-start.20 = (f32[2,128,256]{2,1,0:T(8,128)S(1)}, f32[2,128,256]{2,1,0:T(8,128)S(1)}, u32[]{:S(2)}, u32[]{:S(2)}) collective-permute-start(f32[2,128,256]{2,1,0:T(8,128)S(1)} %get-tuple-element.94), channel_id=1, source_target_pairs={{0,4},{2,6},{4,0},{6,2},{8,12},{10,14},{12,8},{14,10},{16,20},{18,... | collective-permute-start | bytes 786440 | tf_op jit(solution)/shard_map/ppermute | solution.py:322
  113.1 14.2 %collective-permute-start.21 = (f32[2,128,256]{2,1,0:T(8,128)S(1)}, f32[2,128,256]{2,1,0:T(8,128)S(1)}, u32[]{:S(2)}, u32[]{:S(2)}) collective-permute-start(f32[2,128,256]{2,1,0:T(8,128)S(1)} %get-tuple-element.95), channel_id=1, source_target_pairs={{0,6},{2,4},{4,2},{6,0},{8,14},{10,12},{12,10},{14,8},{16,22},{18,... | collective-permute-start | bytes 786440 | tf_op jit(solution)/shard_map/ppermute | solution.py:322
  120.2 15.5 %collective-permute-start = (f32[2,128,256]{2,1,0:T(8,128)S(1)}, f32[2,128,256]{2,1,0:T(8,128)S(1)}, u32[]{:S(2)}, u32[]{:S(2)}) collective-permute-start(f32[2,128,256]{2,1,0:T(8,128)S(1)} %get-tuple-element.70), channel_id=1, source_target_pairs={{0,2},{2,0},{4,6},{6,4},{8,10},{10,8},{12,14},{14,12},{16,18},{18,... | collective-permute-start | bytes 786440 | tf_op jit(solution)/shard_map/ppermute | solution.py:322
  124.2 12.5 %collective-permute-start.1 = (f32[2,128,256]{2,1,0:T(8,128)S(1)}, f32[2,128,256]{2,1,0:T(8,128)S(1)}, u32[]{:S(2)}, u32[]{:S(2)}) collective-permute-start(f32[2,128,256]{2,1,0:T(8,128)S(1)} %get-tuple-element.71), channel_id=1, source_target_pairs={{0,4},{2,6},{4,0},{6,2},{8,12},{10,14},{12,8},{14,10},{16,20},{18,... | collective-permute-start | bytes 786440 | tf_op jit(solution)/shard_map/ppermute | solution.py:322
  127.2 10.3 %collective-permute-start.2 = (f32[2,128,256]{2,1,0:T(8,128)S(1)}, f32[2,128,256]{2,1,0:T(8,128)S(1)}, u32[]{:S(2)}, u32[]{:S(2)}) collective-permute-start(f32[2,128,256]{2,1,0:T(8,128)S(1)} %get-tuple-element.72), channel_id=1, source_target_pairs={{0,6},{2,4},{4,2},{6,0},{8,14},{10,12},{12,10},{14,8},{16,22},{18,... | collective-permute-start | bytes 786440 | tf_op jit(solution)/shard_map/ppermute | solution.py:322
  128.4 21.5 %collective-permute-start.28 = (f32[7,128,256]{2,1,0:T(8,128)S(1)}, f32[7,128,256]{2,1,0:T(8,128)S(1)}, u32[]{:S(2)}, u32[]{:S(2)}) collective-permute-start(f32[7,128,256]{2,1,0:T(8,128)S(1)} %get-tuple-element.105), channel_id=1, source_target_pairs={{0,1},{1,0},{2,3},{3,2},{4,5},{5,4},{6,7},{7,6},{8,9},{9,8},{10,11... | collective-permute-start | bytes 2752520 | tf_op jit(solution)/shard_map/ppermute | solution.py:316
  128.4 9.1 %copy-start.8 = (f32[2,128,256]{2,1,0:T(8,128)S(1)}, f32[2,128,256]{2,1,0:T(8,128)}, u32[]{:S(2)}) copy-start(f32[2,128,256]{2,1,0:T(8,128)} %get-tuple-element.69.refs_0_) | copy-start | bytes 786436
  135.7 9.3 %collective-permute-start.29 = (f32[3,128,256]{2,1,0:T(8,128)S(1)}, f32[3,128,256]{2,1,0:T(8,128)S(1)}, u32[]{:S(2)}, u32[]{:S(2)}) collective-permute-start(f32[3,128,256]{2,1,0:T(8,128)S(1)} %get-tuple-element.107), channel_id=1, source_target_pairs={{0,1},{1,0},{2,3},{3,2},{4,5},{5,4},{6,7},{7,6},{8,9},{9,8},{10,11... | collective-permute-start | bytes 1179656 | tf_op jit(solution)/shard_map/ppermute | solution.py:316
  136.7 8.2 %collective-permute-start.31 = (f32[3,128,256]{2,1,0:T(8,128)S(1)}, f32[3,128,256]{2,1,0:T(8,128)S(1)}, u32[]{:S(2)}, u32[]{:S(2)}) collective-permute-start(f32[3,128,256]{2,1,0:T(8,128)S(1)} %get-tuple-element.109), channel_id=1, source_target_pairs={{0,1},{1,0},{2,3},{3,2},{4,5},{5,4},{6,7},{7,6},{8,9},{9,8},{10,11... | collective-permute-start | bytes 1179656 | tf_op jit(solution)/shard_map/ppermute | solution.py:316
  137.5 7.4 %copy-start.12 = (f32[7,128,256]{2,1,0:T(8,128)S(1)}, f32[7,128,256]{2,1,0:T(8,128)}, u32[]{:S(2)}) copy-start(f32[7,128,256]{2,1,0:T(8,128)} %get-tuple-element.139) | copy-start | bytes 2752516
  144.9 5.0 %collective-permute-start.40 = (f32[3,128,256]{2,1,0:T(8,128)S(1)}, f32[3,128,256]{2,1,0:T(8,128)S(1)}, u32[]{:S(2)}, u32[]{:S(2)}) collective-permute-start(f32[3,128,256]{2,1,0:T(8,128)S(1)} %get-tuple-element.120), channel_id=1, source_target_pairs={{0,1},{1,0},{2,3},{3,2},{4,5},{5,4},{6,7},{7,6},{8,9},{9,8},{10,11... | collective-permute-start | bytes 1179656 | tf_op jit(solution)/shard_map/ppermute | solution.py:316
  144.9 2.9 %copy-start.14 = (f32[2,128,256]{2,1,0:T(8,128)S(1)}, f32[2,128,256]{2,1,0:T(8,128)}, u32[]{:S(2)}) copy-start(f32[2,128,256]{2,1,0:T(8,128)} %get-tuple-element.102) | copy-start | bytes 786436
  145.1 16.6 %collective-permute-start.30 = (f32[3,128,256]{2,1,0:T(8,128)S(1)}, f32[3,128,256]{2,1,0:T(8,128)S(1)}, u32[]{:S(2)}, u32[]{:S(2)}) collective-permute-start(f32[3,128,256]{2,1,0:T(8,128)S(1)} %get-tuple-element.140), channel_id=1, source_target_pairs={{0,8},{2,10},{4,12},{6,14},{8,0},{10,2},{12,4},{14,6},{16,24},{18,... | collective-permute-start | bytes 1179656 | tf_op jit(solution)/shard_map/ppermute | solution.py:313
  145.9 9.2 %collective-permute-start.25 = (f32[2,128,256]{2,1,0:T(8,128)S(1)}, f32[2,128,256]{2,1,0:T(8,128)S(1)}, u32[]{:S(2)}, u32[]{:S(2)}) collective-permute-start(f32[2,128,256]{2,1,0:T(8,128)S(1)} %copy-done.13), channel_id=1, source_target_pairs={{0,2},{2,0},{4,6},{6,4},{8,10},{10,8},{12,14},{14,12},{16,18},{18,... | collective-permute-start | bytes 786440 | tf_op jit(solution)/shard_map/ppermute | solution.py:322
  147.9 13.8 %collective-permute-start.26 = (f32[2,128,256]{2,1,0:T(8,128)S(1)}, f32[2,128,256]{2,1,0:T(8,128)S(1)}, u32[]{:S(2)}, u32[]{:S(2)}) collective-permute-start(f32[2,128,256]{2,1,0:T(8,128)S(1)} %copy-done.14), channel_id=1, source_target_pairs={{0,4},{2,6},{4,0},{6,2},{8,12},{10,14},{12,8},{14,10},{16,20},{18,... | collective-permute-start | bytes 786440 | tf_op jit(solution)/shard_map/ppermute | solution.py:322
  149.9 14.8 %collective-permute-start.44 = (f32[3,128,256]{2,1,0:T(8,128)S(1)}, f32[3,128,256]{2,1,0:T(8,128)S(1)}, u32[]{:S(2)}, u32[]{:S(2)}) collective-permute-start(f32[3,128,256]{2,1,0:T(8,128)S(1)} %get-tuple-element.122), channel_id=1, source_target_pairs={{0,1},{1,0},{2,3},{3,2},{4,5},{5,4},{6,7},{7,6},{8,9},{9,8},{10,11... | collective-permute-start | bytes 1179656 | tf_op jit(solution)/shard_map/ppermute | solution.py:316
  149.9 1.9 collective-permute-start.33
  150.4 1.4 copy-start.15
  151.8 17.3 %collective-permute-start.27 = (f32[2,128,256]{2,1,0:T(8,128)S(1)}, f32[2,128,256]{2,1,0:T(8,128)S(1)}, u32[]{:S(2)}, u32[]{:S(2)}) collective-permute-start(f32[2,128,256]{2,1,0:T(8,128)S(1)} %copy-done.15), channel_id=1, source_target_pairs={{0,6},{2,4},{4,2},{6,0},{8,14},{10,12},{12,10},{14,8},{16,22},{18,... | collective-permute-start | bytes 786440 | tf_op jit(solution)/shard_map/ppermute | solution.py:322
  155.1 26.3 %collective-permute-start.32 = (f32[3,128,256]{2,1,0:T(8,128)S(1)}, f32[3,128,256]{2,1,0:T(8,128)S(1)}, u32[]{:S(2)}, u32[]{:S(2)}) collective-permute-start(f32[3,128,256]{2,1,0:T(8,128)S(1)} %get-tuple-element.134), channel_id=1, source_target_pairs={{0,8},{2,10},{4,12},{6,14},{8,0},{10,2},{12,4},{14,6},{16,24},{18,... | collective-permute-start | bytes 1179656 | tf_op jit(solution)/shard_map/ppermute | solution.py:313
  161.7 3.3 %collective-permute-start.36 = (f32[1,128,256]{2,1,0:T(8,128)S(1)}, f32[1,128,256]{2,1,0:T(8,128)S(1)}, u32[]{:S(2)}, u32[]{:S(2)}) collective-permute-start(f32[1,128,256]{2,1,0:T(8,128)S(1)} %get-tuple-element.118), channel_id=1, source_target_pairs={{0,1},{1,0},{2,3},{3,2},{4,5},{5,4},{6,7},{7,6},{8,9},{9,8},{10,11... | collective-permute-start | bytes 393224 | tf_op jit(solution)/shard_map/ppermute | solution.py:316
  161.7 27.8 %collective-permute-start.41 = (f32[3,128,256]{2,1,0:T(8,128)S(1)}, f32[3,128,256]{2,1,0:T(8,128)S(1)}, u32[]{:S(2)}, u32[]{:S(2)}) collective-permute-start(f32[3,128,256]{2,1,0:T(8,128)S(1)} %add.59), channel_id=1, source_target_pairs={{0,8},{2,10},{4,12},{6,14},{24,16},{26,18},{28,20},{30,22},{1,9},{... | collective-permute-start | bytes 1179656 | tf_op jit(solution)/shard_map/ppermute | solution.py:313
  164.7 12.2 %collective-permute-start.34 = (f32[1,128,256]{2,1,0:T(8,128)S(1)}, f32[1,128,256]{2,1,0:T(8,128)S(1)}, u32[]{:S(2)}, u32[]{:S(2)}) collective-permute-start(f32[1,128,256]{2,1,0:T(8,128)S(1)} %get-tuple-element.132), channel_id=1, source_target_pairs={{0,8},{2,10},{4,12},{6,14},{8,0},{10,2},{12,4},{14,6},{16,24},{18,... | collective-permute-start | bytes 393224 | tf_op jit(solution)/shard_map/ppermute | solution.py:313
  164.9 22.9 %copy-start.17 = (f32[2,128,256]{2,1,0:T(8,128)S(1)}, f32[2,128,256]{2,1,0:T(8,128)}, u32[]{:S(2)}) copy-start(f32[2,128,256]{2,1,0:T(8,128)} %get-tuple-element.90) | copy-start | bytes 786436
  164.9 24.6 %copy-start.18 = (f32[2,128,256]{2,1,0:T(8,128)S(1)}, f32[2,128,256]{2,1,0:T(8,128)}, u32[]{:S(2)}) copy-start(f32[2,128,256]{2,1,0:T(8,128)} %get-tuple-element.91) | copy-start | bytes 786436
  164.9 16.4 %copy-start.16 = (f32[2,128,256]{2,1,0:T(8,128)S(1)}, f32[2,128,256]{2,1,0:T(8,128)}, u32[]{:S(2)}) copy-start(f32[2,128,256]{2,1,0:T(8,128)} %get-tuple-element.89) | copy-start | bytes 786436
  165.0 27.1 %collective-permute-start.45 = (f32[3,128,256]{2,1,0:T(8,128)S(1)}, f32[3,128,256]{2,1,0:T(8,128)S(1)}, u32[]{:S(2)}, u32[]{:S(2)}) collective-permute-start(f32[3,128,256]{2,1,0:T(8,128)S(1)} %add.62), channel_id=1, source_target_pairs={{0,8},{2,10},{4,12},{6,14},{24,16},{26,18},{28,20},{30,22},{1,9},{... | collective-permute-start | bytes 1179656 | tf_op jit(solution)/shard_map/ppermute | solution.py:313
  169.1 23.8 %collective-permute-start.43 = (f32[3,128,256]{2,1,0:T(8,128)S(1)}, f32[3,128,256]{2,1,0:T(8,128)S(1)}, u32[]{:S(2)}, u32[]{:S(2)}) collective-permute-start(f32[3,128,256]{2,1,0:T(8,128)S(1)} %add.61), channel_id=1, source_target_pairs={{8,16},{10,18},{12,20},{14,22},{16,8},{18,10},{20,12},{22,14},{9,1... | collective-permute-start | bytes 1179656 | tf_op jit(solution)/shard_map/ppermute | solution.py:313
  177.0 10.8 %collective-permute-start.37 = (f32[1,128,256]{2,1,0:T(8,128)S(1)}, f32[1,128,256]{2,1,0:T(8,128)S(1)}, u32[]{:S(2)}, u32[]{:S(2)}) collective-permute-start(f32[1,128,256]{2,1,0:T(8,128)S(1)} %add.56), channel_id=1, source_target_pairs={{0,8},{2,10},{4,12},{6,14},{24,16},{26,18},{28,20},{30,22},{1,9},{... | collective-permute-start | bytes 393224 | tf_op jit(solution)/shard_map/ppermute | solution.py:313
  181.4 12.3 %collective-permute-start.16 = (f32[2,128,256]{2,1,0:T(8,128)S(1)}, f32[2,128,256]{2,1,0:T(8,128)S(1)}, u32[]{:S(2)}, u32[]{:S(2)}) collective-permute-start(f32[2,128,256]{2,1,0:T(8,128)S(1)} %copy-done.16), channel_id=1, source_target_pairs={{0,2},{2,0},{4,6},{6,4},{8,10},{10,8},{12,14},{14,12},{16,18},{18,... | collective-permute-start | bytes 786440 | tf_op jit(solution)/shard_map/ppermute | solution.py:322
  187.7 13.5 %collective-permute-start.17 = (f32[2,128,256]{2,1,0:T(8,128)S(1)}, f32[2,128,256]{2,1,0:T(8,128)S(1)}, u32[]{:S(2)}, u32[]{:S(2)}) collective-permute-start(f32[2,128,256]{2,1,0:T(8,128)S(1)} %copy-done.17), channel_id=1, source_target_pairs={{0,4},{2,6},{4,0},{6,2},{8,12},{10,14},{12,8},{14,10},{16,20},{18,... | collective-permute-start | bytes 786440 | tf_op jit(solution)/shard_map/ppermute | solution.py:322
  189.5 13.0 %collective-permute-start.18 = (f32[2,128,256]{2,1,0:T(8,128)S(1)}, f32[2,128,256]{2,1,0:T(8,128)S(1)}, u32[]{:S(2)}, u32[]{:S(2)}) collective-permute-start(f32[2,128,256]{2,1,0:T(8,128)S(1)} %copy-done.18), channel_id=1, source_target_pairs={{0,6},{2,4},{4,2},{6,0},{8,14},{10,12},{12,10},{14,8},{16,22},{18,... | collective-permute-start | bytes 786440 | tf_op jit(solution)/shard_map/ppermute | solution.py:322
  189.5 1.0 copy-start.5
  189.5 1.1 copy-start.7
  192.1 40.6 %collective-permute-start.35 = (f32[1,128,256]{2,1,0:T(8,128)S(1)}, f32[1,128,256]{2,1,0:T(8,128)S(1)}, u32[]{:S(2)}, u32[]{:S(2)}) collective-permute-start(f32[1,128,256]{2,1,0:T(8,128)S(1)} %add.55), channel_id=1, source_target_pairs={{8,16},{10,18},{12,20},{14,22},{16,8},{18,10},{20,12},{22,14},{9,1... | collective-permute-start | bytes 393224 | tf_op jit(solution)/shard_map/ppermute | solution.py:313
  192.8 11.2 %copy-start.6 = (f32[2,128,256]{2,1,0:T(8,128)S(1)}, f32[2,128,256]{2,1,0:T(8,128)}, u32[]{:S(2)}) copy-start(f32[2,128,256]{2,1,0:T(8,128)} %get-tuple-element.88.refs_0_) | copy-start | bytes 786436
  192.9 38.2 %collective-permute-start.39 = (f32[3,128,256]{2,1,0:T(8,128)S(1)}, f32[3,128,256]{2,1,0:T(8,128)S(1)}, u32[]{:S(2)}, u32[]{:S(2)}) collective-permute-start(f32[3,128,256]{2,1,0:T(8,128)S(1)} %add.58), channel_id=1, source_target_pairs={{8,16},{10,18},{12,20},{14,22},{16,8},{18,10},{20,12},{22,14},{9,1... | collective-permute-start | bytes 1179656 | tf_op jit(solution)/shard_map/ppermute | solution.py:313
  193.7 39.0 %collective-permute-start.38 = (f32[1,128,256]{2,1,0:T(8,128)S(1)}, f32[1,128,256]{2,1,0:T(8,128)S(1)}, u32[]{:S(2)}, u32[]{:S(2)}) collective-permute-start(f32[1,128,256]{2,1,0:T(8,128)S(1)} %add.57), channel_id=1, source_target_pairs={{8,24},{10,26},{12,28},{14,30},{16,0},{18,2},{20,4},{22,6},{9,25},... | collective-permute-start | bytes 393224 | tf_op jit(solution)/shard_map/ppermute | solution.py:313
  201.2 29.8 %collective-permute-start.42 = (f32[3,128,256]{2,1,0:T(8,128)S(1)}, f32[3,128,256]{2,1,0:T(8,128)S(1)}, u32[]{:S(2)}, u32[]{:S(2)}) collective-permute-start(f32[3,128,256]{2,1,0:T(8,128)S(1)} %add.60), channel_id=1, source_target_pairs={{8,24},{10,26},{12,28},{14,30},{16,0},{18,2},{20,4},{22,6},{9,25},... | collective-permute-start | bytes 1179656 | tf_op jit(solution)/shard_map/ppermute | solution.py:313
  202.5 26.9 %collective-permute-start.46 = (f32[3,128,256]{2,1,0:T(8,128)S(1)}, f32[3,128,256]{2,1,0:T(8,128)S(1)}, u32[]{:S(2)}, u32[]{:S(2)}) collective-permute-start(f32[3,128,256]{2,1,0:T(8,128)S(1)} %add.63), channel_id=1, source_target_pairs={{8,24},{10,26},{12,28},{14,30},{16,0},{18,2},{20,4},{22,6},{9,25},... | collective-permute-start | bytes 1179656 | tf_op jit(solution)/shard_map/ppermute | solution.py:313
  204.0 25.4 %copy-start.1 = (f32[7,1,128,256]{3,2,1,0:T(8,128)S(1)}, f32[7,1,128,256]{3,2,1,0:T(8,128)}, u32[]{:S(2)}) copy-start(f32[7,1,128,256]{3,2,1,0:T(8,128)} %one_ref.5) | copy-start | bytes 2752516
  204.0 25.4 %copy-start.2 = (f32[7,1,128,256]{3,2,1,0:T(8,128)S(1)}, f32[7,1,128,256]{3,2,1,0:T(8,128)}, u32[]{:S(2)}) copy-start(f32[7,1,128,256]{3,2,1,0:T(8,128)} %two_ref.5) | copy-start | bytes 2752516
  (2 other events, 1.6 us)
